TPU v7x, 32 devices: a whole 2x2x4 slice. The times are simulated.
32 devices in a mesh: blk: 8 (over z, core), seq: 4 (over y, x).
Axes of the slice: x: 2, y: 2, z: 4, core: 2. Of those that a mesh axis runs over, the one named last changes fastest.
Arguments:
- activations: bfloat16 [8, 2048, 8192], P('blk', 'seq'), may hold values from -6 to 6
- base_weight: bfloat16 [8192, 1024], P('blk', 'seq'), may hold values from -0.0625 to 0.0625
- adapter_down: bfloat16 [8, 16, 8192], P('blk'), may hold values from -0.0625 to 0.0625
- adapter_up: bfloat16 [8, 16, 1024], P('blk'), may hold values from -1.5 to 1.5
- cotangent: bfloat16 [8, 2048, 1024], P('blk', 'seq'), may hold values from -12 to 12
Outputs:
- projected: bfloat16 [8, 2048, 1024], P('blk', 'seq')
- gradient_inputs: bfloat16 [8, 2048, 8192], P('blk', 'seq')
- down_gradient: float32 [8, 16, 8192], P('blk')
- up_gradient: float32 [8, 16, 1024], P('blk')
All inputs are finite; a program needn't handle non-finite values.
Results may differ from a plain program's by a relative error of at most 0.0047.
Values may be sent and summed in bfloat16 or wider, within the bound.
No kernel may reach another device: no remote copies, remote signals or barrier semaphores. Data moves between devices by JAX's collectives and lax.ppermute only.
A program may use at most 128 MiB of HBM per device.

v0:
```python
import jax
import jax.numpy as jnp
from jax import lax
from jax.sharding import PartitionSpec as P

adapter_scale = 2.0


def body(activations, base_weight, adapter_down, adapter_up, cotangent):
    token_inputs = activations[0]
    down_matrix = adapter_down[0]
    up_matrix = adapter_up[0]
    output_cotangent = cotangent[0]
    token_count = token_inputs.shape[0] * lax.axis_size("seq")
    panel = lax.all_gather(base_weight, "seq", axis=1, tiled=True)
    lowrank_forward = jnp.dot(
        token_inputs, down_matrix.T, preferred_element_type=jnp.float32
    ).astype(jnp.bfloat16)
    lowrank_backward = jnp.dot(
        output_cotangent, up_matrix.T, preferred_element_type=jnp.float32
    ).astype(jnp.bfloat16)
    frozen_keys = jnp.dot(
        token_inputs,
        lax.all_gather(panel, "blk", axis=0, tiled=True),
        preferred_element_type=jnp.float32,
    )
    frozen_gradient = lax.dot_general(
        output_cotangent,
        lax.all_gather(panel, "blk", axis=0, tiled=True),
        (((1,), (1,)), ((), ())),
        preferred_element_type=jnp.float32,
    )
    projected = frozen_keys + adapter_scale * jnp.dot(
        lowrank_forward, up_matrix, preferred_element_type=jnp.float32
    )
    gradient_inputs = frozen_gradient + adapter_scale * jnp.dot(
        lowrank_backward, down_matrix, preferred_element_type=jnp.float32
    )
    local_down = jnp.dot(lowrank_backward.T, token_inputs, preferred_element_type=jnp.float32)
    local_up = jnp.dot(lowrank_forward.T, output_cotangent, preferred_element_type=jnp.float32)
    sum_down, sum_up = lax.psum((local_down, local_up), "seq")
    scale_factor = adapter_scale / token_count
    return (
        projected.astype(jnp.bfloat16)[None],
        gradient_inputs.astype(jnp.bfloat16)[None],
        (scale_factor * sum_down)[None],
        (scale_factor * sum_up)[None],
    )


def solution(mesh):
    return jax.shard_map(
        body,
        mesh=mesh,
        in_specs=(
            P("blk", "seq", None),
            P("blk", "seq"),
            P("blk", None, None),
            P("blk", None, None),
            P("blk", "seq", None),
        ),
        out_specs=(
            P("blk", "seq", None),
            P("blk", "seq", None),
            P("blk", None, None),
            P("blk", None, None),
        ),
        check_vma=False,
    )
```

profile of v0, /device:TPU:0, one launch (start us, length us, event | category | flops | bytes accessed | tf_op | source)
XLA Modules:
  0.0 299.8 jit_solution(208566958700023274)
XLA Ops:
  7.2 0.0 copy-start
  7.2 0.0 all-gather.3.cloned.1.call-start
  7.2 0.7 all-gather.3.cloned.1.call-update
  7.9 0.0 all-reduce.3.cloned.1.call-start
  8.0 0.4 copy-done
  8.4 0.0 copy-start.1
  8.4 1.3 convolution_convert_fusion
  9.7 6.0 %fusion.12 = bf16[512,16]{0,1:T(8,128)(2,1)S(1)} fusion(bf16[1,512,8192]{2,1,0:T(8,128)(2,1)} %param.5, bf16[1,16,8192]{2,1,0:T(8,128)(2,1)} %param.7), kind=kOutput, calls=%fused_computation.10 | convolution fusion | flops 134225920 | bytes 8667136 | tf_op jit(solution)/shard_map/dot_general | solution.py:16
  15.6 0.0 copy-start.3
  15.6 0.9 fusion.15
  16.5 0.0 copy-done.1
  16.6 2.0 fusion.1
  18.6 0.0 all-reduce.3.cloned.1.call-update
  18.6 0.2 all-gather.5.cloned.1.call-start
  18.8 28.9 %all-gather.3.cloned.1.call-done = bf16[1024,1024]{1,0:T(8,128)(2,1)} async-done(((bf16[1024,256]{1,0:T(8,128)(2,1)}), bf16[1024,1024]{1,0:T(8,128)(2,1)}) %all-gather.3.cloned.1.call-update) | async-done | bytes 2097168 | tf_op jit(solution)/shard_map/all_gather | solution.py:15
  47.7 0.0 all-gather.5.cloned.1.call-update
  47.8 0.0 copy-done.3
  47.8 0.5 fusion.23
  48.2 49.4 %all-reduce.3.cloned.1.call-done = (f32[16,8192]{1,0:T(8,128)}, f32[16,1024]{1,0:T(8,128)}) async-done(((f32[16,8192]{1,0:T(8,128)}, f32[16,1024]{1,0:T(8,128)}), (f32[16,8192]{1,0:T(8,128)}, f32[16,1024]{1,0:T(8,128)})) %all-reduce.3.cloned.1.call-update) | async-done | bytes 589840 | tf_op jit(solution)/shard_map/psum | solution.py:41
  97.6 1.5 multiply_bitcast_fusion.1
  99.1 1.9 multiply_bitcast_fusion
  100.9 0.0 copy-start.2
  100.9 149.5 %all-gather.5.cloned.1.call-done = bf16[8192,1024]{1,0:T(8,128)(2,1)} async-done(((bf16[1024,1024]{1,0:T(8,128)(2,1)}), bf16[8192,1024]{1,0:T(8,128)(2,1)}) %all-gather.5.cloned.1.call-update) | async-done | bytes 16777232 | tf_op jit(solution)/shard_map/all_gather | solution.py:24
  250.4 15.8 %fusion.18 = f32[512,8192]{1,0:T(8,128)} fusion(bf16[8192,1024]{1,0:T(8,128)(2,1)} %all-gather.5.cloned.1.call-done, bf16[1,512,1024]{2,1,0:T(8,128)(2,1)S(1)} %copy-done), kind=kOutput, calls=%fused_computation.15 | convolution fusion | flops 8589934592 | bytes 34603008 | tf_op jit(solution)/shard_map/dot_general | solution.py:27
  266.2 0.0 copy-done.2
  266.2 11.5 %fusion = bf16[1,512,8192]{2,1,0:T(8,128)(2,1)} fusion(f32[512,8192]{1,0:T(8,128)} %fusion.18, bf16[512,16]{0,1:T(8,128)(2,1)S(1)} %convolution_convert_fusion, bf16[1,16,8192]{2,1,0:T(8,128)(2,1)S(1)} %copy-done.2), kind=kOutput, calls=%fused_computation.1 | convolution fusion | flops 146800640 | bytes 25444352 | tf_op jit(solution)/shard_map/dot_general | solution.py:36
  277.7 15.5 %fusion.9 = bf16[1,512,1024]{2,1,0:T(8,128)(2,1)} fusion(f32[512,1024]{1,0:T(8,128)S(1)} %fusion.23, bf16[8192,1024]{1,0:T(8,128)(2,1)} %all-gather.5.cloned.1.call-done, bf16[1,512,8192]{2,1,0:T(8,128)(2,1)} %param.5), kind=kOutput, calls=%fused_computation.9 | convolution fusion | flops 8591507456 | bytes 28311552 | tf_op jit(solution)/shard_map/dot_general | solution.py:22
Async XLA Ops:
  7.2 1.2 copy-start
  7.2 40.6 %all-gather.3.cloned.1.call-start = ((), (), s32[]{:S(2)}) async-start(), calls=%async_computation | async-start | bytes 2621440 | tf_op jit(solution)/shard_map/all_gather | solution.py:15
  7.9 89.7 %all-reduce.3.cloned.1.call-start = ((), (), s32[]{:S(2)}) async-start(), calls=%async_computation.2 | async-start | bytes 1179648 | tf_op jit(solution)/shard_map/psum | solution.py:41
  8.4 8.2 %copy-start.1 = (bf16[1,512,8192]{2,1,0:T(8,128)(2,1)S(1)}, bf16[1,512,8192]{2,1,0:T(8,128)(2,1)}, u32[]{:S(2)}) copy-start(bf16[1,512,8192]{2,1,0:T(8,128)(2,1)} %param.5) | copy-start | bytes 25165828
  15.6 32.1 %copy-start.3 = (bf16[1,16,1024]{2,1,0:T(8,128)(2,1)S(1)}, bf16[1,16,1024]{2,1,0:T(8,128)(2,1)}, u32[]{:S(2)}) copy-start(bf16[1,16,1024]{2,1,0:T(8,128)(2,1)} %param.8) | copy-start | bytes 98308
  18.6 231.8 %all-gather.5.cloned.1.call-start = ((), (), s32[]{:S(2)}) async-start(), calls=%async_computation.1 | async-start | bytes 18874368 | tf_op jit(solution)/shard_map/all_gather | solution.py:24
  100.9 165.3 %copy-start.2 = (bf16[1,16,8192]{2,1,0:T(8,128)(2,1)S(1)}, bf16[1,16,8192]{2,1,0:T(8,128)(2,1)}, u32[]{:S(2)}) copy-start(bf16[1,16,8192]{2,1,0:T(8,128)(2,1)} %param.7) | copy-start | bytes 786436
Sparse Core Ops, SparseCore 0:
  9.8 37.8 all-gather.2
  51.3 46.2 all-reduce.2
  99.3 151.0 all-gather.4
where the time goes:
time: 300 us
  waiting for transfers between devices  228 us (76%)
  matrix products  53.4 us (18%)
  between operations  13.8 us (5%)
  other arithmetic  3.34 us (1%)
    all_gather x1, waiting for transfers between devices, body(): lax.all_gather(panel, 'blk', axis=0, tiled=True)  149 us
    psum x1, waiting for transfers between devices, body(): sum_down, sum_up = lax.psum((local_down, local_up), 'seq')  49.4 us
    all_gather x1, waiting for transfers between devices, body(): panel = lax.all_gather(base_weight, 'seq', axis=1, tiled=True)  28.9 us
    dot_general x1, matrix products, body(): lax.dot_general(output_cotangent, lax.all_gather(panel, 'blk', axis=0, ti...  15.8 us
    dot_general x1, matrix products, body(): jnp.dot(token_inputs, lax.all_gather(panel, 'blk', axis=0, tiled=True), p...  15.5 us
    dot_general x1, matrix products, body(): jnp.dot(lowrank_backward, down_matrix, preferred_element_type=jnp.float32)  11.5 us
  transfers between devices with their start and end apart: 3, of which 3 were waited for; matrix products, arithmetic and copies ran while one was open for 5% of the time, Pallas kernels for 0%

commit v1 on v0

v1 whole, which is shorter than its diff:
```python
import functools

import jax
import jax.numpy as jnp
import numpy as np
from jax import lax
from jax.experimental import pallas as pl
from jax.experimental.pallas import tpu as pltpu
from jax.sharding import PartitionSpec as P

adapter_scale = 2.0
axes = ("blk", "seq")
f32 = jnp.float32
bf16 = jnp.bfloat16


def dot(a, b, contract):
    return lax.dot_general(a, b, (contract, ((), ())), preferred_element_type=f32)


class Layout:
    def __init__(self, mesh):
        self.blocks, self.seqs = mesh.shape["blk"], mesh.shape["seq"]
        self.depth = self.blocks // 2
        self.cycle = list(range(0, self.seqs, 2)) + list(range(self.seqs - 1, 0, -2))
        self.place = {seq: at for at, seq in enumerate(self.cycle)}
        self.forward_steps = self.seqs // 2
        self.backward_steps = self.seqs - 1 - self.forward_steps
        self.offsets = [0] + list(range(1, self.forward_steps + 1))
        self.offsets += [-step for step in range(1, self.backward_steps + 1)]

    def permute(self, value, target):
        pairs = []
        for blk in range(self.blocks):
            for seq in range(self.seqs):
                to_blk, to_seq = target(blk // 2, blk % 2, seq)
                pairs.append((blk * self.seqs + seq, to_blk * self.seqs + to_seq))
        return lax.ppermute(value, axes, pairs)

    def along_depth(self, value, shift):
        return self.permute(
            value, lambda z, core, seq: (((z + shift) % self.depth) * 2 + core, seq)
        )

    def along_cycle(self, value, step):
        def target(z, core, seq):
            sign = step if core == 0 else -step
            return z * 2 + core, self.cycle[(self.place[seq] + sign) % self.seqs]

        return self.permute(value, target)

    def swap_cores(self, value):
        return self.permute(value, lambda z, core, seq: (z * 2 + 1 - core, seq))

    def column_of(self, core, seq):
        sign = 1 if core == 0 else -1
        return [
            self.cycle[(self.place[seq] - sign * offset) % self.seqs] for offset in self.offsets
        ]

    def rank(self, core, seq):
        bits = self.seqs.bit_length() - 1
        if core == 1:
            return seq
        return int("".join(reversed(format(seq, f"0{bits}b"))), 2)

    def seq_of_rank(self, core, rank):
        return next(s for s in range(self.seqs) if self.rank(core, s) == rank)

    def across_rank(self, value, flip):
        def target(z, core, seq):
            return z * 2 + core, self.seq_of_rank(core, self.rank(core, seq) ^ flip)

        return self.permute(value, target)


def local_kernel(steps, a_ref, c_ref, down_ref, up_ref, low_f_ref, low_b_ref, grad_ref, acc_ref):
    step = pl.program_id(0)
    width = a_ref.shape[1]

    @pl.when(step == 0)
    def _():
        low_b_ref[...] = dot(c_ref[...], up_ref[...], ((1,), (1,))).astype(bf16)
        acc_ref[...] = jnp.zeros_like(acc_ref)

    block = a_ref[...]
    acc_ref[...] += dot(block, down_ref[...], ((1,), (1,)))
    grad_ref[step, :, :width] = dot(low_b_ref[...], block, ((0,), (0,)))

    @pl.when(step == steps - 1)
    def _():
        low_f = acc_ref[...].astype(bf16)
        low_f_ref[...] = low_f
        part = c_ref.shape[1] // steps
        for q in range(steps):
            grad_ref[q, :, width:] = dot(
                low_f, c_ref[:, q * part : (q + 1) * part], ((0,), (0,))
            )


def local_terms(a, c, down, up, steps):
    tokens, width = a.shape
    rank, keys = up.shape
    part = width // steps
    return pl.pallas_call(
        functools.partial(local_kernel, steps),
        grid=(steps,),
        in_specs=[
            pl.BlockSpec((tokens, part), lambda i: (0, i)),
            pl.BlockSpec((tokens, keys), lambda i: (0, 0)),
            pl.BlockSpec((rank, part), lambda i: (0, i)),
            pl.BlockSpec((rank, keys), lambda i: (0, 0)),
        ],
        out_specs=[
            pl.BlockSpec((tokens, rank), lambda i: (0, 0)),
            pl.BlockSpec((tokens, rank), lambda i: (0, 0)),
            pl.BlockSpec((steps, rank, part + keys // steps), lambda i: (0, 0, 0)),
        ],
        out_shape=[
            jax.ShapeDtypeStruct((tokens, rank), bf16),
            jax.ShapeDtypeStruct((tokens, rank), bf16),
            jax.ShapeDtypeStruct((steps, rank, part + keys // steps), f32),
        ],
        scratch_shapes=[pltpu.VMEM((tokens, rank), f32)],
        cost_estimate=pl.CostEstimate(
            flops=2 * tokens * width * 512, bytes_accessed=2 * tokens * width, transcendentals=0
        ),
        name="local_terms",
    )(a, c, down, up)


def slab_kernel(count, chunks, first, last, where_ref, *refs):
    refs = list(refs)
    pieces = [refs[:count], refs[count : 2 * count]]
    refs = refs[2 * count :]
    a_ref, c_ref, low_b_ref, down_ref = refs[:4]
    refs = refs[4:]
    if first:
        low_f_ref, up_ref = refs[:2]
        refs = refs[2:]
    else:
        acc_in_ref = refs[0]
        refs = refs[2:]
    keys_ref, grad_ref = refs[:2]
    acc_ref = refs[2] if last else keys_ref
    step = pl.program_id(0)
    part = c_ref.shape[1] // count

    @pl.when(step == 0)
    def _():
        if first:
            for j in range(count):
                at = pl.multiple_of(where_ref[2 + j] * part, part)
                acc_ref[:, j * part : (j + 1) * part] = adapter_scale * dot(
                    low_f_ref[...], up_ref[:, pl.ds(at, part)], ((1,), (0,))
                )
        else:
            acc_ref[...] = acc_in_ref[...]

    cot = jnp.concatenate(
        [
            c_ref[:, pl.ds(pl.multiple_of(where_ref[2 + j] * part, part), part)]
            for j in range(count)
        ],
        axis=1,
    )

    def work(held):
        panel = jnp.concatenate([ref[...] for ref in held], axis=1)
        acc_ref[...] += dot(a_ref[...], panel, ((1,), (0,)))
        grad = dot(cot, panel, ((1,), (1,)))
        grad += adapter_scale * dot(low_b_ref[...], down_ref[...], ((1,), (0,)))
        grad_ref[...] = grad.astype(bf16)

    for core in range(2):

        @pl.when(step // chunks == core)
        def _(core=core):
            work(pieces[core])

    if last:

        @pl.when(step == 2 * chunks - 1)
        def _():
            for j in range(count):
                at = pl.multiple_of(where_ref[2 + j] * part, part)
                keys_ref[:, pl.ds(at, part)] = acc_ref[:, j * part : (j + 1) * part].astype(bf16)


def slab(where, mine, other, a, c, low_b, down, low_f, up, acc, grad, first, last):
    count = len(mine)
    tokens, width = a.shape
    rank, keys = up.shape
    rows, part = mine[0].shape
    chunks = max(1, rows // 512)
    size = rows // chunks

    def row_block(i, where):
        return where[i // chunks] * chunks + i % chunks

    fixed = lambda i, where: (0, 0)
    in_specs = [
        pl.BlockSpec((size, part), lambda i, where: (jnp.minimum(i, chunks - 1), 0))
        for _ in range(count)
    ]
    in_specs += [
        pl.BlockSpec((size, part), lambda i, where: (jnp.maximum(i - chunks, 0), 0))
        for _ in range(count)
    ]
    in_specs += [
        pl.BlockSpec((tokens, size), lambda i, where: (0, row_block(i, where))),
        pl.BlockSpec((tokens, keys), fixed),
        pl.BlockSpec((tokens, rank), fixed),
        pl.BlockSpec((rank, size), lambda i, where: (0, row_block(i, where))),
    ]
    operands = [where, *mine, *other, a, c, low_b, down]
    aliases = {}
    if first:
        in_specs += [pl.BlockSpec((tokens, rank), fixed), pl.BlockSpec((rank, keys), fixed)]
        operands += [low_f, up]
    else:
        in_specs += [pl.BlockSpec((tokens, keys), fixed), pl.BlockSpec(memory_space=pl.ANY)]
        operands += [acc, grad]
        aliases = {len(operands) - 1: 1}
    return pl.pallas_call(
        functools.partial(slab_kernel, count, chunks, first, last),
        grid_spec=pltpu.PrefetchScalarGridSpec(
            num_scalar_prefetch=1,
            grid=(2 * chunks,),
            in_specs=in_specs,
            out_specs=[
                pl.BlockSpec((tokens, keys), fixed),
                pl.BlockSpec((tokens, size), lambda i, where: (0, row_block(i, where))),
            ],
            scratch_shapes=[pltpu.VMEM((tokens, keys), f32)] if last else [],
        ),
        out_shape=[
            jax.ShapeDtypeStruct((tokens, keys), bf16 if last else f32),
            jax.ShapeDtypeStruct((tokens, width), bf16),
        ],
        input_output_aliases=aliases,
        cost_estimate=pl.CostEstimate(
            flops=8 * tokens * rows * keys, bytes_accessed=16 * tokens * rows, transcendentals=0
        ),
        name="slab",
    )(*operands)


def reduce_over_seq(layout, partial, rank):
    half = partial.shape[0] // 2
    held = partial
    while half:
        bit = (rank // half) % 2
        kept = lax.dynamic_slice_in_dim(held, bit * half, half, 0)
        sent = lax.dynamic_slice_in_dim(held, (1 - bit) * half, half, 0)
        held = kept + layout.across_rank(sent, half)
        half //= 2
    half = 1
    while half < partial.shape[0]:
        bit = (rank // half) % 2
        other = layout.across_rank(held, half)
        both = jnp.concatenate([held, other], 0)
        swapped = jnp.concatenate([other, held], 0)
        held = jnp.where(bit == 0, both, swapped)
        half *= 2
    return held


def body(layout, activations, base_weight, adapter_down, adapter_up, cotangent):
    a, down, up, c = activations[0], adapter_down[0], adapter_up[0], cotangent[0]
    count = layout.seqs
    token_count = a.shape[0] * count
    blk, seq = lax.axis_index("blk"), lax.axis_index("seq")
    z, core = blk // 2, blk % 2
    columns = np.array(
        [[layout.column_of(k, s) for s in range(count)] for k in range(2)], np.int32
    )
    my_columns = jnp.asarray(columns)[core, seq]
    ranks = np.array([[layout.rank(k, s) for s in range(count)] for k in range(2)], np.int32)
    my_rank = jnp.asarray(ranks)[core, seq]
    where_of = []

    shifts = [0]
    for step in range(1, layout.depth // 2 + 1):
        shifts.append(step)
        if layout.depth - step != step:
            shifts.append(layout.depth - step)
    shards = {0: base_weight}
    for shift in shifts[1:]:
        shards[shift] = layout.along_depth(base_weight, shift)

    low_f, low_b, partial = local_terms(a, c, down, up, count)

    acc = grad = None
    for at, shift in enumerate(shifts):
        shard = shards[shift]
        forward, backward = [shard], [shard]
        for step in range(max(layout.forward_steps, layout.backward_steps)):
            if step < layout.forward_steps:
                forward.append(layout.along_cycle(forward[-1], 1))
            if step < layout.backward_steps:
                backward.append(layout.along_cycle(backward[-1], -1))
        mine = forward + backward[1:]
        swapped = [layout.swap_cores(piece) for piece in mine]
        by_offset = {-offset % count: piece for offset, piece in zip(layout.offsets, swapped)}
        other = [by_offset[offset % count] for offset in layout.offsets]
        source = (z - shift) % layout.depth
        where = jnp.concatenate(
            [jnp.stack([source * 2 + core, source * 2 + 1 - core]).astype(jnp.int32), my_columns]
        )
        acc, grad = slab(
            where, mine, other, a, c, low_b, down, low_f, up, acc, grad,
            at == 0, at == len(shifts) - 1,
        )

    sums = reduce_over_seq(layout, partial, my_rank) * (adapter_scale / token_count)
    width = a.shape[1] // count
    down_gradient = sums[:, :, :width].transpose(1, 0, 2).reshape(down.shape)
    up_gradient = sums[:, :, width:].transpose(1, 0, 2).reshape(up.shape)
    return acc[None], grad[None], down_gradient[None], up_gradient[None]


def solution(mesh):
    return jax.shard_map(
        functools.partial(body, Layout(mesh)),
        mesh=mesh,
        in_specs=(
            P("blk", "seq", None),
            P("blk", "seq"),
            P("blk", None, None),
            P("blk", None, None),
            P("blk", "seq", None),
        ),
        out_specs=(
            P("blk", "seq", None),
            P("blk", "seq", None),
            P("blk", None, None),
            P("blk", None, None),
        ),
        check_vma=False,
    )
```

time: 300 us -> 179 us (0.60)
  waiting for transfers between devices: 228 us -> 82.8 us
  Pallas kernels: 0 us -> 54.8 us
  matrix products: 53.4 us -> 0 us
  starting transfers between devices: 0.3 us -> 27.9 us
  between operations: 13.8 us -> 3.68 us
  local copies, waits for them, and re-layouts: 0.45 us -> 6.34 us
    all_gather x2 -> x0, waiting for transfers between devices: 178 us -> none  [the longest x1 149 us: body(): lax.all_gather(panel, 'blk', axis=0, tiled=True)]
    ppermute x0 -> x35, waiting for transfers between devices: none -> 82.8 us  [permute(): return lax.ppermute(value, axes, pairs)]
    pallas_call x0 -> x5, Pallas kernels: none -> 54.8 us  [the longest x4 46.7 us: slab(): pl.pallas_call(functools.partial(slab_kernel, count, chunks, first, last)...]
    dot_general x8 -> x0, matrix products: 53.4 us -> none  [the longest x1 15.8 us: body(): lax.dot_general(output_cotangent, lax.all_gather(panel, 'blk', axis=0, ti...]
    psum x1 -> x0, waiting for transfers between devices: 49.4 us -> none  [body(): sum_down, sum_up = lax.psum((local_down, local_up), 'seq')]
    ppermute x0 -> x35, starting transfers between devices: none -> 27.9 us  [permute(): return lax.ppermute(value, axes, pairs)]
    broadcast_in_dim x2 -> x0, other arithmetic: 3.34 us -> none  [the longest x1 1.87 us: body(): (scale_factor * sum_down)[None]]
  transfers between devices with their start and end apart: 3 -> 35, of which waited for: 3 -> 13; matrix products, arithmetic and copies ran while one was open for 5% -> 3% of each run, Pallas kernels for 0% -> 20%
where the time goes in v1:
time: 179 us
  waiting for transfers between devices  82.8 us (46%)
  Pallas kernels  54.8 us (31%)
  starting transfers between devices  27.9 us (16%)
  local copies, waits for them, and re-layouts  6.34 us (4%)
  between operations  3.68 us (2%)
  other arithmetic  3.53 us (2%)
    ppermute x35, waiting for transfers between devices, permute(): return lax.ppermute(value, axes, pairs)  82.8 us
    pallas_call x4, Pallas kernels, slab(): pl.pallas_call(functools.partial(slab_kernel, count, chunks, first, last)...  46.7 us
    ppermute x35, starting transfers between devices, permute(): return lax.ppermute(value, axes, pairs)  27.9 us
    pallas_call x1, Pallas kernels, local_terms(): pl.pallas_call(functools.partial(local_kernel, steps), grid=(steps,), in_...  8.07 us
  transfers between devices with their start and end apart: 35, of which 13 were waited for; matrix products, arithmetic and copies ran while one was open for 3% of the time, Pallas kernels for 20%

profile of v1, /device:TPU:0, one launch (start us, length us, event | category | flops | bytes accessed | tf_op | source)
XLA Modules:
  0.0 179.0 jit_solution(3256708820295739292)
XLA Ops:
  0.6 1.3 dynamic_slice.19
  4.6 8.1 %local_terms.1 = (bf16[512,16]{1,0:T(8,128)(2,1)}, bf16[512,16]{1,0:T(8,128)(2,1)}, f32[4,16,2304]{2,1,0:T(8,128)}) custom-call(bf16[512,8192]{1,0:T(8,128)(2,1)} %bitcast.21, bf16[512,1024]{1,0:T(8,128)(2,1)} %bitcast.27, bf16[16,8192]{1,0:T(8,128)(2,1)} %bitcast.32, bf16[16,1024]{1,0:T(8,128)(2,1)} %bitcast.38), custom_call_target="tpu_custom_call" | custom-call | flops 4294967296 | bytes 8388608 | tf_op jit(solution)/shard_map/local_terms/pallas_call | solution.py:105
  12.6 1.0 constant_dynamic-slice_fusion.1
  13.6 3.0 %collective-permute-start.31 = (f32[2,16,2304]{2,1,0:T(8,128)S(1)}, f32[2,16,2304]{2,1,0:T(8,128)S(1)}, u32[]{:S(2)}, u32[]{:S(2)}) collective-permute-start(f32[2,16,2304]{2,1,0:T(8,128)S(1)} %constant_dynamic-slice_fusion.1), channel_id=1, source_target_pairs={{0,1},{1,0},{2,3},{3,2},{4,6},{5,7},{6,4},{7,5},{8,9},{9,8},{10,11... | collective-permute-start | bytes 884744 | tf_op jit(solution)/shard_map/ppermute | solution.py:38
  16.6 4.7 %collective-permute-done.31 = f32[2,16,2304]{2,1,0:T(8,128)S(1)} collective-permute-done((f32[2,16,2304]{2,1,0:T(8,128)S(1)}, f32[2,16,2304]{2,1,0:T(8,128)S(1)}, u32[]{:S(2)}, u32[]{:S(2)}) %collective-permute-start.31) | collective-permute-done | bytes 294944 | tf_op jit(solution)/shard_map/ppermute | solution.py:38
  21.3 1.0 dynamic-slice_add_fusion
  22.3 2.1 %collective-permute-start.32 = (f32[1,16,2304]{2,1,0:T(8,128)S(1)}, f32[1,16,2304]{2,1,0:T(8,128)S(1)}, u32[]{:S(2)}, u32[]{:S(2)}) collective-permute-start(f32[1,16,2304]{2,1,0:T(8,128)S(1)} %constant_dynamic-slice_fusion), channel_id=1, source_target_pairs={{0,2},{1,3},{2,0},{3,1},{4,5},{5,4},{6,7},{7,6},{8,10},{9,11},{10,... | collective-permute-start | bytes 442376 | tf_op jit(solution)/shard_map/ppermute | solution.py:38
  24.5 2.0 %collective-permute-start.26 = (bf16[1024,256]{1,0:T(8,128)(2,1)S(1)}, bf16[1024,256]{1,0:T(8,128)(2,1)}, u32[]{:S(2)}, u32[]{:S(2)}) collective-permute-start(bf16[1024,256]{1,0:T(8,128)(2,1)S(1)} %copy-done.11), channel_id=1, source_target_pairs={{0,1},{1,3},{2,0},{3,2},{4,6},{5,4},{6,7},{7,5},{8,9},{9,11},{10,8... | collective-permute-start | bytes 1572872 | tf_op jit(solution)/shard_map/ppermute | solution.py:38
  26.5 2.7 %collective-permute-done.32 = f32[1,16,2304]{2,1,0:T(8,128)S(1)} collective-permute-done((f32[1,16,2304]{2,1,0:T(8,128)S(1)}, f32[1,16,2304]{2,1,0:T(8,128)S(1)}, u32[]{:S(2)}, u32[]{:S(2)}) %collective-permute-start.32) | collective-permute-done | bytes 147488 | tf_op jit(solution)/shard_map/ppermute | solution.py:38
  29.2 2.0 %collective-permute-start.33 = (f32[1,16,2304]{2,1,0:T(8,128)S(1)}, f32[1,16,2304]{2,1,0:T(8,128)S(1)}, u32[]{:S(2)}, u32[]{:S(2)}) collective-permute-start(f32[1,16,2304]{2,1,0:T(8,128)S(1)} %dynamic-slice_add_fusion.1), channel_id=1, source_target_pairs={{0,2},{1,3},{2,0},{3,1},{4,5},{5,4},{6,7},{7,6},{8,10},{9,11},{10,... | collective-permute-start | bytes 442376 | tf_op jit(solution)/shard_map/ppermute | solution.py:38
  31.2 1.6 collective-permute-start.16
  32.8 5.9 %collective-permute-done.24.refs_1_ = bf16[1024,256]{1,0:T(8,128)(2,1)S(1)} collective-permute-done((bf16[1024,256]{1,0:T(8,128)(2,1)S(1)}, bf16[1024,256]{1,0:T(8,128)(2,1)S(1)}, u32[]{:S(2)}, u32[]{:S(2)}) %collective-permute-start.24) | collective-permute-done | bytes 524320 | tf_op jit(solution)/shard_map/ppermute | solution.py:38
  38.7 3.8 %collective-permute-start.8 = (bf16[1024,256]{1,0:T(8,128)(2,1)S(1)}, bf16[1024,256]{1,0:T(8,128)(2,1)S(1)}, u32[]{:S(2)}, u32[]{:S(2)}) collective-permute-start(bf16[1024,256]{1,0:T(8,128)(2,1)S(1)} %copy-done.11), channel_id=1, source_target_pairs={{0,24},{1,25},{2,26},{3,27},{4,28},{5,29},{6,30},{7,31},{8,0},{9,1... | collective-permute-start | bytes 1572872 | tf_op jit(solution)/shard_map/ppermute | solution.py:38
  42.7 1.8 %collective-permute-start.34 = (f32[2,16,2304]{2,1,0:T(8,128)S(1)}, f32[2,16,2304]{2,1,0:T(8,128)S(1)}, u32[]{:S(2)}, u32[]{:S(2)}) collective-permute-start(f32[2,16,2304]{2,1,0:T(8,128)S(1)} %maximum_select_fusion.1), channel_id=1, source_target_pairs={{0,1},{1,0},{2,3},{3,2},{4,6},{5,7},{6,4},{7,5},{8,9},{9,8},{10,11... | collective-permute-start | bytes 884744 | tf_op jit(solution)/shard_map/ppermute | solution.py:38
  45.0 2.7 %collective-permute-done.16.refs_0_ = bf16[1024,256]{1,0:T(8,128)(2,1)S(1)} collective-permute-done((bf16[1024,256]{1,0:T(8,128)(2,1)S(1)}, bf16[1024,256]{1,0:T(8,128)(2,1)S(1)}, u32[]{:S(2)}, u32[]{:S(2)}) %collective-permute-start.16) | collective-permute-done | bytes 524320 | tf_op jit(solution)/shard_map/ppermute | solution.py:38
  47.8 10.9 %collective-permute-done.8.refs_0_ = bf16[1024,256]{1,0:T(8,128)(2,1)S(1)} collective-permute-done((bf16[1024,256]{1,0:T(8,128)(2,1)S(1)}, bf16[1024,256]{1,0:T(8,128)(2,1)S(1)}, u32[]{:S(2)}, u32[]{:S(2)}) %collective-permute-start.8) | collective-permute-done | bytes 524320 | tf_op jit(solution)/shard_map/ppermute | solution.py:38
  58.6 22.5 %collective-permute-done.refs_0_ = bf16[1024,256]{1,0:T(8,128)(2,1)S(1)} collective-permute-done((bf16[1024,256]{1,0:T(8,128)(2,1)S(1)}, bf16[1024,256]{1,0:T(8,128)(2,1)S(1)}, u32[]{:S(2)}, u32[]{:S(2)}) %collective-permute-start) | collective-permute-done | bytes 524320 | tf_op jit(solution)/shard_map/ppermute | solution.py:38
  81.7 1.5 collective-permute-start.19
  83.8 1.5 collective-permute-start.11
  85.3 10.4 %collective-permute-done.17.refs_1_ = bf16[1024,256]{1,0:T(8,128)(2,1)} collective-permute-done((bf16[1024,256]{1,0:T(8,128)(2,1)S(1)}, bf16[1024,256]{1,0:T(8,128)(2,1)}, u32[]{:S(2)}, u32[]{:S(2)}) %collective-permute-start.17) | collective-permute-done | bytes 524320 | tf_op jit(solution)/shard_map/ppermute | solution.py:38
  96.6 1.5 collective-permute-start.1
  100.7 6.2 %collective-permute-done.9.refs_1_ = bf16[1024,256]{1,0:T(8,128)(2,1)} collective-permute-done((bf16[1024,256]{1,0:T(8,128)(2,1)S(1)}, bf16[1024,256]{1,0:T(8,128)(2,1)}, u32[]{:S(2)}, u32[]{:S(2)}) %collective-permute-start.9) | collective-permute-done | bytes 524320 | tf_op jit(solution)/shard_map/ppermute | solution.py:38
  108.3 9.8 %collective-permute-done.1.refs_1_ = bf16[1024,256]{1,0:T(8,128)(2,1)S(1)} collective-permute-done((bf16[1024,256]{1,0:T(8,128)(2,1)S(1)}, bf16[1024,256]{1,0:T(8,128)(2,1)S(1)}, u32[]{:S(2)}, u32[]{:S(2)}) %collective-permute-start.1) | collective-permute-done | bytes 524320 | tf_op jit(solution)/shard_map/ppermute | solution.py:38
  118.2 1.2 fusion
  119.4 1.1 collective-permute-start.10
  120.9 1.2 broadcast_in_dim_reshape.6
  122.2 1.9 %collective-permute-done.18.refs_2_ = bf16[1024,256]{1,0:T(8,128)(2,1)} collective-permute-done((bf16[1024,256]{1,0:T(8,128)(2,1)}, bf16[1024,256]{1,0:T(8,128)(2,1)}, u32[]{:S(2)}, u32[]{:S(2)}) %collective-permute-start.18) | collective-permute-done | bytes 524320 | tf_op jit(solution)/shard_map/ppermute | solution.py:38
  125.8 3.9 %collective-permute-done.10.refs_2_ = bf16[1024,256]{1,0:T(8,128)(2,1)} collective-permute-done((bf16[1024,256]{1,0:T(8,128)(2,1)}, bf16[1024,256]{1,0:T(8,128)(2,1)}, u32[]{:S(2)}, u32[]{:S(2)}) %collective-permute-start.10) | collective-permute-done | bytes 524320 | tf_op jit(solution)/shard_map/ppermute | solution.py:38
  129.7 11.4 %slab.4 = (f32[512,1024]{1,0:T(8,128)}, bf16[512,8192]{1,0:T(8,128)(2,1)}) custom-call(s32[6]{0:T(128)} %get-tuple-element.26.where_ref, bf16[1024,256]{1,0:T(8,128)(2,1)} %refs_0_.1, bf16[1024,256]{1,0:T(8,128)(2,1)} %copy-done.12, bf16[1024,256]{1,0:T(8,128)(2,1)} %collective-permute-done.25.refs_2_, bf16[1024,256]{1,0:T(8,128)(2,1)} %collective-permute-done.26.refs_3_, ...), custom_call_target="tpu_custom_call" | custom-call | flops 4294967296 | bytes 8388608 | tf_op jit(solution)/shard_map/slab/pallas_call | solution.py:225
  142.4 11.8 %slab.5 = (f32[512,1024]{1,0:T(8,128)}, bf16[512,8192]{1,0:T(8,128)(2,1)}) custom-call(s32[6]{0:T(128)} %get-tuple-element.28.where_ref, bf16[1024,256]{1,0:T(8,128)(2,1)} %copy-done.2, bf16[1024,256]{1,0:T(8,128)(2,1)} %collective-permute-done.17.refs_1_, bf16[1024,256]{1,0:T(8,128)(2,1)} %collective-permute-done.18.refs_2_, ...), custom_call_target="tpu_custom_call", output_to_operand_aliasing={{1}: (14, {})} | custom-call | flops 4294967296 | bytes 8388608 | tf_op jit(solution)/shard_map/slab/pallas_call | solution.py:225
  154.2 11.8 %slab.6 = (f32[512,1024]{1,0:T(8,128)}, bf16[512,8192]{1,0:T(8,128)(2,1)}) custom-call(s32[6]{0:T(128)} %get-tuple-element.27.where_ref, bf16[1024,256]{1,0:T(8,128)(2,1)} %copy-done.1, bf16[1024,256]{1,0:T(8,128)(2,1)} %collective-permute-done.9.refs_1_, bf16[1024,256]{1,0:T(8,128)(2,1)} %collective-permute-done.10.refs_2_, ...), custom_call_target="tpu_custom_call", output_to_operand_aliasing={{1}: (14, {})} | custom-call | flops 4294967296 | bytes 8388608 | tf_op jit(solution)/shard_map/slab/pallas_call | solution.py:225
  167.2 11.7 %slab.7 = (bf16[512,1024]{1,0:T(8,128)(2,1)}, bf16[512,8192]{1,0:T(8,128)(2,1)}) custom-call(s32[6]{0:T(128)} %add_add_fusion.where_ref, bf16[1024,256]{1,0:T(8,128)(2,1)} %copy-done, bf16[1024,256]{1,0:T(8,128)(2,1)} %copy-done.3, bf16[1024,256]{1,0:T(8,128)(2,1)} %copy-done.6, ...), custom_call_target="tpu_custom_call", output_to_operand_aliasing={{1}: (14, {})} | custom-call | flops 4294967296 | bytes 8388608 | tf_op jit(solution)/shard_map/slab/pallas_call | solution.py:225
  (89 shorter events, 11.3 us)
Async XLA Ops:
  24.5 14.2 %collective-permute-start.24 = (bf16[1024,256]{1,0:T(8,128)(2,1)S(1)}, bf16[1024,256]{1,0:T(8,128)(2,1)S(1)}, u32[]{:S(2)}, u32[]{:S(2)}) collective-permute-start(bf16[1024,256]{1,0:T(8,128)(2,1)S(1)} %copy-done.11), channel_id=1, source_target_pairs={{0,2},{1,0},{2,3},{3,1},{4,5},{5,7},{6,4},{7,6},{8,10},{9,8},{10,1... | collective-permute-start | bytes 1572872 | tf_op jit(solution)/shard_map/ppermute | solution.py:38
  24.5 18.2 %collective-permute-start.26 = (bf16[1024,256]{1,0:T(8,128)(2,1)S(1)}, bf16[1024,256]{1,0:T(8,128)(2,1)}, u32[]{:S(2)}, u32[]{:S(2)}) collective-permute-start(bf16[1024,256]{1,0:T(8,128)(2,1)S(1)} %copy-done.11), channel_id=1, source_target_pairs={{0,1},{1,3},{2,0},{3,2},{4,6},{5,4},{6,7},{7,5},{8,9},{9,11},{10,8... | collective-permute-start | bytes 1572872 | tf_op jit(solution)/shard_map/ppermute | solution.py:38
  29.2 13.3 %collective-permute-start.33 = (f32[1,16,2304]{2,1,0:T(8,128)S(1)}, f32[1,16,2304]{2,1,0:T(8,128)S(1)}, u32[]{:S(2)}, u32[]{:S(2)}) collective-permute-start(f32[1,16,2304]{2,1,0:T(8,128)S(1)} %dynamic-slice_add_fusion.1), channel_id=1, source_target_pairs={{0,2},{1,3},{2,0},{3,1},{4,5},{5,4},{6,7},{7,6},{8,10},{9,11},{10,... | collective-permute-start | bytes 442376 | tf_op jit(solution)/shard_map/ppermute | solution.py:38
  31.2 13.4 %collective-permute-start.27 = (bf16[1024,256]{1,0:T(8,128)(2,1)S(1)}, bf16[1024,256]{1,0:T(8,128)(2,1)}, u32[]{:S(2)}, u32[]{:S(2)}) collective-permute-start(bf16[1024,256]{1,0:T(8,128)(2,1)S(1)} %copy-done.11), channel_id=1, source_target_pairs={{0,4},{1,5},{2,6},{3,7},{4,0},{5,1},{6,2},{7,3},{8,12},{9,13},{10,... | collective-permute-start | bytes 1572872 | tf_op jit(solution)/shard_map/ppermute | solution.py:38
  31.2 16.6 %collective-permute-start.16 = (bf16[1024,256]{1,0:T(8,128)(2,1)S(1)}, bf16[1024,256]{1,0:T(8,128)(2,1)S(1)}, u32[]{:S(2)}, u32[]{:S(2)}) collective-permute-start(bf16[1024,256]{1,0:T(8,128)(2,1)S(1)} %copy-done.11), channel_id=1, source_target_pairs={{0,8},{1,9},{2,10},{3,11},{4,12},{5,13},{6,14},{7,15},{8,16},{9,17... | collective-permute-start | bytes 1572872 | tf_op jit(solution)/shard_map/ppermute | solution.py:38
  38.7 19.9 %collective-permute-start.8 = (bf16[1024,256]{1,0:T(8,128)(2,1)S(1)}, bf16[1024,256]{1,0:T(8,128)(2,1)S(1)}, u32[]{:S(2)}, u32[]{:S(2)}) collective-permute-start(bf16[1024,256]{1,0:T(8,128)(2,1)S(1)} %copy-done.11), channel_id=1, source_target_pairs={{0,24},{1,25},{2,26},{3,27},{4,28},{5,29},{6,30},{7,31},{8,0},{9,1... | collective-permute-start | bytes 1572872 | tf_op jit(solution)/shard_map/ppermute | solution.py:38
  42.5 38.6 %collective-permute-start = (bf16[1024,256]{1,0:T(8,128)(2,1)S(1)}, bf16[1024,256]{1,0:T(8,128)(2,1)S(1)}, u32[]{:S(2)}, u32[]{:S(2)}) collective-permute-start(bf16[1024,256]{1,0:T(8,128)(2,1)S(1)} %copy-done.11), channel_id=1, source_target_pairs={{0,16},{1,17},{2,18},{3,19},{4,20},{5,21},{6,22},{7,23},{8,24},{9,... | collective-permute-start | bytes 1572872 | tf_op jit(solution)/shard_map/ppermute | solution.py:38
  42.7 38.9 %collective-permute-start.34 = (f32[2,16,2304]{2,1,0:T(8,128)S(1)}, f32[2,16,2304]{2,1,0:T(8,128)S(1)}, u32[]{:S(2)}, u32[]{:S(2)}) collective-permute-start(f32[2,16,2304]{2,1,0:T(8,128)S(1)} %maximum_select_fusion.1), channel_id=1, source_target_pairs={{0,1},{1,0},{2,3},{3,2},{4,6},{5,7},{6,4},{7,5},{8,9},{9,8},{10,11... | collective-permute-start | bytes 884744 | tf_op jit(solution)/shard_map/ppermute | solution.py:38
  44.6 38.6 %collective-permute-start.25 = (bf16[1024,256]{1,0:T(8,128)(2,1)S(1)}, bf16[1024,256]{1,0:T(8,128)(2,1)}, u32[]{:S(2)}, u32[]{:S(2)}) collective-permute-start(bf16[1024,256]{1,0:T(8,128)(2,1)S(1)} %collective-permute-done.24.refs_1_), channel_id=1, source_target_pairs={{0,2},{1,0},{2,3},{3,1},{4,5},{5,7},{6,4},{7,6},{8,10},{9,8},{10,1... | collective-permute-start | bytes 1572872 | tf_op jit(solution)/shard_map/ppermute | solution.py:38
  47.8 35.4 %collective-permute-start.30 = (bf16[1024,256]{1,0:T(8,128)(2,1)S(1)}, bf16[1024,256]{1,0:T(8,128)(2,1)S(1)}, u32[]{:S(2)}, u32[]{:S(2)}) collective-permute-start(bf16[1024,256]{1,0:T(8,128)(2,1)S(1)} %collective-permute-done.24.refs_1_), channel_id=1, source_target_pairs={{0,4},{1,5},{2,6},{3,7},{4,0},{5,1},{6,2},{7,3},{8,12},{9,13},{10,... | collective-permute-start | bytes 1572872 | tf_op jit(solution)/shard_map/ppermute | solution.py:38
  58.6 25.1 %collective-permute-start.28 = (bf16[1024,256]{1,0:T(8,128)(2,1)}, bf16[1024,256]{1,0:T(8,128)(2,1)S(1)}, u32[]{:S(2)}, u32[]{:S(2)}) collective-permute-start(bf16[1024,256]{1,0:T(8,128)(2,1)} %collective-permute-done.26.refs_3_), channel_id=1, source_target_pairs={{0,4},{1,5},{2,6},{3,7},{4,0},{5,1},{6,2},{7,3},{8,12},{9,13},{10,... | collective-permute-start | bytes 1572872 | tf_op jit(solution)/shard_map/ppermute | solution.py:38
  81.1 14.6 %collective-permute-start.17 = (bf16[1024,256]{1,0:T(8,128)(2,1)S(1)}, bf16[1024,256]{1,0:T(8,128)(2,1)}, u32[]{:S(2)}, u32[]{:S(2)}) collective-permute-start(bf16[1024,256]{1,0:T(8,128)(2,1)S(1)} %collective-permute-done.16.refs_0_), channel_id=1, source_target_pairs={{0,2},{1,0},{2,3},{3,1},{4,5},{5,7},{6,4},{7,6},{8,10},{9,8},{10,1... | collective-permute-start | bytes 1572872 | tf_op jit(solution)/shard_map/ppermute | solution.py:38
  81.7 15.0 %collective-permute-start.19 = (bf16[1024,256]{1,0:T(8,128)(2,1)S(1)}, bf16[1024,256]{1,0:T(8,128)(2,1)}, u32[]{:S(2)}, u32[]{:S(2)}) collective-permute-start(bf16[1024,256]{1,0:T(8,128)(2,1)S(1)} %collective-permute-done.16.refs_0_), channel_id=1, source_target_pairs={{0,1},{1,3},{2,0},{3,2},{4,6},{5,4},{6,7},{7,5},{8,9},{9,11},{10,8... | collective-permute-start | bytes 1572872 | tf_op jit(solution)/shard_map/ppermute | solution.py:38
  83.1 15.7 %collective-permute-start.20 = (bf16[1024,256]{1,0:T(8,128)(2,1)S(1)}, bf16[1024,256]{1,0:T(8,128)(2,1)S(1)}, u32[]{:S(2)}, u32[]{:S(2)}) collective-permute-start(bf16[1024,256]{1,0:T(8,128)(2,1)S(1)} %collective-permute-done.16.refs_0_), channel_id=1, source_target_pairs={{0,4},{1,5},{2,6},{3,7},{4,0},{5,1},{6,2},{7,3},{8,12},{9,13},{10,... | collective-permute-start | bytes 1572872 | tf_op jit(solution)/shard_map/ppermute | solution.py:38
  83.2 23.8 %collective-permute-start.9 = (bf16[1024,256]{1,0:T(8,128)(2,1)S(1)}, bf16[1024,256]{1,0:T(8,128)(2,1)}, u32[]{:S(2)}, u32[]{:S(2)}) collective-permute-start(bf16[1024,256]{1,0:T(8,128)(2,1)S(1)} %collective-permute-done.8.refs_0_), channel_id=1, source_target_pairs={{0,2},{1,0},{2,3},{3,1},{4,5},{5,7},{6,4},{7,6},{8,10},{9,8},{10,1... | collective-permute-start | bytes 1572872 | tf_op jit(solution)/shard_map/ppermute | solution.py:38
  83.8 24.0 %collective-permute-start.11 = (bf16[1024,256]{1,0:T(8,128)(2,1)S(1)}, bf16[1024,256]{1,0:T(8,128)(2,1)S(1)}, u32[]{:S(2)}, u32[]{:S(2)}) collective-permute-start(bf16[1024,256]{1,0:T(8,128)(2,1)S(1)} %collective-permute-done.8.refs_0_), channel_id=1, source_target_pairs={{0,1},{1,3},{2,0},{3,2},{4,6},{5,4},{6,7},{7,5},{8,9},{9,11},{10,8... | collective-permute-start | bytes 1572872 | tf_op jit(solution)/shard_map/ppermute | solution.py:38
  95.7 12.1 %collective-permute-start.12 = (bf16[1024,256]{1,0:T(8,128)(2,1)S(1)}, bf16[1024,256]{1,0:T(8,128)(2,1)}, u32[]{:S(2)}, u32[]{:S(2)}) collective-permute-start(bf16[1024,256]{1,0:T(8,128)(2,1)S(1)} %collective-permute-done.8.refs_0_), channel_id=1, source_target_pairs={{0,4},{1,5},{2,6},{3,7},{4,0},{5,1},{6,2},{7,3},{8,12},{9,13},{10,... | collective-permute-start | bytes 1572872 | tf_op jit(solution)/shard_map/ppermute | solution.py:38
  96.6 21.4 %collective-permute-start.1 = (bf16[1024,256]{1,0:T(8,128)(2,1)S(1)}, bf16[1024,256]{1,0:T(8,128)(2,1)S(1)}, u32[]{:S(2)}, u32[]{:S(2)}) collective-permute-start(bf16[1024,256]{1,0:T(8,128)(2,1)S(1)} %collective-permute-done.refs_0_), channel_id=1, source_target_pairs={{0,2},{1,0},{2,3},{3,1},{4,5},{5,7},{6,4},{7,6},{8,10},{9,8},{10,1... | collective-permute-start | bytes 1572872 | tf_op jit(solution)/shard_map/ppermute | solution.py:38
  98.8 20.6 %collective-permute-start.3 = (bf16[1024,256]{1,0:T(8,128)(2,1)S(1)}, bf16[1024,256]{1,0:T(8,128)(2,1)}, u32[]{:S(2)}, u32[]{:S(2)}) collective-permute-start(bf16[1024,256]{1,0:T(8,128)(2,1)S(1)} %collective-permute-done.refs_0_), channel_id=1, source_target_pairs={{0,1},{1,3},{2,0},{3,2},{4,6},{5,4},{6,7},{7,5},{8,9},{9,11},{10,8... | collective-permute-start | bytes 1572872 | tf_op jit(solution)/shard_map/ppermute | solution.py:38
  106.9 17.2 %collective-permute-start.18 = (bf16[1024,256]{1,0:T(8,128)(2,1)}, bf16[1024,256]{1,0:T(8,128)(2,1)}, u32[]{:S(2)}, u32[]{:S(2)}) collective-permute-start(bf16[1024,256]{1,0:T(8,128)(2,1)} %collective-permute-done.17.refs_1_), channel_id=1, source_target_pairs={{0,2},{1,0},{2,3},{3,1},{4,5},{5,7},{6,4},{7,6},{8,10},{9,8},{10,1... | collective-permute-start | bytes 1572872 | tf_op jit(solution)/shard_map/ppermute | solution.py:38
  107.8 16.4 %collective-permute-start.23 = (bf16[1024,256]{1,0:T(8,128)(2,1)}, bf16[1024,256]{1,0:T(8,128)(2,1)}, u32[]{:S(2)}, u32[]{:S(2)}) collective-permute-start(bf16[1024,256]{1,0:T(8,128)(2,1)} %collective-permute-done.17.refs_1_), channel_id=1, source_target_pairs={{0,4},{1,5},{2,6},{3,7},{4,0},{5,1},{6,2},{7,3},{8,12},{9,13},{10,... | collective-permute-start | bytes 1572872 | tf_op jit(solution)/shard_map/ppermute | solution.py:38
  107.8 14.3 %collective-permute-start.29 = (bf16[1024,256]{1,0:T(8,128)(2,1)}, bf16[1024,256]{1,0:T(8,128)(2,1)}, u32[]{:S(2)}, u32[]{:S(2)}) collective-permute-start(bf16[1024,256]{1,0:T(8,128)(2,1)} %collective-permute-done.25.refs_2_), channel_id=1, source_target_pairs={{0,4},{1,5},{2,6},{3,7},{4,0},{5,1},{6,2},{7,3},{8,12},{9,13},{10,... | collective-permute-start | bytes 1572872 | tf_op jit(solution)/shard_map/ppermute | solution.py:38
  119.4 10.3 %collective-permute-start.10 = (bf16[1024,256]{1,0:T(8,128)(2,1)}, bf16[1024,256]{1,0:T(8,128)(2,1)}, u32[]{:S(2)}, u32[]{:S(2)}) collective-permute-start(bf16[1024,256]{1,0:T(8,128)(2,1)} %collective-permute-done.9.refs_1_), channel_id=1, source_target_pairs={{0,2},{1,0},{2,3},{3,1},{4,5},{5,7},{6,4},{7,6},{8,10},{9,8},{10,1... | collective-permute-start | bytes 1572872 | tf_op jit(solution)/shard_map/ppermute | solution.py:38
  122.1 19.1 %collective-permute-start.15 = (bf16[1024,256]{1,0:T(8,128)(2,1)}, bf16[1024,256]{1,0:T(8,128)(2,1)}, u32[]{:S(2)}, u32[]{:S(2)}) collective-permute-start(bf16[1024,256]{1,0:T(8,128)(2,1)} %collective-permute-done.9.refs_1_), channel_id=1, source_target_pairs={{0,4},{1,5},{2,6},{3,7},{4,0},{5,1},{6,2},{7,3},{8,12},{9,13},{10,... | collective-permute-start | bytes 1572872 | tf_op jit(solution)/shard_map/ppermute | solution.py:38
  124.1 17.7 %collective-permute-start.13 = (bf16[1024,256]{1,0:T(8,128)(2,1)}, bf16[1024,256]{1,0:T(8,128)(2,1)}, u32[]{:S(2)}, u32[]{:S(2)}) collective-permute-start(bf16[1024,256]{1,0:T(8,128)(2,1)} %copy-done.4), channel_id=1, source_target_pairs={{0,4},{1,5},{2,6},{3,7},{4,0},{5,1},{6,2},{7,3},{8,12},{9,13},{10,... | collective-permute-start | bytes 1572872 | tf_op jit(solution)/shard_map/ppermute | solution.py:38
  124.1 17.7 %collective-permute-start.2 = (bf16[1024,256]{1,0:T(8,128)(2,1)S(1)}, bf16[1024,256]{1,0:T(8,128)(2,1)S(1)}, u32[]{:S(2)}, u32[]{:S(2)}) collective-permute-start(bf16[1024,256]{1,0:T(8,128)(2,1)S(1)} %collective-permute-done.1.refs_1_), channel_id=1, source_target_pairs={{0,2},{1,0},{2,3},{3,1},{4,5},{5,7},{6,4},{7,6},{8,10},{9,8},{10,1... | collective-permute-start | bytes 1572872 | tf_op jit(solution)/shard_map/ppermute | solution.py:38
  124.7 17.6 %collective-permute-start.22 = (bf16[1024,256]{1,0:T(8,128)(2,1)}, bf16[1024,256]{1,0:T(8,128)(2,1)}, u32[]{:S(2)}, u32[]{:S(2)}) collective-permute-start(bf16[1024,256]{1,0:T(8,128)(2,1)} %collective-permute-done.18.refs_2_), channel_id=1, source_target_pairs={{0,4},{1,5},{2,6},{3,7},{4,0},{5,1},{6,2},{7,3},{8,12},{9,13},{10,... | collective-permute-start | bytes 1572872 | tf_op jit(solution)/shard_map/ppermute | solution.py:38
  129.7 24.5 %collective-permute-start.14 = (bf16[1024,256]{1,0:T(8,128)(2,1)}, bf16[1024,256]{1,0:T(8,128)(2,1)}, u32[]{:S(2)}, u32[]{:S(2)}) collective-permute-start(bf16[1024,256]{1,0:T(8,128)(2,1)} %collective-permute-done.10.refs_2_), channel_id=1, source_target_pairs={{0,4},{1,5},{2,6},{3,7},{4,0},{5,1},{6,2},{7,3},{8,12},{9,13},{10,... | collective-permute-start | bytes 1572872 | tf_op jit(solution)/shard_map/ppermute | solution.py:38
  141.2 24.9 %collective-permute-start.4 = (bf16[1024,256]{1,0:T(8,128)(2,1)S(1)}, bf16[1024,256]{1,0:T(8,128)(2,1)S(1)}, u32[]{:S(2)}, u32[]{:S(2)}) collective-permute-start(bf16[1024,256]{1,0:T(8,128)(2,1)S(1)} %collective-permute-done.refs_0_), channel_id=1, source_target_pairs={{0,4},{1,5},{2,6},{3,7},{4,0},{5,1},{6,2},{7,3},{8,12},{9,13},{10,... | collective-permute-start | bytes 1572872 | tf_op jit(solution)/shard_map/ppermute | solution.py:38
  141.8 24.3 %collective-permute-start.7 = (bf16[1024,256]{1,0:T(8,128)(2,1)S(1)}, bf16[1024,256]{1,0:T(8,128)(2,1)S(1)}, u32[]{:S(2)}, u32[]{:S(2)}) collective-permute-start(bf16[1024,256]{1,0:T(8,128)(2,1)S(1)} %collective-permute-done.1.refs_1_), channel_id=1, source_target_pairs={{0,4},{1,5},{2,6},{3,7},{4,0},{5,1},{6,2},{7,3},{8,12},{9,13},{10,... | collective-permute-start | bytes 1572872 | tf_op jit(solution)/shard_map/ppermute | solution.py:38
  141.9 24.2 %collective-permute-start.5 = (bf16[1024,256]{1,0:T(8,128)(2,1)}, bf16[1024,256]{1,0:T(8,128)(2,1)S(1)}, u32[]{:S(2)}, u32[]{:S(2)}) collective-permute-start(bf16[1024,256]{1,0:T(8,128)(2,1)} %collective-permute-done.3.refs_3_), channel_id=1, source_target_pairs={{0,4},{1,5},{2,6},{3,7},{4,0},{5,1},{6,2},{7,3},{8,12},{9,13},{10,... | collective-permute-start | bytes 1572872 | tf_op jit(solution)/shard_map/ppermute | solution.py:38
  142.3 23.8 %collective-permute-start.6 = (bf16[1024,256]{1,0:T(8,128)(2,1)S(1)}, bf16[1024,256]{1,0:T(8,128)(2,1)}, u32[]{:S(2)}, u32[]{:S(2)}) collective-permute-start(bf16[1024,256]{1,0:T(8,128)(2,1)S(1)} %collective-permute-done.2.refs_2_), channel_id=1, source_target_pairs={{0,4},{1,5},{2,6},{3,7},{4,0},{5,1},{6,2},{7,3},{8,12},{9,13},{10,... | collective-permute-start | bytes 1572872 | tf_op jit(solution)/shard_map/ppermute | solution.py:38
  (18 other events, 431.9 us)

commit v2 on v1

v2 whole, which is shorter than its diff:
```python
import functools

import jax
import jax.numpy as jnp
from jax import lax
from jax.experimental import pallas as pl
from jax.experimental.pallas import tpu as pltpu
from jax.sharding import PartitionSpec as P

adapter_scale = 2.0
axes = ("blk", "seq")
f32 = jnp.float32
bf16 = jnp.bfloat16


def dot(a, b, contract):
    return lax.dot_general(a, b, (contract, ((), ())), preferred_element_type=f32)


class Layout:
    def __init__(self, mesh):
        self.blocks, self.seqs = mesh.shape["blk"], mesh.shape["seq"]
        self.depth = self.blocks // 2
        self.cycle = list(range(0, self.seqs, 2)) + list(range(self.seqs - 1, 0, -2))
        self.place = {seq: at for at, seq in enumerate(self.cycle)}
        self.forward_steps = self.seqs // 2
        self.backward_steps = self.seqs - 1 - self.forward_steps
        self.offsets = [0] + list(range(1, self.forward_steps + 1))
        self.offsets += [-step for step in range(1, self.backward_steps + 1)]

    def permute(self, value, target):
        pairs = []
        for blk in range(self.blocks):
            for seq in range(self.seqs):
                to_blk, to_seq = target(blk // 2, blk % 2, seq)
                pairs.append((blk * self.seqs + seq, to_blk * self.seqs + to_seq))
        moved = lax.ppermute(value, axes, pairs)
        if value.dtype == bf16:
            moved = pltpu.with_memory_space_constraint(moved, pltpu.HBM)
        return moved

    def along_depth(self, value, shift):
        return self.permute(
            value, lambda z, core, seq: (((z + shift) % self.depth) * 2 + core, seq)
        )

    def along_cycle(self, value, step):
        def target(z, core, seq):
            sign = step if core == 0 else -step
            return z * 2 + core, self.cycle[(self.place[seq] + sign) % self.seqs]

        return self.permute(value, target)

    def swap_cores(self, value):
        return self.permute(value, lambda z, core, seq: (z * 2 + 1 - core, seq))

    def column_of(self, core, seq):
        sign = 1 if core == 0 else -1
        return [
            self.cycle[(self.place[seq] - sign * offset) % self.seqs] for offset in self.offsets
        ]

    def rank(self, core, seq):
        bits = self.seqs.bit_length() - 1
        if core == 1:
            return seq
        return int("".join(reversed(format(seq, f"0{bits}b"))), 2)

    def seq_of_rank(self, core, rank):
        return next(s for s in range(self.seqs) if self.rank(core, s) == rank)

    def across_rank(self, value, flip):
        def target(z, core, seq):
            return z * 2 + core, self.seq_of_rank(core, self.rank(core, seq) ^ flip)

        return self.permute(value, target)


def local_kernel(steps, a_ref, c_ref, down_ref, up_ref, low_f_ref, low_b_ref, grad_ref, acc_ref):
    step = pl.program_id(0)
    width = a_ref.shape[1]

    @pl.when(step == 0)
    def _():
        low_b_ref[...] = dot(c_ref[...], up_ref[...], ((1,), (1,))).astype(bf16)
        acc_ref[...] = jnp.zeros_like(acc_ref)

    block = a_ref[...]
    acc_ref[...] += dot(block, down_ref[...], ((1,), (1,)))
    here = pl.ds(pl.multiple_of(step * width, width), width)
    grad_ref[:, here] = dot(low_b_ref[...], block, ((0,), (0,)))

    @pl.when(step == steps - 1)
    def _():
        low_f = acc_ref[...].astype(bf16)
        low_f_ref[...] = low_f
        grad_ref[:, steps * width :] = dot(low_f, c_ref[...], ((0,), (0,)))


def local_terms(a, c, down, up, steps):
    tokens, width = a.shape
    rank, keys = up.shape
    part = width // steps
    return pl.pallas_call(
        functools.partial(local_kernel, steps),
        grid=(steps,),
        in_specs=[
            pl.BlockSpec((tokens, part), lambda i: (0, i)),
            pl.BlockSpec((tokens, keys), lambda i: (0, 0)),
            pl.BlockSpec((rank, part), lambda i: (0, i)),
            pl.BlockSpec((rank, keys), lambda i: (0, 0)),
        ],
        out_specs=[
            pl.BlockSpec((tokens, rank), lambda i: (0, 0)),
            pl.BlockSpec((tokens, rank), lambda i: (0, 0)),
            pl.BlockSpec((rank, width + keys), lambda i: (0, 0)),
        ],
        out_shape=[
            jax.ShapeDtypeStruct((tokens, rank), bf16),
            jax.ShapeDtypeStruct((tokens, rank), bf16),
            jax.ShapeDtypeStruct((rank, width + keys), f32),
        ],
        scratch_shapes=[pltpu.VMEM((tokens, rank), f32)],
        compiler_params=pltpu.CompilerParams(vmem_limit_bytes=16 << 20),
        cost_estimate=pl.CostEstimate(
            flops=1, bytes_accessed=1, transcendentals=0
        ),
        name="local_terms",
    )(a, c, down, up)


def slab_kernel(layout, shift, first, last, *refs):
    count = layout.seqs
    pieces = [refs[:count], refs[count : 2 * count]]
    a_ref, c_ref, low_b_ref, down_ref, *refs = refs[2 * count :]
    if first:
        low_f_ref, up_ref, *refs = refs
    else:
        acc_in_ref, _, *refs = refs
    keys_ref, grad_ref, panel_ref, rows_a_ref, cot_ref, rows_down_ref, out_ref, *refs = refs
    if last:
        acc_ref, *refs = refs
    else:
        acc_ref = keys_ref
    panel_sem, a_sem, cot_sem, down_sem, out_sem = refs
    rows, part = pieces[0][0].shape
    chunks, size = panel_sem.shape[1], out_ref.shape[2]

    blk, seq = lax.axis_index("blk"), lax.axis_index("seq")
    z, core = blk // 2, blk % 2
    source = lax.rem(z + (layout.depth - shift), layout.depth)
    starts = [
        pl.multiple_of((source * 2 + core) * rows, rows),
        pl.multiple_of((source * 2 + 1 - core) * rows, rows),
    ]
    columns = []
    for j in range(count):
        column = jnp.int32(0)
        for k in range(2):
            for s in range(count):
                here = jnp.logical_and(core == k, seq == s)
                column = jnp.where(here, layout.column_of(k, s)[j], column)
        columns.append(pl.ds(pl.multiple_of(column * part, part), part))
    places = [pl.ds(j * part, part) for j in range(count)]

    def cot_copy(j):
        return pltpu.make_async_copy(
            c_ref.at[:, columns[j]], cot_ref.at[:, places[j]], cot_sem.at[j]
        )

    def panel_copy(k, r, j):
        span = pl.ds(r * size, size)
        return pltpu.make_async_copy(
            pieces[k][j].at[span, :], panel_ref.at[k, span, places[j]], panel_sem.at[k, r, j]
        )

    def a_copy(k):
        return pltpu.make_async_copy(
            a_ref.at[:, pl.ds(starts[k], rows)], rows_a_ref.at[k], a_sem.at[k]
        )

    def down_copy(k):
        return pltpu.make_async_copy(
            down_ref.at[:, pl.ds(starts[k], rows)], rows_down_ref.at[k], down_sem.at[k]
        )

    def out_copy(k, r):
        to = pl.ds(pl.multiple_of(starts[k] + r * size, size), size)
        return pltpu.make_async_copy(
            out_ref.at[k * chunks + r], grad_ref.at[:, to], out_sem.at[k, r]
        )

    for j in range(count):
        cot_copy(j).start()
    for k in range(2):
        down_copy(k).start()
        for r in range(chunks):
            for j in range(count):
                panel_copy(k, r, j).start()
        a_copy(k).start()

    low_b = low_b_ref[...] * jnp.asarray(adapter_scale, bf16)
    if first:
        low_f = low_f_ref[...] * jnp.asarray(adapter_scale, bf16)
        for j in range(count):
            acc_ref[:, places[j]] = dot(low_f, up_ref[:, columns[j]], ((1,), (0,)))
    for j in range(count):
        cot_copy(j).wait()
    for k in range(2):
        down_copy(k).wait()
        for r in range(chunks):
            for j in range(count):
                panel_copy(k, r, j).wait()
            span = slice(r * size, (r + 1) * size)
            grad = dot(cot_ref[...], panel_ref[k, span, :], ((1,), (1,)))
            grad += dot(low_b, rows_down_ref[k, :, span], ((1,), (0,)))
            out_ref[k * chunks + r] = grad.astype(bf16)
            out_copy(k, r).start()
        a_copy(k).wait()
        base = acc_ref if first or k else acc_in_ref
        acc_ref[...] = base[...] + dot(rows_a_ref[k], panel_ref[k], ((1,), (0,)))
    if last:
        for j in range(count):
            keys_ref[:, columns[j]] = acc_ref[:, places[j]].astype(bf16)
    for k in range(2):
        for r in range(chunks):
            out_copy(k, r).wait()


def slab(layout, shift, mine, other, a, c, low_b, down, low_f, up, acc, grad, first, last):
    count = len(mine)
    tokens, width = a.shape
    rank, keys = up.shape
    rows = mine[0].shape[0]
    chunks = max(1, rows // 512)
    size = rows // chunks
    whole = pl.BlockSpec(memory_space=pltpu.VMEM)
    remote = pl.BlockSpec(memory_space=pl.ANY)
    held = [pltpu.with_memory_space_constraint(piece, pltpu.HBM) for piece in [*mine, *other]]
    in_specs = [remote] * (2 * count + 2) + [whole, remote]
    operands = [*held, a, c, low_b, down]
    aliases = {}
    if first:
        in_specs += [whole, whole]
        operands += [low_f, up]
    else:
        in_specs += [whole, remote]
        operands += [pltpu.with_memory_space_constraint(acc, pltpu.VMEM), grad]
        aliases = {len(operands) - 1: 1}
        if not last:
            aliases[len(operands) - 2] = 0
    keys_type = jax.ShapeDtypeStruct if last else pltpu.VMEM
    scratch = [
        pltpu.VMEM((2, rows, keys), bf16),
        pltpu.VMEM((2, tokens, rows), bf16),
        pltpu.VMEM((tokens, keys), bf16),
        pltpu.VMEM((2, rank, rows), bf16),
        pltpu.VMEM((2 * chunks, tokens, size), bf16),
    ]
    scratch += [pltpu.VMEM((tokens, keys), f32)] if last else []
    scratch += [
        pltpu.SemaphoreType.DMA((2, chunks, count)),
        pltpu.SemaphoreType.DMA((2,)),
        pltpu.SemaphoreType.DMA((count,)),
        pltpu.SemaphoreType.DMA((2,)),
        pltpu.SemaphoreType.DMA((2, chunks)),
    ]
    return pl.pallas_call(
        functools.partial(slab_kernel, layout, shift, first, last),
        in_specs=in_specs,
        out_specs=[whole, remote],
        scratch_shapes=scratch,
        out_shape=[
            keys_type((tokens, keys), bf16 if last else f32),
            jax.ShapeDtypeStruct((tokens, width), bf16),
        ],
        input_output_aliases=aliases,
        compiler_params=pltpu.CompilerParams(vmem_limit_bytes=24 << 20),
        cost_estimate=pl.CostEstimate(
            flops=1, bytes_accessed=1, transcendentals=0
        ),
        name="slab",
    )(*operands)


def stages_of(layout):
    depth, rounds = layout.depth, layout.forward_steps
    if (depth, layout.seqs) == (4, 4):
        exchanges = [
            ("turn", 0, 1),
            ("turn", 0, -1),
            ("turn", 0, 2),
            ("sum",),
            ("turn", 1, 1),
            ("turn", 1, -1),
            ("turn", 1, 2),
            ("turn", 2, 1),
            ("turn", 3, 1),
            ("turn", 2, 2),
            ("turn", 3, 2),
            ("sum",),
        ]
        besides = {
            0: [("rise", 1, 0, 0), ("local",)],
            2: [("rise", 2, 0, 0)],
            4: [("rise", 3, 0, 1)],
            5: [("slab", 0)],
            6: [("rise", 2, -1, 0)],
            8: [("rise", 3, -1, 1), ("slab", 1)],
            10: [("slab", 2)],
        }
        stages = []
        for at, exchange in enumerate(exchanges[:-1]):
            starts = exchanges[: 2] if at == 0 else exchanges[at + 1 : at + 2]
            starts = starts + besides.get(at, [])
            dones = [exchange]
            dones += [name for name in besides.get(at - 1, []) if name[0] == "rise"]
            stages.append((starts, dones))
        return stages
    stages = [([("local",), ("rise", 1, 0, 0)], [("rise", 1, 0, 0)])]
    for at in range(depth):
        for step in range(1, rounds + 1):
            starts = [("turn", at, step)]
            if step <= layout.backward_steps:
                starts.append(("turn", at, -step))
            dones = list(starts)
            if step == 1 and 0 < at < depth - 1:
                starts.append(("rise", at + 1, 0, 0))
            if step == rounds and at:
                dones.append(("rise", at + 1, 0, 0))
                starts.append(("slab", at - 1))
            stages.append((starts, dones))
    stages += [([("sum",)], [("sum",)])] * (layout.seqs.bit_length() - 1)
    return stages


def body(layout, activations, base_weight, adapter_down, adapter_up, cotangent):
    a, down, up, c = activations[0], adapter_down[0], adapter_up[0], cotangent[0]
    count, depth, width = layout.seqs, layout.depth, activations.shape[2]
    a, c, down, up = (pltpu.with_memory_space_constraint(x, pltpu.HBM) for x in (a, c, down, up))
    scale = adapter_scale / (a.shape[0] * count)

    shifts = [0]
    for step in range(1, depth // 2 + 1):
        shifts += [step] if 2 * step == depth else [step, depth - step]

    here = {("mine", 0, 0): base_weight}
    flying = {}
    state = {}
    flips = [layout.seqs >> step for step in range(1, layout.seqs.bit_length())]
    swapped = set()

    def result_of(name):
        return ("mine", *name[1:3]) if name[0] in ("turn", "rise") else name

    def multiply(at):
        for name in [name for name in flying if name[0] == "other" and name[1] == at]:
            here[name] = flying.pop(name)
        mine = [here[("mine", at, offset)] for offset in layout.offsets]
        other = [here.pop(("other", at, offset)) for offset in layout.offsets]
        state["acc"], state["grad"] = slab(
            layout, shifts[at], mine, other, a, c, state["low_b"], down, state["low_f"], up,
            state.get("acc"), state.get("grad"), at == 0, at == depth - 1,
        )

    def swap_ready():
        names = []
        for side, at, offset in list(here):
            turned = next(o for o in layout.offsets if (o + offset) % count == 0)
            name = ("other", at, turned)
            if side == "mine" and name not in swapped:
                swapped.add(name)
                flying[name] = layout.swap_cores(here[(side, at, offset)])
                names.append(name)
        return names

    def start(name):
        if name[0] == "local":
            state["low_f"], state["low_b"], state["sum"] = local_terms(a, c, down, up, count)
        elif name[0] == "slab":
            multiply(name[1])
        elif name[0] == "rise":
            _, at, offset, source = name
            shift = (shifts[at] - shifts[source]) % depth
            flying[result_of(name)] = layout.along_depth(here[("mine", source, offset)], shift)
        elif name[0] == "sum":
            flying[name] = layout.across_rank(state["sum"], flips.pop(0))
        else:
            _, at, offset = name
            step = 1 if offset > 0 else -1
            flying[result_of(name)] = layout.along_cycle(here[("mine", at, offset - step)], step)

    def close(names):
        for name in names:
            if name in flying:
                value = flying.pop(name)
                if name[0] == "sum":
                    state["sum"] = state["sum"] + value
                else:
                    here[name] = value
        new_here, new_state = lax.optimization_barrier((dict(here), dict(state)))
        here.update(new_here)
        state.update(new_state)

    turning = []
    for starts, dones in stages_of(layout):
        for name in starts:
            if name[0] not in ("local", "slab"):
                start(name)
        late, turning = turning, swap_ready()
        for name in starts:
            if name[0] in ("local", "slab"):
                start(name)
        close([result_of(name) for name in dones] + late)
    close([name for name in flying if name[0] != "sum"])
    swap_ready()
    multiply(depth - 1)
    sums = state["sum"]
    if "sum" in [name[0] for name in flying]:
        sums = sums + flying[("sum",)]
    state["down"], state["up"] = sums[:, :width] * scale, sums[:, width:] * scale
    return tuple(state[name][None] for name in ("acc", "grad", "down", "up"))


def solution(mesh):
    return jax.shard_map(
        functools.partial(body, Layout(mesh)),
        mesh=mesh,
        in_specs=(
            P("blk", "seq", None),
            P("blk", "seq"),
            P("blk", None, None),
            P("blk", None, None),
            P("blk", "seq", None),
        ),
        out_specs=(
            P("blk", "seq", None),
            P("blk", "seq", None),
            P("blk", None, None),
            P("blk", None, None),
        ),
        check_vma=False,
    )
```

time: 179 us -> 121 us (0.68)
  waiting for transfers between devices: 82.8 us -> 46.4 us
  Pallas kernels: 54.8 us -> 44.9 us
  local copies, waits for them, and re-layouts: 6.34 us -> 2.5 us
  starting transfers between devices: 27.9 us -> 24.2 us
  between operations: 3.68 us -> 1.17 us
  other arithmetic: 3.53 us -> 1.59 us
    ppermute x35 -> x33, waiting for transfers between devices: 82.8 us -> 46.4 us  [permute(): moved = lax.ppermute(value, axes, pairs)]
    pallas_call x4, Pallas kernels: 46.7 us -> 37.8 us  [slab(): pl.pallas_call(functools.partial(slab_kernel, layout, shift, first, last)...]
    ppermute x35 -> x33, starting transfers between devices: 27.9 us -> 24.2 us  [permute(): moved = lax.ppermute(value, axes, pairs)]
    dynamic_slice x3 -> x0, local copies, waits for them, and re-layouts: 2.27 us -> none  [the longest x1 1.27 us: body(): my_rank = jnp.asarray(ranks)[core, seq]]
    another operation x2 -> x0, local copies, waits for them, and re-layouts: 1.82 us -> none  [body(): return (acc[None], grad[None], down_gradient[None], up_gradient[None])]
  transfers between devices with their start and end apart: 35 -> 33, of which waited for: 13 -> 12; matrix products, arithmetic and copies ran while one was open for 3% -> 1% of each run, Pallas kernels for 20% -> 29%
where the time goes in v2:
time: 121 us
  waiting for transfers between devices  46.4 us (38%)
  Pallas kernels  44.9 us (37%)
  starting transfers between devices  24.2 us (20%)
  local copies, waits for them, and re-layouts  2.5 us (2%)
  other arithmetic  1.59 us (1%)
    ppermute x33, waiting for transfers between devices, permute(): moved = lax.ppermute(value, axes, pairs)  46.4 us
    pallas_call x4, Pallas kernels, slab(): pl.pallas_call(functools.partial(slab_kernel, layout, shift, first, last)...  37.8 us
    ppermute x33, starting transfers between devices, permute(): moved = lax.ppermute(value, axes, pairs)  24.2 us
    pallas_call x1, Pallas kernels, local_terms(): pl.pallas_call(functools.partial(local_kernel, steps), grid=(steps,), in_...  7.09 us
    unnamed x64, local copies, waits for them, and re-layouts  2.5 us
  transfers between devices with their start and end apart: 33, of which 12 were waited for; matrix products, arithmetic and copies ran while one was open for 1% of the time, Pallas kernels for 29%

profile of v2, /device:TPU:0, one launch (start us, length us, event | category | flops | bytes accessed | tf_op | source)
XLA Modules:
  0.0 120.8 jit_solution(16464168679860509624)
XLA Ops:
  0.6 3.0 %collective-permute-start.1 = (bf16[1024,256]{1,0:T(8,128)(2,1)}, bf16[1024,256]{1,0:T(8,128)(2,1)S(1)}, u32[]{:S(2)}, u32[]{:S(2)}) collective-permute-start(bf16[1024,256]{1,0:T(8,128)(2,1)} %refs_0_), channel_id=1, source_target_pairs={{0,2},{1,0},{2,3},{3,1},{4,5},{5,7},{6,4},{7,6},{8,10},{9,8},{10,1... | collective-permute-start | bytes 1572872 | tf_op jit(solution)/shard_map/ppermute | solution.py:37
  3.7 2.0 %collective-permute-start.2 = (bf16[1024,256]{1,0:T(8,128)(2,1)}, bf16[1024,256]{1,0:T(8,128)(2,1)S(1)}, u32[]{:S(2)}, u32[]{:S(2)}) collective-permute-start(bf16[1024,256]{1,0:T(8,128)(2,1)} %refs_0_), channel_id=1, source_target_pairs={{0,8},{1,9},{2,10},{3,11},{4,12},{5,13},{6,14},{7,15},{8,16},{9,17... | collective-permute-start | bytes 1572872 | tf_op jit(solution)/shard_map/ppermute | solution.py:37
  5.7 7.1 %local_terms.1 = (bf16[512,16]{1,0:T(8,128)(2,1)S(1)}, bf16[512,16]{1,0:T(8,128)(2,1)S(1)}, f32[16,9216]{1,0:T(8,128)S(1)}) custom-call(bf16[512,8192]{1,0:T(8,128)(2,1)} %bitcast.10, bf16[512,1024]{1,0:T(8,128)(2,1)} %bitcast.16, bf16[16,8192]{1,0:T(8,128)(2,1)} %bitcast.21, bf16[16,1024]{1,0:T(8,128)(2,1)} %bitcast.26), custom_call_target="tpu_custom_call" | custom-call | flops 1 | bytes 1 | tf_op jit(solution)/shard_map/local_terms/pallas_call | solution.py:104
  12.8 3.3 %collective-permute-done.1.refs_1_ = bf16[1024,256]{1,0:T(8,128)(2,1)S(1)} collective-permute-done((bf16[1024,256]{1,0:T(8,128)(2,1)}, bf16[1024,256]{1,0:T(8,128)(2,1)S(1)}, u32[]{:S(2)}, u32[]{:S(2)}) %collective-permute-start.1) | collective-permute-done | bytes 524320 | tf_op jit(solution)/shard_map/ppermute | solution.py:37
  16.1 3.3 %collective-permute-done.2.refs_0_ = bf16[1024,256]{1,0:T(8,128)(2,1)S(1)} collective-permute-done((bf16[1024,256]{1,0:T(8,128)(2,1)}, bf16[1024,256]{1,0:T(8,128)(2,1)S(1)}, u32[]{:S(2)}, u32[]{:S(2)}) %collective-permute-start.2) | collective-permute-done | bytes 524320 | tf_op jit(solution)/shard_map/ppermute | solution.py:37
  19.4 1.6 %collective-permute-start.9 = (f32[16,9216]{1,0:T(8,128)S(1)}, f32[16,9216]{1,0:T(8,128)S(1)}, u32[]{:S(2)}, u32[]{:S(2)}) collective-permute-start(f32[16,9216]{1,0:T(8,128)S(1)} %get-tuple-element.180), channel_id=1, source_target_pairs={{0,1},{1,0},{2,3},{3,2},{4,6},{5,7},{6,4},{7,5},{8,9},{9,8},{10,11... | collective-permute-start | bytes 1769480 | tf_op jit(solution)/shard_map/ppermute | solution.py:37
  20.9 1.5 %collective-permute-start.4 = (bf16[1024,256]{1,0:T(8,128)(2,1)S(1)}, bf16[1024,256]{1,0:T(8,128)(2,1)S(1)}, u32[]{:S(2)}, u32[]{:S(2)}) collective-permute-start(bf16[1024,256]{1,0:T(8,128)(2,1)S(1)} %collective-permute-done.1.refs_1_), channel_id=1, source_target_pairs={{0,2},{1,0},{2,3},{3,1},{4,5},{5,7},{6,4},{7,6},{8,10},{9,8},{10,1... | collective-permute-start | bytes 1572872 | tf_op jit(solution)/shard_map/ppermute | solution.py:37
  22.5 1.7 %collective-permute-start.6 = (bf16[1024,256]{1,0:T(8,128)(2,1)S(1)}, bf16[1024,256]{1,0:T(8,128)(2,1)S(1)}, u32[]{:S(2)}, u32[]{:S(2)}) collective-permute-start(bf16[1024,256]{1,0:T(8,128)(2,1)S(1)} %copy-done), channel_id=1, source_target_pairs={{0,24},{1,25},{2,26},{3,27},{4,28},{5,29},{6,30},{7,31},{8,0},{9,1... | collective-permute-start | bytes 1572872 | tf_op jit(solution)/shard_map/ppermute | solution.py:37
  24.4 10.5 %collective-permute-done.4.refs_2_ = bf16[1024,256]{1,0:T(8,128)(2,1)S(1)} collective-permute-done((bf16[1024,256]{1,0:T(8,128)(2,1)S(1)}, bf16[1024,256]{1,0:T(8,128)(2,1)S(1)}, u32[]{:S(2)}, u32[]{:S(2)}) %collective-permute-start.4) | collective-permute-done | bytes 524320 | tf_op jit(solution)/shard_map/ppermute | solution.py:37
  35.0 0.6 collective-permute-start.10
  35.6 1.2 collective-permute-done.6.refs_0_
  36.9 1.5 %collective-permute-start.12 = (bf16[1024,256]{1,0:T(8,128)(2,1)S(1)}, bf16[1024,256]{1,0:T(8,128)(2,1)S(1)}, u32[]{:S(2)}, u32[]{:S(2)}) collective-permute-start(bf16[1024,256]{1,0:T(8,128)(2,1)S(1)} %collective-permute-done.2.refs_0_), channel_id=1, source_target_pairs={{0,1},{1,3},{2,0},{3,2},{4,6},{5,4},{6,7},{7,5},{8,9},{9,11},{10,8... | collective-permute-start | bytes 1572872 | tf_op jit(solution)/shard_map/ppermute | solution.py:37
  38.4 10.4 %collective-permute-done.10.refs_1_ = bf16[1024,256]{1,0:T(8,128)(2,1)S(1)} collective-permute-done((bf16[1024,256]{1,0:T(8,128)(2,1)S(1)}, bf16[1024,256]{1,0:T(8,128)(2,1)S(1)}, u32[]{:S(2)}, u32[]{:S(2)}) %collective-permute-start.10) | collective-permute-done | bytes 524320 | tf_op jit(solution)/shard_map/ppermute | solution.py:37
  48.8 0.5 collective-permute-start.15
  49.7 9.6 %slab.4 = (f32[512,1024]{1,0:T(8,128)S(1)}, bf16[512,8192]{1,0:T(8,128)(2,1)}) custom-call(bf16[1024,256]{1,0:T(8,128)(2,1)} %refs_0_, bf16[1024,256]{1,0:T(8,128)(2,1)} %copy-done.2, bf16[1024,256]{1,0:T(8,128)(2,1)} %copy-done.4, bf16[1024,256]{1,0:T(8,128)(2,1)} %copy-done.1, bf16[1024,256]{1,0:T(8,128)(2,1)} %copy-done.3, bf16[1024,256]{1,0:T(8,128)(2,1)} %copy-done.6, ...), custom_call_target="tpu_custom_call" | custom-call | flops 1 | bytes 1 | tf_op jit(solution)/shard_map/slab/pallas_call | solution.py:268
  59.3 1.5 %collective-permute-start.17 = (bf16[1024,256]{1,0:T(8,128)(2,1)}, bf16[1024,256]{1,0:T(8,128)(2,1)S(1)}, u32[]{:S(2)}, u32[]{:S(2)}) collective-permute-start(bf16[1024,256]{1,0:T(8,128)(2,1)} %copy-done.1), channel_id=1, source_target_pairs={{0,24},{1,25},{2,26},{3,27},{4,28},{5,29},{6,30},{7,31},{8,0},{9,1... | collective-permute-start | bytes 1572872 | tf_op jit(solution)/shard_map/ppermute | solution.py:37
  60.8 2.5 %collective-permute-start.18 = (bf16[1024,256]{1,0:T(8,128)(2,1)S(1)}, bf16[1024,256]{1,0:T(8,128)(2,1)S(1)}, u32[]{:S(2)}, u32[]{:S(2)}) collective-permute-start(bf16[1024,256]{1,0:T(8,128)(2,1)S(1)} %collective-permute-done.6.refs_0_), channel_id=1, source_target_pairs={{0,2},{1,0},{2,3},{3,1},{4,5},{5,7},{6,4},{7,6},{8,10},{9,8},{10,1... | collective-permute-start | bytes 1572872 | tf_op jit(solution)/shard_map/ppermute | solution.py:37
  63.9 9.7 %collective-permute-done.17.refs_3_ = bf16[1024,256]{1,0:T(8,128)(2,1)S(1)} collective-permute-done((bf16[1024,256]{1,0:T(8,128)(2,1)}, bf16[1024,256]{1,0:T(8,128)(2,1)S(1)}, u32[]{:S(2)}, u32[]{:S(2)}) %collective-permute-start.17) | collective-permute-done | bytes 524320 | tf_op jit(solution)/shard_map/ppermute | solution.py:37
  73.6 2.5 %collective-permute-start.21 = (bf16[1024,256]{1,0:T(8,128)(2,1)S(1)}, bf16[1024,256]{1,0:T(8,128)(2,1)S(1)}, u32[]{:S(2)}, u32[]{:S(2)}) collective-permute-start(bf16[1024,256]{1,0:T(8,128)(2,1)S(1)} %collective-permute-done.13.refs_0_), channel_id=1, source_target_pairs={{0,2},{1,0},{2,3},{3,1},{4,5},{5,7},{6,4},{7,6},{8,10},{9,8},{10,1... | collective-permute-start | bytes 1572872 | tf_op jit(solution)/shard_map/ppermute | solution.py:37
  77.5 9.0 %slab.5 = (f32[512,1024]{1,0:T(8,128)S(1)}, bf16[512,8192]{1,0:T(8,128)(2,1)}) custom-call(bf16[1024,256]{1,0:T(8,128)(2,1)} %copy-done.10, bf16[1024,256]{1,0:T(8,128)(2,1)} %copy-done.14, bf16[1024,256]{1,0:T(8,128)(2,1)} %copy-done.20, bf16[1024,256]{1,0:T(8,128)(2,1)} %copy-done.16, ...), custom_call_target="tpu_custom_call", output_to_operand_aliasing={{1}: (13, {}), {0}: (12, {})} | custom-call | flops 1 | bytes 1 | tf_op jit(solution)/shard_map/slab/pallas_call | solution.py:268
  86.6 1.9 %collective-permute-done.23.refs_2_ = bf16[1024,256]{1,0:T(8,128)(2,1)S(1)} collective-permute-done((bf16[1024,256]{1,0:T(8,128)(2,1)S(1)}, bf16[1024,256]{1,0:T(8,128)(2,1)S(1)}, u32[]{:S(2)}, u32[]{:S(2)}) %collective-permute-start.23) | collective-permute-done | bytes 524320 | tf_op jit(solution)/shard_map/ppermute | solution.py:37
  88.5 4.0 %collective-permute-done.24.refs_3_ = bf16[1024,256]{1,0:T(8,128)(2,1)S(1)} collective-permute-done((bf16[1024,256]{1,0:T(8,128)(2,1)S(1)}, bf16[1024,256]{1,0:T(8,128)(2,1)S(1)}, u32[]{:S(2)}, u32[]{:S(2)}) %collective-permute-start.24) | collective-permute-done | bytes 524320 | tf_op jit(solution)/shard_map/ppermute | solution.py:37
  92.5 1.0 collective-permute-start.32
  94.0 0.6 collective-permute-start.27
  95.5 0.8 copy-done.30
  96.3 9.0 %slab.6 = (f32[512,1024]{1,0:T(8,128)S(1)}, bf16[512,8192]{1,0:T(8,128)(2,1)}) custom-call(bf16[1024,256]{1,0:T(8,128)(2,1)} %copy-done.8, bf16[1024,256]{1,0:T(8,128)(2,1)} %copy-done.18, bf16[1024,256]{1,0:T(8,128)(2,1)} %copy-done.22, bf16[1024,256]{1,0:T(8,128)(2,1)} %copy-done.17, ...), custom_call_target="tpu_custom_call", output_to_operand_aliasing={{1}: (13, {}), {0}: (12, {})} | custom-call | flops 1 | bytes 1 | tf_op jit(solution)/shard_map/slab/pallas_call | solution.py:268
  105.3 1.7 %collective-permute-done.27.refs_2_ = bf16[1024,256]{1,0:T(8,128)(2,1)S(1)} collective-permute-done((bf16[1024,256]{1,0:T(8,128)(2,1)S(1)}, bf16[1024,256]{1,0:T(8,128)(2,1)S(1)}, u32[]{:S(2)}, u32[]{:S(2)}) %collective-permute-start.27) | collective-permute-done | bytes 524320 | tf_op jit(solution)/shard_map/ppermute | solution.py:37
  107.0 0.9 collective-permute-start.31
  108.1 0.8 fusion
  109.0 0.6 fusion.1
  109.6 0.8 copy-done.31
  110.4 10.3 %slab.7 = (bf16[512,1024]{1,0:T(8,128)(2,1)}, bf16[512,8192]{1,0:T(8,128)(2,1)}) custom-call(bf16[1024,256]{1,0:T(8,128)(2,1)} %copy-done.9, bf16[1024,256]{1,0:T(8,128)(2,1)} %copy-done.15, bf16[1024,256]{1,0:T(8,128)(2,1)} %copy-done.26, bf16[1024,256]{1,0:T(8,128)(2,1)} %copy-done.19, ...), custom_call_target="tpu_custom_call", output_to_operand_aliasing={{1}: (13, {})} | custom-call | flops 1 | bytes 1 | tf_op jit(solution)/shard_map/slab/pallas_call | solution.py:268
  (107 shorter events, 4.1 us)
Async XLA Ops:
  0.6 15.5 %collective-permute-start.1 = (bf16[1024,256]{1,0:T(8,128)(2,1)}, bf16[1024,256]{1,0:T(8,128)(2,1)S(1)}, u32[]{:S(2)}, u32[]{:S(2)}) collective-permute-start(bf16[1024,256]{1,0:T(8,128)(2,1)} %refs_0_), channel_id=1, source_target_pairs={{0,2},{1,0},{2,3},{3,1},{4,5},{5,7},{6,4},{7,6},{8,10},{9,8},{10,1... | collective-permute-start | bytes 1572872 | tf_op jit(solution)/shard_map/ppermute | solution.py:37
  3.7 12.4 %collective-permute-start = (bf16[1024,256]{1,0:T(8,128)(2,1)}, bf16[1024,256]{1,0:T(8,128)(2,1)S(1)}, u32[]{:S(2)}, u32[]{:S(2)}) collective-permute-start(bf16[1024,256]{1,0:T(8,128)(2,1)} %refs_0_), channel_id=1, source_target_pairs={{0,1},{1,3},{2,0},{3,2},{4,6},{5,4},{6,7},{7,5},{8,9},{9,11},{10,8... | collective-permute-start | bytes 1572872 | tf_op jit(solution)/shard_map/ppermute | solution.py:37
  3.7 15.7 %collective-permute-start.2 = (bf16[1024,256]{1,0:T(8,128)(2,1)}, bf16[1024,256]{1,0:T(8,128)(2,1)S(1)}, u32[]{:S(2)}, u32[]{:S(2)}) collective-permute-start(bf16[1024,256]{1,0:T(8,128)(2,1)} %refs_0_), channel_id=1, source_target_pairs={{0,8},{1,9},{2,10},{3,11},{4,12},{5,13},{6,14},{7,15},{8,16},{9,17... | collective-permute-start | bytes 1572872 | tf_op jit(solution)/shard_map/ppermute | solution.py:37
  5.7 13.6 %collective-permute-start.3 = (bf16[1024,256]{1,0:T(8,128)(2,1)}, bf16[1024,256]{1,0:T(8,128)(2,1)S(1)}, u32[]{:S(2)}, u32[]{:S(2)}) collective-permute-start(bf16[1024,256]{1,0:T(8,128)(2,1)} %refs_0_), channel_id=1, source_target_pairs={{0,4},{1,5},{2,6},{3,7},{4,0},{5,1},{6,2},{7,3},{8,12},{9,13},{10,... | collective-permute-start | bytes 1572872 | tf_op jit(solution)/shard_map/ppermute | solution.py:37
  19.4 16.2 %collective-permute-start.9 = (f32[16,9216]{1,0:T(8,128)S(1)}, f32[16,9216]{1,0:T(8,128)S(1)}, u32[]{:S(2)}, u32[]{:S(2)}) collective-permute-start(f32[16,9216]{1,0:T(8,128)S(1)} %get-tuple-element.180), channel_id=1, source_target_pairs={{0,1},{1,0},{2,3},{3,2},{4,6},{5,7},{6,4},{7,5},{8,9},{9,8},{10,11... | collective-permute-start | bytes 1769480 | tf_op jit(solution)/shard_map/ppermute | solution.py:37
  20.9 14.0 %collective-permute-start.4 = (bf16[1024,256]{1,0:T(8,128)(2,1)S(1)}, bf16[1024,256]{1,0:T(8,128)(2,1)S(1)}, u32[]{:S(2)}, u32[]{:S(2)}) collective-permute-start(bf16[1024,256]{1,0:T(8,128)(2,1)S(1)} %collective-permute-done.1.refs_1_), channel_id=1, source_target_pairs={{0,2},{1,0},{2,3},{3,1},{4,5},{5,7},{6,4},{7,6},{8,10},{9,8},{10,1... | collective-permute-start | bytes 1572872 | tf_op jit(solution)/shard_map/ppermute | solution.py:37
  22.5 12.5 %collective-permute-start.5 = (bf16[1024,256]{1,0:T(8,128)(2,1)S(1)}, bf16[1024,256]{1,0:T(8,128)(2,1)S(1)}, u32[]{:S(2)}, u32[]{:S(2)}) collective-permute-start(bf16[1024,256]{1,0:T(8,128)(2,1)S(1)} %collective-permute-done.1.refs_1_), channel_id=1, source_target_pairs={{0,4},{1,5},{2,6},{3,7},{4,0},{5,1},{6,2},{7,3},{8,12},{9,13},{10,... | collective-permute-start | bytes 1572872 | tf_op jit(solution)/shard_map/ppermute | solution.py:37
  22.5 14.3 %collective-permute-start.6 = (bf16[1024,256]{1,0:T(8,128)(2,1)S(1)}, bf16[1024,256]{1,0:T(8,128)(2,1)S(1)}, u32[]{:S(2)}, u32[]{:S(2)}) collective-permute-start(bf16[1024,256]{1,0:T(8,128)(2,1)S(1)} %copy-done), channel_id=1, source_target_pairs={{0,24},{1,25},{2,26},{3,27},{4,28},{5,29},{6,30},{7,31},{8,0},{9,1... | collective-permute-start | bytes 1572872 | tf_op jit(solution)/shard_map/ppermute | solution.py:37
  24.2 12.6 %collective-permute-start.7 = (bf16[1024,256]{1,0:T(8,128)(2,1)S(1)}, bf16[1024,256]{1,0:T(8,128)(2,1)S(1)}, u32[]{:S(2)}, u32[]{:S(2)}) collective-permute-start(bf16[1024,256]{1,0:T(8,128)(2,1)S(1)} %collective-permute-done.refs_3_), channel_id=1, source_target_pairs={{0,4},{1,5},{2,6},{3,7},{4,0},{5,1},{6,2},{7,3},{8,12},{9,13},{10,... | collective-permute-start | bytes 1572872 | tf_op jit(solution)/shard_map/ppermute | solution.py:37
  35.0 13.8 %collective-permute-start.10 = (bf16[1024,256]{1,0:T(8,128)(2,1)S(1)}, bf16[1024,256]{1,0:T(8,128)(2,1)S(1)}, u32[]{:S(2)}, u32[]{:S(2)}) collective-permute-start(bf16[1024,256]{1,0:T(8,128)(2,1)S(1)} %collective-permute-done.2.refs_0_), channel_id=1, source_target_pairs={{0,2},{1,0},{2,3},{3,1},{4,5},{5,7},{6,4},{7,6},{8,10},{9,8},{10,1... | collective-permute-start | bytes 1572872 | tf_op jit(solution)/shard_map/ppermute | solution.py:37
  35.5 13.3 %collective-permute-start.11 = (bf16[1024,256]{1,0:T(8,128)(2,1)S(1)}, bf16[1024,256]{1,0:T(8,128)(2,1)S(1)}, u32[]{:S(2)}, u32[]{:S(2)}) collective-permute-start(bf16[1024,256]{1,0:T(8,128)(2,1)S(1)} %collective-permute-done.4.refs_2_), channel_id=1, source_target_pairs={{0,4},{1,5},{2,6},{3,7},{4,0},{5,1},{6,2},{7,3},{8,12},{9,13},{10,... | collective-permute-start | bytes 1572872 | tf_op jit(solution)/shard_map/ppermute | solution.py:37
  36.9 22.4 %collective-permute-start.12 = (bf16[1024,256]{1,0:T(8,128)(2,1)S(1)}, bf16[1024,256]{1,0:T(8,128)(2,1)S(1)}, u32[]{:S(2)}, u32[]{:S(2)}) collective-permute-start(bf16[1024,256]{1,0:T(8,128)(2,1)S(1)} %collective-permute-done.2.refs_0_), channel_id=1, source_target_pairs={{0,1},{1,3},{2,0},{3,2},{4,6},{5,4},{6,7},{7,5},{8,9},{9,11},{10,8... | collective-permute-start | bytes 1572872 | tf_op jit(solution)/shard_map/ppermute | solution.py:37
  38.4 20.9 %collective-permute-start.13 = (bf16[1024,256]{1,0:T(8,128)(2,1)S(1)}, bf16[1024,256]{1,0:T(8,128)(2,1)S(1)}, u32[]{:S(2)}, u32[]{:S(2)}) collective-permute-start(bf16[1024,256]{1,0:T(8,128)(2,1)S(1)} %collective-permute-done.2.refs_0_), channel_id=1, source_target_pairs={{0,8},{1,9},{2,10},{3,11},{4,12},{5,13},{6,14},{7,15},{8,16},{9,17... | collective-permute-start | bytes 1572872 | tf_op jit(solution)/shard_map/ppermute | solution.py:37
  38.4 20.9 %collective-permute-start.14 = (bf16[1024,256]{1,0:T(8,128)(2,1)S(1)}, bf16[1024,256]{1,0:T(8,128)(2,1)S(1)}, u32[]{:S(2)}, u32[]{:S(2)}) collective-permute-start(bf16[1024,256]{1,0:T(8,128)(2,1)S(1)} %collective-permute-done.6.refs_0_), channel_id=1, source_target_pairs={{0,4},{1,5},{2,6},{3,7},{4,0},{5,1},{6,2},{7,3},{8,12},{9,13},{10,... | collective-permute-start | bytes 1572872 | tf_op jit(solution)/shard_map/ppermute | solution.py:37
  48.8 14.5 %collective-permute-start.15 = (bf16[1024,256]{1,0:T(8,128)(2,1)S(1)}, bf16[1024,256]{1,0:T(8,128)(2,1)S(1)}, u32[]{:S(2)}, u32[]{:S(2)}) collective-permute-start(bf16[1024,256]{1,0:T(8,128)(2,1)S(1)} %collective-permute-done.10.refs_1_), channel_id=1, source_target_pairs={{0,2},{1,0},{2,3},{3,1},{4,5},{5,7},{6,4},{7,6},{8,10},{9,8},{10,1... | collective-permute-start | bytes 1572872 | tf_op jit(solution)/shard_map/ppermute | solution.py:37
  49.3 14.5 %collective-permute-start.16 = (bf16[1024,256]{1,0:T(8,128)(2,1)S(1)}, bf16[1024,256]{1,0:T(8,128)(2,1)S(1)}, u32[]{:S(2)}, u32[]{:S(2)}) collective-permute-start(bf16[1024,256]{1,0:T(8,128)(2,1)S(1)} %collective-permute-done.10.refs_1_), channel_id=1, source_target_pairs={{0,4},{1,5},{2,6},{3,7},{4,0},{5,1},{6,2},{7,3},{8,12},{9,13},{10,... | collective-permute-start | bytes 1572872 | tf_op jit(solution)/shard_map/ppermute | solution.py:37
  59.3 14.3 %collective-permute-start.17 = (bf16[1024,256]{1,0:T(8,128)(2,1)}, bf16[1024,256]{1,0:T(8,128)(2,1)S(1)}, u32[]{:S(2)}, u32[]{:S(2)}) collective-permute-start(bf16[1024,256]{1,0:T(8,128)(2,1)} %copy-done.1), channel_id=1, source_target_pairs={{0,24},{1,25},{2,26},{3,27},{4,28},{5,29},{6,30},{7,31},{8,0},{9,1... | collective-permute-start | bytes 1572872 | tf_op jit(solution)/shard_map/ppermute | solution.py:37
  60.8 15.4 %collective-permute-start.18 = (bf16[1024,256]{1,0:T(8,128)(2,1)S(1)}, bf16[1024,256]{1,0:T(8,128)(2,1)S(1)}, u32[]{:S(2)}, u32[]{:S(2)}) collective-permute-start(bf16[1024,256]{1,0:T(8,128)(2,1)S(1)} %collective-permute-done.6.refs_0_), channel_id=1, source_target_pairs={{0,2},{1,0},{2,3},{3,1},{4,5},{5,7},{6,4},{7,6},{8,10},{9,8},{10,1... | collective-permute-start | bytes 1572872 | tf_op jit(solution)/shard_map/ppermute | solution.py:37
  63.3 12.8 %collective-permute-start.19 = (bf16[1024,256]{1,0:T(8,128)(2,1)S(1)}, bf16[1024,256]{1,0:T(8,128)(2,1)S(1)}, u32[]{:S(2)}, u32[]{:S(2)}) collective-permute-start(bf16[1024,256]{1,0:T(8,128)(2,1)S(1)} %collective-permute-done.12.refs_3_), channel_id=1, source_target_pairs={{0,4},{1,5},{2,6},{3,7},{4,0},{5,1},{6,2},{7,3},{8,12},{9,13},{10,... | collective-permute-start | bytes 1572872 | tf_op jit(solution)/shard_map/ppermute | solution.py:37
  63.4 12.8 %collective-permute-start.20 = (bf16[1024,256]{1,0:T(8,128)(2,1)S(1)}, bf16[1024,256]{1,0:T(8,128)(2,1)S(1)}, u32[]{:S(2)}, u32[]{:S(2)}) collective-permute-start(bf16[1024,256]{1,0:T(8,128)(2,1)S(1)} %collective-permute-done.13.refs_0_), channel_id=1, source_target_pairs={{0,4},{1,5},{2,6},{3,7},{4,0},{5,1},{6,2},{7,3},{8,12},{9,13},{10,... | collective-permute-start | bytes 1572872 | tf_op jit(solution)/shard_map/ppermute | solution.py:37
  63.9 12.7 %collective-permute-start.22 = (bf16[1024,256]{1,0:T(8,128)(2,1)S(1)}, bf16[1024,256]{1,0:T(8,128)(2,1)S(1)}, u32[]{:S(2)}, u32[]{:S(2)}) collective-permute-start(bf16[1024,256]{1,0:T(8,128)(2,1)S(1)} %collective-permute-done.15.refs_2_), channel_id=1, source_target_pairs={{0,4},{1,5},{2,6},{3,7},{4,0},{5,1},{6,2},{7,3},{8,12},{9,13},{10,... | collective-permute-start | bytes 1572872 | tf_op jit(solution)/shard_map/ppermute | solution.py:37
  73.6 12.9 %collective-permute-start.21 = (bf16[1024,256]{1,0:T(8,128)(2,1)S(1)}, bf16[1024,256]{1,0:T(8,128)(2,1)S(1)}, u32[]{:S(2)}, u32[]{:S(2)}) collective-permute-start(bf16[1024,256]{1,0:T(8,128)(2,1)S(1)} %collective-permute-done.13.refs_0_), channel_id=1, source_target_pairs={{0,2},{1,0},{2,3},{3,1},{4,5},{5,7},{6,4},{7,6},{8,10},{9,8},{10,1... | collective-permute-start | bytes 1572872 | tf_op jit(solution)/shard_map/ppermute | solution.py:37
  76.2 12.3 %collective-permute-start.23 = (bf16[1024,256]{1,0:T(8,128)(2,1)S(1)}, bf16[1024,256]{1,0:T(8,128)(2,1)S(1)}, u32[]{:S(2)}, u32[]{:S(2)}) collective-permute-start(bf16[1024,256]{1,0:T(8,128)(2,1)S(1)} %collective-permute-done.18.refs_1_), channel_id=1, source_target_pairs={{0,2},{1,0},{2,3},{3,1},{4,5},{5,7},{6,4},{7,6},{8,10},{9,8},{10,1... | collective-permute-start | bytes 1572872 | tf_op jit(solution)/shard_map/ppermute | solution.py:37
  76.3 16.1 %collective-permute-start.25 = (bf16[1024,256]{1,0:T(8,128)(2,1)S(1)}, bf16[1024,256]{1,0:T(8,128)(2,1)S(1)}, u32[]{:S(2)}, u32[]{:S(2)}) collective-permute-start(bf16[1024,256]{1,0:T(8,128)(2,1)S(1)} %collective-permute-done.18.refs_1_), channel_id=1, source_target_pairs={{0,4},{1,5},{2,6},{3,7},{4,0},{5,1},{6,2},{7,3},{8,12},{9,13},{10,... | collective-permute-start | bytes 1572872 | tf_op jit(solution)/shard_map/ppermute | solution.py:37
  76.3 16.1 %collective-permute-start.24 = (bf16[1024,256]{1,0:T(8,128)(2,1)S(1)}, bf16[1024,256]{1,0:T(8,128)(2,1)S(1)}, u32[]{:S(2)}, u32[]{:S(2)}) collective-permute-start(bf16[1024,256]{1,0:T(8,128)(2,1)S(1)} %collective-permute-done.12.refs_3_), channel_id=1, source_target_pairs={{0,8},{1,9},{2,10},{3,11},{4,12},{5,13},{6,14},{7,15},{8,16},{9,17... | collective-permute-start | bytes 1572872 | tf_op jit(solution)/shard_map/ppermute | solution.py:37
  76.6 15.9 %collective-permute-start.26 = (bf16[1024,256]{1,0:T(8,128)(2,1)S(1)}, bf16[1024,256]{1,0:T(8,128)(2,1)S(1)}, u32[]{:S(2)}, u32[]{:S(2)}) collective-permute-start(bf16[1024,256]{1,0:T(8,128)(2,1)S(1)} %collective-permute-done.17.refs_3_), channel_id=1, source_target_pairs={{0,4},{1,5},{2,6},{3,7},{4,0},{5,1},{6,2},{7,3},{8,12},{9,13},{10,... | collective-permute-start | bytes 1572872 | tf_op jit(solution)/shard_map/ppermute | solution.py:37
  92.5 15.6 %collective-permute-start.32 = (f32[16,9216]{1,0:T(8,128)S(1)}, f32[16,9216]{1,0:T(8,128)S(1)}, u32[]{:S(2)}, u32[]{:S(2)}) collective-permute-start(f32[16,9216]{1,0:T(8,128)S(1)} %add.6), channel_id=1, source_target_pairs={{0,2},{1,3},{2,0},{3,1},{4,5},{5,4},{6,7},{7,6},{8,10},{9,11},{10,... | collective-permute-start | bytes 1769480 | tf_op jit(solution)/shard_map/ppermute | solution.py:37
  93.5 2.0 %collective-permute-start.29 = (bf16[1024,256]{1,0:T(8,128)(2,1)S(1)}, bf16[1024,256]{1,0:T(8,128)(2,1)S(1)}, u32[]{:S(2)}, u32[]{:S(2)}) collective-permute-start(bf16[1024,256]{1,0:T(8,128)(2,1)S(1)} %collective-permute-done.23.refs_2_), channel_id=1, source_target_pairs={{0,4},{1,5},{2,6},{3,7},{4,0},{5,1},{6,2},{7,3},{8,12},{9,13},{10,... | collective-permute-start | bytes 1572872 | tf_op jit(solution)/shard_map/ppermute | solution.py:37
  94.0 13.1 %collective-permute-start.27 = (bf16[1024,256]{1,0:T(8,128)(2,1)S(1)}, bf16[1024,256]{1,0:T(8,128)(2,1)S(1)}, u32[]{:S(2)}, u32[]{:S(2)}) collective-permute-start(bf16[1024,256]{1,0:T(8,128)(2,1)S(1)} %collective-permute-done.21.refs_1_), channel_id=1, source_target_pairs={{0,2},{1,0},{2,3},{3,1},{4,5},{5,7},{6,4},{7,6},{8,10},{9,8},{10,1... | collective-permute-start | bytes 1572872 | tf_op jit(solution)/shard_map/ppermute | solution.py:37
  94.6 12.4 %collective-permute-start.28 = (bf16[1024,256]{1,0:T(8,128)(2,1)S(1)}, bf16[1024,256]{1,0:T(8,128)(2,1)S(1)}, u32[]{:S(2)}, u32[]{:S(2)}) collective-permute-start(bf16[1024,256]{1,0:T(8,128)(2,1)S(1)} %collective-permute-done.21.refs_1_), channel_id=1, source_target_pairs={{0,4},{1,5},{2,6},{3,7},{4,0},{5,1},{6,2},{7,3},{8,12},{9,13},{10,... | collective-permute-start | bytes 1572872 | tf_op jit(solution)/shard_map/ppermute | solution.py:37
  94.8 12.2 %collective-permute-start.30 = (bf16[1024,256]{1,0:T(8,128)(2,1)S(1)}, bf16[1024,256]{1,0:T(8,128)(2,1)S(1)}, u32[]{:S(2)}, u32[]{:S(2)}) collective-permute-start(bf16[1024,256]{1,0:T(8,128)(2,1)S(1)} %collective-permute-done.24.refs_3_), channel_id=1, source_target_pairs={{0,4},{1,5},{2,6},{3,7},{4,0},{5,1},{6,2},{7,3},{8,12},{9,13},{10,... | collective-permute-start | bytes 1572872 | tf_op jit(solution)/shard_map/ppermute | solution.py:37
  107.0 2.5 %collective-permute-start.31 = (bf16[1024,256]{1,0:T(8,128)(2,1)S(1)}, bf16[1024,256]{1,0:T(8,128)(2,1)S(1)}, u32[]{:S(2)}, u32[]{:S(2)}) collective-permute-start(bf16[1024,256]{1,0:T(8,128)(2,1)S(1)} %collective-permute-done.27.refs_2_), channel_id=1, source_target_pairs={{0,4},{1,5},{2,6},{3,7},{4,0},{5,1},{6,2},{7,3},{8,12},{9,13},{10,... | collective-permute-start | bytes 1572872 | tf_op jit(solution)/shard_map/ppermute | solution.py:37
  (33 other events, 535.1 us)

commit v3 on v2

--- a/solution.py
+++ b/solution.py
@@ -139,7 +139,7 @@
         acc_in_ref, _, *refs = refs
     keys_ref, grad_ref, panel_ref, rows_a_ref, cot_ref, rows_down_ref, out_ref, *refs = refs
     if last:
-        acc_ref, *refs = refs
+        acc_ref, keys_out_ref, keys_sem, *refs = refs
     else:
         acc_ref = keys_ref
     panel_sem, a_sem, cot_sem, down_sem, out_sem = refs
@@ -190,15 +190,39 @@
             out_ref.at[k * chunks + r], grad_ref.at[:, to], out_sem.at[k, r]
         )
 
+    def keys_copy(j):
+        return pltpu.make_async_copy(
+            keys_out_ref.at[:, places[j]], keys_ref.at[:, columns[j]], keys_sem.at[j]
+        )
+
+    def fetch(k, r):
+        for j in range(count):
+            panel_copy(k, r, j).start()
+
+    def landed(k, rs=range(chunks)):
+        for r in rs:
+            for j in range(count):
+                panel_copy(k, r, j).wait()
+
+    def frozen_gradient(k, r):
+        span = slice(r * size, (r + 1) * size)
+        grad = dot(cot_ref[...], panel_ref[k, span, :], ((1,), (1,)))
+        grad += dot(low_b, rows_down_ref[k, :, span], ((1,), (0,)))
+        out_ref[k * chunks + r] = grad.astype(bf16)
+        out_copy(k, r).start()
+
+    def add_keys(k):
+        a_copy(k).wait()
+        base = acc_ref if first or k else acc_in_ref
+        acc_ref[...] = base[...] + dot(rows_a_ref[k], panel_ref[k], ((1,), (0,)))
+
     for j in range(count):
         cot_copy(j).start()
     for k in range(2):
         down_copy(k).start()
         for r in range(chunks):
-            for j in range(count):
-                panel_copy(k, r, j).start()
+            fetch(k, r)
         a_copy(k).start()
-
     low_b = low_b_ref[...] * jnp.asarray(adapter_scale, bf16)
     if first:
         low_f = low_f_ref[...] * jnp.asarray(adapter_scale, bf16)
@@ -208,20 +232,23 @@
         cot_copy(j).wait()
     for k in range(2):
         down_copy(k).wait()
-        for r in range(chunks):
-            for j in range(count):
-                panel_copy(k, r, j).wait()
-            span = slice(r * size, (r + 1) * size)
-            grad = dot(cot_ref[...], panel_ref[k, span, :], ((1,), (1,)))
-            grad += dot(low_b, rows_down_ref[k, :, span], ((1,), (0,)))
-            out_ref[k * chunks + r] = grad.astype(bf16)
-            out_copy(k, r).start()
-        a_copy(k).wait()
-        base = acc_ref if first or k else acc_in_ref
-        acc_ref[...] = base[...] + dot(rows_a_ref[k], panel_ref[k], ((1,), (0,)))
+    for r in range(chunks):
+        landed(0, [r])
+        frozen_gradient(0, r)
+    add_keys(0)
+    landed(1)
+    if last:
+        add_keys(1)
+        for j in range(count):
+            keys_out_ref[:, places[j]] = acc_ref[:, places[j]].astype(bf16)
+            keys_copy(j).start()
+    for r in range(chunks):
+        frozen_gradient(1, r)
     if last:
         for j in range(count):
-            keys_ref[:, columns[j]] = acc_ref[:, places[j]].astype(bf16)
+            keys_copy(j).wait()
+    else:
+        add_keys(1)
     for k in range(2):
         for r in range(chunks):
             out_copy(k, r).wait()
@@ -257,7 +284,12 @@
         pltpu.VMEM((2, rank, rows), bf16),
         pltpu.VMEM((2 * chunks, tokens, size), bf16),
     ]
-    scratch += [pltpu.VMEM((tokens, keys), f32)] if last else []
+    if last:
+        scratch += [
+            pltpu.VMEM((tokens, keys), f32),
+            pltpu.VMEM((tokens, keys), bf16),
+            pltpu.SemaphoreType.DMA((count,)),
+        ]
     scratch += [
         pltpu.SemaphoreType.DMA((2, chunks, count)),
         pltpu.SemaphoreType.DMA((2,)),
@@ -268,7 +300,7 @@
     return pl.pallas_call(
         functools.partial(slab_kernel, layout, shift, first, last),
         in_specs=in_specs,
-        out_specs=[whole, remote],
+        out_specs=[remote if last else whole, remote],
         scratch_shapes=scratch,
         out_shape=[
             keys_type((tokens, keys), bf16 if last else f32),
@@ -293,24 +325,23 @@
             ("sum",),
             ("turn", 1, 1),
             ("turn", 1, -1),
+            ("turn", 2, 1),
             ("turn", 1, 2),
-            ("turn", 2, 1),
+            ("turn", 2, 2),
             ("turn", 3, 1),
-            ("turn", 2, 2),
+            ("sum",),
             ("turn", 3, 2),
-            ("sum",),
         ]
         besides = {
             0: [("rise", 1, 0, 0), ("local",)],
             2: [("rise", 2, 0, 0)],
-            4: [("rise", 3, 0, 1)],
-            5: [("slab", 0)],
+            4: [("rise", 3, 0, 1), ("slab", 0)],
             6: [("rise", 2, -1, 0)],
             8: [("rise", 3, -1, 1), ("slab", 1)],
             10: [("slab", 2)],
         }
         stages = []
-        for at, exchange in enumerate(exchanges[:-1]):
+        for at, exchange in enumerate(exchanges):
             starts = exchanges[: 2] if at == 0 else exchanges[at + 1 : at + 2]
             starts = starts + besides.get(at, [])
             dones = [exchange]
@@ -354,6 +385,7 @@
         return ("mine", *name[1:3]) if name[0] in ("turn", "rise") else name
 
     def multiply(at):
+        swap_ready(at)
         for name in [name for name in flying if name[0] == "other" and name[1] == at]:
             here[name] = flying.pop(name)
         mine = [here[("mine", at, offset)] for offset in layout.offsets]
@@ -363,15 +395,18 @@
             state.get("acc"), state.get("grad"), at == 0, at == depth - 1,
         )
 
-    def swap_ready():
+    def swap_ready(only=None, most=2):
         names = []
         for side, at, offset in list(here):
             turned = next(o for o in layout.offsets if (o + offset) % count == 0)
             name = ("other", at, turned)
-            if side == "mine" and name not in swapped:
-                swapped.add(name)
-                flying[name] = layout.swap_cores(here[(side, at, offset)])
-                names.append(name)
+            if side != "mine" or name in swapped or only not in (None, at):
+                continue
+            if only is None and len(names) == most:
+                break
+            swapped.add(name)
+            flying[name] = layout.swap_cores(here[(side, at, offset)])
+            names.append(name)
         return names
 
     def start(name):
@@ -402,22 +437,17 @@
         here.update(new_here)
         state.update(new_state)
 
-    turning = []
     for starts, dones in stages_of(layout):
         for name in starts:
             if name[0] not in ("local", "slab"):
                 start(name)
-        late, turning = turning, swap_ready()
+        turning = swap_ready()
         for name in starts:
             if name[0] in ("local", "slab"):
                 start(name)
-        close([result_of(name) for name in dones] + late)
-    close([name for name in flying if name[0] != "sum"])
-    swap_ready()
+        close([result_of(name) for name in dones] + turning)
     multiply(depth - 1)
     sums = state["sum"]
-    if "sum" in [name[0] for name in flying]:
-        sums = sums + flying[("sum",)]
     state["down"], state["up"] = sums[:, :width] * scale, sums[:, width:] * scale
     return tuple(state[name][None] for name in ("acc", "grad", "down", "up"))
 

time: 121 us -> 110 us (0.909)
  waiting for transfers between devices: 46.4 us -> 35.5 us
    ppermute x33, waiting for transfers between devices: 46.4 us -> 35.5 us  [permute(): moved = lax.ppermute(value, axes, pairs)]
  transfers between devices with their start and end apart: 33 -> 33, of which waited for: 12 -> 10; matrix products, arithmetic and copies ran while one was open for 1% -> 2% of each run, Pallas kernels for 29% -> 31%
where the time goes in v3:
time: 110 us; the launch traced here: 109 us
  Pallas kernels  43.8 us (40%)
  waiting for transfers between devices  35.5 us (32%)
  starting transfers between devices  25.4 us (23%)
  other arithmetic  1.75 us (2%)
  local copies, waits for them, and re-layouts  1.68 us (2%)
  between operations  1.29 us (1%)
    pallas_call x4, Pallas kernels, slab(): pl.pallas_call(functools.partial(slab_kernel, layout, shift, first, last)...  36.7 us
    ppermute x33, waiting for transfers between devices, permute(): moved = lax.ppermute(value, axes, pairs)  35.5 us
    ppermute x33, starting transfers between devices, permute(): moved = lax.ppermute(value, axes, pairs)  25.4 us
    pallas_call x1, Pallas kernels, local_terms(): pl.pallas_call(functools.partial(local_kernel, steps), grid=(steps,), in_...  7.1 us
  transfers between devices with their start and end apart: 33, of which 10 were waited for; matrix products, arithmetic and copies ran while one was open for 2% of the time, Pallas kernels for 31%

profile of v3, /device:TPU:0, one launch (start us, length us, event | category | flops | bytes accessed | tf_op | source)
XLA Modules:
  0.0 109.4 jit_solution(12508055547886467494)
XLA Ops:
  0.6 3.0 %collective-permute-start.1 = (bf16[1024,256]{1,0:T(8,128)(2,1)}, bf16[1024,256]{1,0:T(8,128)(2,1)S(1)}, u32[]{:S(2)}, u32[]{:S(2)}) collective-permute-start(bf16[1024,256]{1,0:T(8,128)(2,1)} %refs_0_), channel_id=1, source_target_pairs={{0,2},{1,0},{2,3},{3,1},{4,5},{5,7},{6,4},{7,6},{8,10},{9,8},{10,1... | collective-permute-start | bytes 1572872 | tf_op jit(solution)/shard_map/ppermute | solution.py:37
  3.7 1.0 collective-permute-start
  4.7 1.6 %collective-permute-start.3 = (bf16[1024,256]{1,0:T(8,128)(2,1)}, bf16[1024,256]{1,0:T(8,128)(2,1)S(1)}, u32[]{:S(2)}, u32[]{:S(2)}) collective-permute-start(bf16[1024,256]{1,0:T(8,128)(2,1)} %refs_0_), channel_id=1, source_target_pairs={{0,8},{1,9},{2,10},{3,11},{4,12},{5,13},{6,14},{7,15},{8,16},{9,17... | collective-permute-start | bytes 1572872 | tf_op jit(solution)/shard_map/ppermute | solution.py:37
  6.3 7.1 %local_terms.1 = (bf16[512,16]{1,0:T(8,128)(2,1)S(1)}, bf16[512,16]{1,0:T(8,128)(2,1)S(1)}, f32[16,9216]{1,0:T(8,128)S(1)}) custom-call(bf16[512,8192]{1,0:T(8,128)(2,1)} %bitcast.10, bf16[512,1024]{1,0:T(8,128)(2,1)} %bitcast.16, bf16[16,8192]{1,0:T(8,128)(2,1)} %bitcast.21, bf16[16,1024]{1,0:T(8,128)(2,1)} %bitcast.26), custom_call_target="tpu_custom_call" | custom-call | flops 1 | bytes 1 | tf_op jit(solution)/shard_map/local_terms/pallas_call | solution.py:104
  13.4 1.9 %collective-permute-done.1.refs_1_ = bf16[1024,256]{1,0:T(8,128)(2,1)S(1)} collective-permute-done((bf16[1024,256]{1,0:T(8,128)(2,1)}, bf16[1024,256]{1,0:T(8,128)(2,1)S(1)}, u32[]{:S(2)}, u32[]{:S(2)}) %collective-permute-start.1) | collective-permute-done | bytes 524320 | tf_op jit(solution)/shard_map/ppermute | solution.py:37
  15.3 2.5 %collective-permute-start.5 = (bf16[1024,256]{1,0:T(8,128)(2,1)S(1)}, bf16[1024,256]{1,0:T(8,128)(2,1)S(1)}, u32[]{:S(2)}, u32[]{:S(2)}) collective-permute-start(bf16[1024,256]{1,0:T(8,128)(2,1)S(1)} %collective-permute-done.1.refs_1_), channel_id=1, source_target_pairs={{0,2},{1,0},{2,3},{3,1},{4,5},{5,7},{6,4},{7,6},{8,10},{9,8},{10,1... | collective-permute-start | bytes 1572872 | tf_op jit(solution)/shard_map/ppermute | solution.py:37
  17.8 3.5 %collective-permute-done.3.refs_0_ = bf16[1024,256]{1,0:T(8,128)(2,1)S(1)} collective-permute-done((bf16[1024,256]{1,0:T(8,128)(2,1)}, bf16[1024,256]{1,0:T(8,128)(2,1)S(1)}, u32[]{:S(2)}, u32[]{:S(2)}) %collective-permute-start.3) | collective-permute-done | bytes 524320 | tf_op jit(solution)/shard_map/ppermute | solution.py:37
  21.9 0.5 collective-permute-start.10
  22.4 2.2 %collective-permute-start.8 = (bf16[1024,256]{1,0:T(8,128)(2,1)S(1)}, bf16[1024,256]{1,0:T(8,128)(2,1)S(1)}, u32[]{:S(2)}, u32[]{:S(2)}) collective-permute-start(bf16[1024,256]{1,0:T(8,128)(2,1)S(1)} %copy-done), channel_id=1, source_target_pairs={{0,24},{1,25},{2,26},{3,27},{4,28},{5,29},{6,30},{7,31},{8,0},{9,1... | collective-permute-start | bytes 1572872 | tf_op jit(solution)/shard_map/ppermute | solution.py:37
  24.6 1.7 %collective-permute-done.5.refs_2_ = bf16[1024,256]{1,0:T(8,128)(2,1)S(1)} collective-permute-done((bf16[1024,256]{1,0:T(8,128)(2,1)S(1)}, bf16[1024,256]{1,0:T(8,128)(2,1)S(1)}, u32[]{:S(2)}, u32[]{:S(2)}) %collective-permute-start.5) | collective-permute-done | bytes 524320 | tf_op jit(solution)/shard_map/ppermute | solution.py:37
  26.5 2.5 %collective-permute-start.11 = (bf16[1024,256]{1,0:T(8,128)(2,1)S(1)}, bf16[1024,256]{1,0:T(8,128)(2,1)S(1)}, u32[]{:S(2)}, u32[]{:S(2)}) collective-permute-start(bf16[1024,256]{1,0:T(8,128)(2,1)S(1)} %collective-permute-done.3.refs_0_), channel_id=1, source_target_pairs={{0,2},{1,0},{2,3},{3,1},{4,5},{5,7},{6,4},{7,6},{8,10},{9,8},{10,1... | collective-permute-start | bytes 1572872 | tf_op jit(solution)/shard_map/ppermute | solution.py:37
  29.0 3.1 %collective-permute-done.10 = f32[16,9216]{1,0:T(8,128)S(1)} collective-permute-done((f32[16,9216]{1,0:T(8,128)S(1)}, f32[16,9216]{1,0:T(8,128)S(1)}, u32[]{:S(2)}, u32[]{:S(2)}) %collective-permute-start.10) | collective-permute-done | bytes 589856 | tf_op jit(solution)/shard_map/ppermute | solution.py:37
  32.2 3.8 %collective-permute-done.8.refs_0_ = bf16[1024,256]{1,0:T(8,128)(2,1)S(1)} collective-permute-done((bf16[1024,256]{1,0:T(8,128)(2,1)S(1)}, bf16[1024,256]{1,0:T(8,128)(2,1)S(1)}, u32[]{:S(2)}, u32[]{:S(2)}) %collective-permute-start.8) | collective-permute-done | bytes 524320 | tf_op jit(solution)/shard_map/ppermute | solution.py:37
  36.1 1.4 %collective-permute-start.13 = (bf16[1024,256]{1,0:T(8,128)(2,1)S(1)}, bf16[1024,256]{1,0:T(8,128)(2,1)S(1)}, u32[]{:S(2)}, u32[]{:S(2)}) collective-permute-start(bf16[1024,256]{1,0:T(8,128)(2,1)S(1)} %collective-permute-done.3.refs_0_), channel_id=1, source_target_pairs={{0,1},{1,3},{2,0},{3,2},{4,6},{5,4},{6,7},{7,5},{8,9},{9,11},{10,8... | collective-permute-start | bytes 1572872 | tf_op jit(solution)/shard_map/ppermute | solution.py:37
  38.1 9.4 %slab.4 = (f32[512,1024]{1,0:T(8,128)S(1)}, bf16[512,8192]{1,0:T(8,128)(2,1)}) custom-call(bf16[1024,256]{1,0:T(8,128)(2,1)} %refs_0_, bf16[1024,256]{1,0:T(8,128)(2,1)} %copy-done.2, bf16[1024,256]{1,0:T(8,128)(2,1)} %copy-done.5, bf16[1024,256]{1,0:T(8,128)(2,1)} %copy-done.1, bf16[1024,256]{1,0:T(8,128)(2,1)} %copy-done.3, bf16[1024,256]{1,0:T(8,128)(2,1)} %copy-done.6, ...), custom_call_target="tpu_custom_call" | custom-call | flops 1 | bytes 1 | tf_op jit(solution)/shard_map/slab/pallas_call | solution.py:300
  48.0 5.5 %collective-permute-done.14.refs_0_ = bf16[1024,256]{1,0:T(8,128)(2,1)S(1)} collective-permute-done((bf16[1024,256]{1,0:T(8,128)(2,1)S(1)}, bf16[1024,256]{1,0:T(8,128)(2,1)S(1)}, u32[]{:S(2)}, u32[]{:S(2)}) %collective-permute-start.14) | collective-permute-done | bytes 524320 | tf_op jit(solution)/shard_map/ppermute | solution.py:37
  54.1 1.0 collective-permute-start.19
  55.1 1.7 %collective-permute-start.20 = (bf16[1024,256]{1,0:T(8,128)(2,1)}, bf16[1024,256]{1,0:T(8,128)(2,1)S(1)}, u32[]{:S(2)}, u32[]{:S(2)}) collective-permute-start(bf16[1024,256]{1,0:T(8,128)(2,1)} %copy-done.1), channel_id=1, source_target_pairs={{0,24},{1,25},{2,26},{3,27},{4,28},{5,29},{6,30},{7,31},{8,0},{9,1... | collective-permute-start | bytes 1572872 | tf_op jit(solution)/shard_map/ppermute | solution.py:37
  57.0 6.3 %collective-permute-done.19.refs_2_ = bf16[1024,256]{1,0:T(8,128)(2,1)S(1)} collective-permute-done((bf16[1024,256]{1,0:T(8,128)(2,1)S(1)}, bf16[1024,256]{1,0:T(8,128)(2,1)S(1)}, u32[]{:S(2)}, u32[]{:S(2)}) %collective-permute-start.19) | collective-permute-done | bytes 524320 | tf_op jit(solution)/shard_map/ppermute | solution.py:37
  63.2 5.6 %collective-permute-done.20.refs_3_ = bf16[1024,256]{1,0:T(8,128)(2,1)S(1)} collective-permute-done((bf16[1024,256]{1,0:T(8,128)(2,1)}, bf16[1024,256]{1,0:T(8,128)(2,1)S(1)}, u32[]{:S(2)}, u32[]{:S(2)}) %collective-permute-start.20) | collective-permute-done | bytes 524320 | tf_op jit(solution)/shard_map/ppermute | solution.py:37
  68.9 1.2 %collective-permute-start.22 = (bf16[1024,256]{1,0:T(8,128)(2,1)S(1)}, bf16[1024,256]{1,0:T(8,128)(2,1)S(1)}, u32[]{:S(2)}, u32[]{:S(2)}) collective-permute-start(bf16[1024,256]{1,0:T(8,128)(2,1)S(1)} %collective-permute-done.16.refs_1_), channel_id=1, source_target_pairs={{0,2},{1,0},{2,3},{3,1},{4,5},{5,7},{6,4},{7,6},{8,10},{9,8},{10,1... | collective-permute-start | bytes 1572872 | tf_op jit(solution)/shard_map/ppermute | solution.py:37
  70.1 0.8 collective-permute-start.23
  71.2 0.8 copy-done.30
  72.0 8.9 %slab.5 = (f32[512,1024]{1,0:T(8,128)S(1)}, bf16[512,8192]{1,0:T(8,128)(2,1)}) custom-call(bf16[1024,256]{1,0:T(8,128)(2,1)} %copy-done.10, bf16[1024,256]{1,0:T(8,128)(2,1)} %copy-done.15, bf16[1024,256]{1,0:T(8,128)(2,1)} %copy-done.25, bf16[1024,256]{1,0:T(8,128)(2,1)} %copy-done.14, ...), custom_call_target="tpu_custom_call", output_to_operand_aliasing={{1}: (13, {}), {0}: (12, {})} | custom-call | flops 1 | bytes 1 | tf_op jit(solution)/shard_map/slab/pallas_call | solution.py:300
  81.1 1.6 %collective-permute-start.30 = (f32[16,9216]{1,0:T(8,128)S(1)}, f32[16,9216]{1,0:T(8,128)S(1)}, u32[]{:S(2)}, u32[]{:S(2)}) collective-permute-start(f32[16,9216]{1,0:T(8,128)S(1)} %add.6), channel_id=1, source_target_pairs={{0,2},{1,3},{2,0},{3,1},{4,5},{5,4},{6,7},{7,6},{8,10},{9,11},{10,... | collective-permute-start | bytes 1769480 | tf_op jit(solution)/shard_map/ppermute | solution.py:37
  82.7 3.8 %collective-permute-done.25.refs_3_ = bf16[1024,256]{1,0:T(8,128)(2,1)S(1)} collective-permute-done((bf16[1024,256]{1,0:T(8,128)(2,1)S(1)}, bf16[1024,256]{1,0:T(8,128)(2,1)S(1)}, u32[]{:S(2)}, u32[]{:S(2)}) %collective-permute-start.25) | collective-permute-done | bytes 524320 | tf_op jit(solution)/shard_map/ppermute | solution.py:37
  87.1 0.8 collective-permute-start.31
  87.9 8.9 %slab.6 = (f32[512,1024]{1,0:T(8,128)S(1)}, bf16[512,8192]{1,0:T(8,128)(2,1)}) custom-call(bf16[1024,256]{1,0:T(8,128)(2,1)} %copy-done.8, bf16[1024,256]{1,0:T(8,128)(2,1)} %copy-done.16, bf16[1024,256]{1,0:T(8,128)(2,1)} %copy-done.22, bf16[1024,256]{1,0:T(8,128)(2,1)} %copy-done.17, ...), custom_call_target="tpu_custom_call", output_to_operand_aliasing={{1}: (13, {}), {0}: (12, {})} | custom-call | flops 1 | bytes 1 | tf_op jit(solution)/shard_map/slab/pallas_call | solution.py:300
  97.0 1.0 multiply_bitcast_fusion
  98.0 0.6 multiply_bitcast_fusion.1
  98.9 0.8 copy-done.31
  99.7 9.5 %slab.7 = (bf16[512,1024]{1,0:T(8,128)(2,1)}, bf16[512,8192]{1,0:T(8,128)(2,1)}) custom-call(bf16[1024,256]{1,0:T(8,128)(2,1)} %copy-done.9, bf16[1024,256]{1,0:T(8,128)(2,1)} %copy-done.19, bf16[1024,256]{1,0:T(8,128)(2,1)} %copy-done.28, bf16[1024,256]{1,0:T(8,128)(2,1)} %copy-done.18, ...), custom_call_target="tpu_custom_call", output_to_operand_aliasing={{1}: (13, {})} | custom-call | flops 1 | bytes 1 | tf_op jit(solution)/shard_map/slab/pallas_call | solution.py:300
  (107 shorter events, 4.0 us)
Async XLA Ops:
  0.6 14.6 %collective-permute-start.1 = (bf16[1024,256]{1,0:T(8,128)(2,1)}, bf16[1024,256]{1,0:T(8,128)(2,1)S(1)}, u32[]{:S(2)}, u32[]{:S(2)}) collective-permute-start(bf16[1024,256]{1,0:T(8,128)(2,1)} %refs_0_), channel_id=1, source_target_pairs={{0,2},{1,0},{2,3},{3,1},{4,5},{5,7},{6,4},{7,6},{8,10},{9,8},{10,1... | collective-permute-start | bytes 1572872 | tf_op jit(solution)/shard_map/ppermute | solution.py:37
  3.7 11.6 %collective-permute-start.2 = (bf16[1024,256]{1,0:T(8,128)(2,1)}, bf16[1024,256]{1,0:T(8,128)(2,1)S(1)}, u32[]{:S(2)}, u32[]{:S(2)}) collective-permute-start(bf16[1024,256]{1,0:T(8,128)(2,1)} %refs_0_), channel_id=1, source_target_pairs={{0,4},{1,5},{2,6},{3,7},{4,0},{5,1},{6,2},{7,3},{8,12},{9,13},{10,... | collective-permute-start | bytes 1572872 | tf_op jit(solution)/shard_map/ppermute | solution.py:37
  3.7 14.2 %collective-permute-start = (bf16[1024,256]{1,0:T(8,128)(2,1)}, bf16[1024,256]{1,0:T(8,128)(2,1)S(1)}, u32[]{:S(2)}, u32[]{:S(2)}) collective-permute-start(bf16[1024,256]{1,0:T(8,128)(2,1)} %refs_0_), channel_id=1, source_target_pairs={{0,1},{1,3},{2,0},{3,2},{4,6},{5,4},{6,7},{7,5},{8,9},{9,11},{10,8... | collective-permute-start | bytes 1572872 | tf_op jit(solution)/shard_map/ppermute | solution.py:37
  4.7 16.6 %collective-permute-start.3 = (bf16[1024,256]{1,0:T(8,128)(2,1)}, bf16[1024,256]{1,0:T(8,128)(2,1)S(1)}, u32[]{:S(2)}, u32[]{:S(2)}) collective-permute-start(bf16[1024,256]{1,0:T(8,128)(2,1)} %refs_0_), channel_id=1, source_target_pairs={{0,8},{1,9},{2,10},{3,11},{4,12},{5,13},{6,14},{7,15},{8,16},{9,17... | collective-permute-start | bytes 1572872 | tf_op jit(solution)/shard_map/ppermute | solution.py:37
  15.3 6.1 %collective-permute-start.4 = (bf16[1024,256]{1,0:T(8,128)(2,1)S(1)}, bf16[1024,256]{1,0:T(8,128)(2,1)S(1)}, u32[]{:S(2)}, u32[]{:S(2)}) collective-permute-start(bf16[1024,256]{1,0:T(8,128)(2,1)S(1)} %collective-permute-done.1.refs_1_), channel_id=1, source_target_pairs={{0,4},{1,5},{2,6},{3,7},{4,0},{5,1},{6,2},{7,3},{8,12},{9,13},{10,... | collective-permute-start | bytes 1572872 | tf_op jit(solution)/shard_map/ppermute | solution.py:37
  15.3 11.1 %collective-permute-start.5 = (bf16[1024,256]{1,0:T(8,128)(2,1)S(1)}, bf16[1024,256]{1,0:T(8,128)(2,1)S(1)}, u32[]{:S(2)}, u32[]{:S(2)}) collective-permute-start(bf16[1024,256]{1,0:T(8,128)(2,1)S(1)} %collective-permute-done.1.refs_1_), channel_id=1, source_target_pairs={{0,2},{1,0},{2,3},{3,1},{4,5},{5,7},{6,4},{7,6},{8,10},{9,8},{10,1... | collective-permute-start | bytes 1572872 | tf_op jit(solution)/shard_map/ppermute | solution.py:37
  21.3 5.1 %collective-permute-start.6 = (bf16[1024,256]{1,0:T(8,128)(2,1)S(1)}, bf16[1024,256]{1,0:T(8,128)(2,1)S(1)}, u32[]{:S(2)}, u32[]{:S(2)}) collective-permute-start(bf16[1024,256]{1,0:T(8,128)(2,1)S(1)} %collective-permute-done.refs_3_), channel_id=1, source_target_pairs={{0,4},{1,5},{2,6},{3,7},{4,0},{5,1},{6,2},{7,3},{8,12},{9,13},{10,... | collective-permute-start | bytes 1572872 | tf_op jit(solution)/shard_map/ppermute | solution.py:37
  21.4 5.0 %collective-permute-start.7 = (bf16[1024,256]{1,0:T(8,128)(2,1)S(1)}, bf16[1024,256]{1,0:T(8,128)(2,1)S(1)}, u32[]{:S(2)}, u32[]{:S(2)}) collective-permute-start(bf16[1024,256]{1,0:T(8,128)(2,1)S(1)} %collective-permute-done.3.refs_0_), channel_id=1, source_target_pairs={{0,4},{1,5},{2,6},{3,7},{4,0},{5,1},{6,2},{7,3},{8,12},{9,13},{10,... | collective-permute-start | bytes 1572872 | tf_op jit(solution)/shard_map/ppermute | solution.py:37
  21.9 10.3 %collective-permute-start.10 = (f32[16,9216]{1,0:T(8,128)S(1)}, f32[16,9216]{1,0:T(8,128)S(1)}, u32[]{:S(2)}, u32[]{:S(2)}) collective-permute-start(f32[16,9216]{1,0:T(8,128)S(1)} %get-tuple-element.191), channel_id=1, source_target_pairs={{0,1},{1,0},{2,3},{3,2},{4,6},{5,7},{6,4},{7,5},{8,9},{9,8},{10,11... | collective-permute-start | bytes 1769480 | tf_op jit(solution)/shard_map/ppermute | solution.py:37
  22.4 13.6 %collective-permute-start.8 = (bf16[1024,256]{1,0:T(8,128)(2,1)S(1)}, bf16[1024,256]{1,0:T(8,128)(2,1)S(1)}, u32[]{:S(2)}, u32[]{:S(2)}) collective-permute-start(bf16[1024,256]{1,0:T(8,128)(2,1)S(1)} %copy-done), channel_id=1, source_target_pairs={{0,24},{1,25},{2,26},{3,27},{4,28},{5,29},{6,30},{7,31},{8,0},{9,1... | collective-permute-start | bytes 1572872 | tf_op jit(solution)/shard_map/ppermute | solution.py:37
  26.4 9.6 %collective-permute-start.9 = (bf16[1024,256]{1,0:T(8,128)(2,1)S(1)}, bf16[1024,256]{1,0:T(8,128)(2,1)S(1)}, u32[]{:S(2)}, u32[]{:S(2)}) collective-permute-start(bf16[1024,256]{1,0:T(8,128)(2,1)S(1)} %collective-permute-done.5.refs_2_), channel_id=1, source_target_pairs={{0,4},{1,5},{2,6},{3,7},{4,0},{5,1},{6,2},{7,3},{8,12},{9,13},{10,... | collective-permute-start | bytes 1572872 | tf_op jit(solution)/shard_map/ppermute | solution.py:37
  26.5 21.0 %collective-permute-start.11 = (bf16[1024,256]{1,0:T(8,128)(2,1)S(1)}, bf16[1024,256]{1,0:T(8,128)(2,1)S(1)}, u32[]{:S(2)}, u32[]{:S(2)}) collective-permute-start(bf16[1024,256]{1,0:T(8,128)(2,1)S(1)} %collective-permute-done.3.refs_0_), channel_id=1, source_target_pairs={{0,2},{1,0},{2,3},{3,1},{4,5},{5,7},{6,4},{7,6},{8,10},{9,8},{10,1... | collective-permute-start | bytes 1572872 | tf_op jit(solution)/shard_map/ppermute | solution.py:37
  36.0 11.5 %collective-permute-start.12 = (bf16[1024,256]{1,0:T(8,128)(2,1)S(1)}, bf16[1024,256]{1,0:T(8,128)(2,1)S(1)}, u32[]{:S(2)}, u32[]{:S(2)}) collective-permute-start(bf16[1024,256]{1,0:T(8,128)(2,1)S(1)} %collective-permute-done.8.refs_0_), channel_id=1, source_target_pairs={{0,4},{1,5},{2,6},{3,7},{4,0},{5,1},{6,2},{7,3},{8,12},{9,13},{10,... | collective-permute-start | bytes 1572872 | tf_op jit(solution)/shard_map/ppermute | solution.py:37
  36.1 11.9 %collective-permute-start.13 = (bf16[1024,256]{1,0:T(8,128)(2,1)S(1)}, bf16[1024,256]{1,0:T(8,128)(2,1)S(1)}, u32[]{:S(2)}, u32[]{:S(2)}) collective-permute-start(bf16[1024,256]{1,0:T(8,128)(2,1)S(1)} %collective-permute-done.3.refs_0_), channel_id=1, source_target_pairs={{0,1},{1,3},{2,0},{3,2},{4,6},{5,4},{6,7},{7,5},{8,9},{9,11},{10,8... | collective-permute-start | bytes 1572872 | tf_op jit(solution)/shard_map/ppermute | solution.py:37
  37.5 16.0 %collective-permute-start.14 = (bf16[1024,256]{1,0:T(8,128)(2,1)S(1)}, bf16[1024,256]{1,0:T(8,128)(2,1)S(1)}, u32[]{:S(2)}, u32[]{:S(2)}) collective-permute-start(bf16[1024,256]{1,0:T(8,128)(2,1)S(1)} %collective-permute-done.3.refs_0_), channel_id=1, source_target_pairs={{0,8},{1,9},{2,10},{3,11},{4,12},{5,13},{6,14},{7,15},{8,16},{9,17... | collective-permute-start | bytes 1572872 | tf_op jit(solution)/shard_map/ppermute | solution.py:37
  47.5 5.9 %collective-permute-start.15 = (bf16[1024,256]{1,0:T(8,128)(2,1)S(1)}, bf16[1024,256]{1,0:T(8,128)(2,1)S(1)}, u32[]{:S(2)}, u32[]{:S(2)}) collective-permute-start(bf16[1024,256]{1,0:T(8,128)(2,1)S(1)} %collective-permute-done.11.refs_1_), channel_id=1, source_target_pairs={{0,4},{1,5},{2,6},{3,7},{4,0},{5,1},{6,2},{7,3},{8,12},{9,13},{10,... | collective-permute-start | bytes 1572872 | tf_op jit(solution)/shard_map/ppermute | solution.py:37
  47.6 9.2 %collective-permute-start.16 = (bf16[1024,256]{1,0:T(8,128)(2,1)S(1)}, bf16[1024,256]{1,0:T(8,128)(2,1)S(1)}, u32[]{:S(2)}, u32[]{:S(2)}) collective-permute-start(bf16[1024,256]{1,0:T(8,128)(2,1)S(1)} %collective-permute-done.8.refs_0_), channel_id=1, source_target_pairs={{0,2},{1,0},{2,3},{3,1},{4,5},{5,7},{6,4},{7,6},{8,10},{9,8},{10,1... | collective-permute-start | bytes 1572872 | tf_op jit(solution)/shard_map/ppermute | solution.py:37
  53.5 3.4 %collective-permute-start.17 = (bf16[1024,256]{1,0:T(8,128)(2,1)S(1)}, bf16[1024,256]{1,0:T(8,128)(2,1)S(1)}, u32[]{:S(2)}, u32[]{:S(2)}) collective-permute-start(bf16[1024,256]{1,0:T(8,128)(2,1)S(1)} %collective-permute-done.13.refs_3_), channel_id=1, source_target_pairs={{0,4},{1,5},{2,6},{3,7},{4,0},{5,1},{6,2},{7,3},{8,12},{9,13},{10,... | collective-permute-start | bytes 1572872 | tf_op jit(solution)/shard_map/ppermute | solution.py:37
  53.6 3.3 %collective-permute-start.18 = (bf16[1024,256]{1,0:T(8,128)(2,1)S(1)}, bf16[1024,256]{1,0:T(8,128)(2,1)S(1)}, u32[]{:S(2)}, u32[]{:S(2)}) collective-permute-start(bf16[1024,256]{1,0:T(8,128)(2,1)S(1)} %collective-permute-done.14.refs_0_), channel_id=1, source_target_pairs={{0,4},{1,5},{2,6},{3,7},{4,0},{5,1},{6,2},{7,3},{8,12},{9,13},{10,... | collective-permute-start | bytes 1572872 | tf_op jit(solution)/shard_map/ppermute | solution.py:37
  54.1 9.2 %collective-permute-start.19 = (bf16[1024,256]{1,0:T(8,128)(2,1)S(1)}, bf16[1024,256]{1,0:T(8,128)(2,1)S(1)}, u32[]{:S(2)}, u32[]{:S(2)}) collective-permute-start(bf16[1024,256]{1,0:T(8,128)(2,1)S(1)} %collective-permute-done.11.refs_1_), channel_id=1, source_target_pairs={{0,2},{1,0},{2,3},{3,1},{4,5},{5,7},{6,4},{7,6},{8,10},{9,8},{10,1... | collective-permute-start | bytes 1572872 | tf_op jit(solution)/shard_map/ppermute | solution.py:37
  55.1 13.7 %collective-permute-start.20 = (bf16[1024,256]{1,0:T(8,128)(2,1)}, bf16[1024,256]{1,0:T(8,128)(2,1)S(1)}, u32[]{:S(2)}, u32[]{:S(2)}) collective-permute-start(bf16[1024,256]{1,0:T(8,128)(2,1)} %copy-done.1), channel_id=1, source_target_pairs={{0,24},{1,25},{2,26},{3,27},{4,28},{5,29},{6,30},{7,31},{8,0},{9,1... | collective-permute-start | bytes 1572872 | tf_op jit(solution)/shard_map/ppermute | solution.py:37
  56.9 11.9 %collective-permute-start.21 = (bf16[1024,256]{1,0:T(8,128)(2,1)S(1)}, bf16[1024,256]{1,0:T(8,128)(2,1)S(1)}, u32[]{:S(2)}, u32[]{:S(2)}) collective-permute-start(bf16[1024,256]{1,0:T(8,128)(2,1)S(1)} %collective-permute-done.16.refs_1_), channel_id=1, source_target_pairs={{0,4},{1,5},{2,6},{3,7},{4,0},{5,1},{6,2},{7,3},{8,12},{9,13},{10,... | collective-permute-start | bytes 1572872 | tf_op jit(solution)/shard_map/ppermute | solution.py:37
  68.8 2.3 %collective-permute-start.24 = (bf16[1024,256]{1,0:T(8,128)(2,1)S(1)}, bf16[1024,256]{1,0:T(8,128)(2,1)S(1)}, u32[]{:S(2)}, u32[]{:S(2)}) collective-permute-start(bf16[1024,256]{1,0:T(8,128)(2,1)S(1)} %collective-permute-done.19.refs_2_), channel_id=1, source_target_pairs={{0,4},{1,5},{2,6},{3,7},{4,0},{5,1},{6,2},{7,3},{8,12},{9,13},{10,... | collective-permute-start | bytes 1572872 | tf_op jit(solution)/shard_map/ppermute | solution.py:37
  68.9 12.0 %collective-permute-start.22 = (bf16[1024,256]{1,0:T(8,128)(2,1)S(1)}, bf16[1024,256]{1,0:T(8,128)(2,1)S(1)}, u32[]{:S(2)}, u32[]{:S(2)}) collective-permute-start(bf16[1024,256]{1,0:T(8,128)(2,1)S(1)} %collective-permute-done.16.refs_1_), channel_id=1, source_target_pairs={{0,2},{1,0},{2,3},{3,1},{4,5},{5,7},{6,4},{7,6},{8,10},{9,8},{10,1... | collective-permute-start | bytes 1572872 | tf_op jit(solution)/shard_map/ppermute | solution.py:37
  70.1 10.9 %collective-permute-start.23 = (bf16[1024,256]{1,0:T(8,128)(2,1)S(1)}, bf16[1024,256]{1,0:T(8,128)(2,1)S(1)}, u32[]{:S(2)}, u32[]{:S(2)}) collective-permute-start(bf16[1024,256]{1,0:T(8,128)(2,1)S(1)} %collective-permute-done.20.refs_3_), channel_id=1, source_target_pairs={{0,4},{1,5},{2,6},{3,7},{4,0},{5,1},{6,2},{7,3},{8,12},{9,13},{10,... | collective-permute-start | bytes 1572872 | tf_op jit(solution)/shard_map/ppermute | solution.py:37
  70.9 15.6 %collective-permute-start.25 = (bf16[1024,256]{1,0:T(8,128)(2,1)S(1)}, bf16[1024,256]{1,0:T(8,128)(2,1)S(1)}, u32[]{:S(2)}, u32[]{:S(2)}) collective-permute-start(bf16[1024,256]{1,0:T(8,128)(2,1)S(1)} %collective-permute-done.13.refs_3_), channel_id=1, source_target_pairs={{0,8},{1,9},{2,10},{3,11},{4,12},{5,13},{6,14},{7,15},{8,16},{9,17... | collective-permute-start | bytes 1572872 | tf_op jit(solution)/shard_map/ppermute | solution.py:37
  70.9 15.6 %collective-permute-start.26 = (bf16[1024,256]{1,0:T(8,128)(2,1)S(1)}, bf16[1024,256]{1,0:T(8,128)(2,1)S(1)}, u32[]{:S(2)}, u32[]{:S(2)}) collective-permute-start(bf16[1024,256]{1,0:T(8,128)(2,1)S(1)} %collective-permute-done.14.refs_0_), channel_id=1, source_target_pairs={{0,2},{1,0},{2,3},{3,1},{4,5},{5,7},{6,4},{7,6},{8,10},{9,8},{10,1... | collective-permute-start | bytes 1572872 | tf_op jit(solution)/shard_map/ppermute | solution.py:37
  80.9 5.6 %collective-permute-start.27 = (bf16[1024,256]{1,0:T(8,128)(2,1)S(1)}, bf16[1024,256]{1,0:T(8,128)(2,1)S(1)}, u32[]{:S(2)}, u32[]{:S(2)}) collective-permute-start(bf16[1024,256]{1,0:T(8,128)(2,1)S(1)} %collective-permute-done.22.refs_2_), channel_id=1, source_target_pairs={{0,4},{1,5},{2,6},{3,7},{4,0},{5,1},{6,2},{7,3},{8,12},{9,13},{10,... | collective-permute-start | bytes 1572872 | tf_op jit(solution)/shard_map/ppermute | solution.py:37
  81.1 15.7 %collective-permute-start.30 = (f32[16,9216]{1,0:T(8,128)S(1)}, f32[16,9216]{1,0:T(8,128)S(1)}, u32[]{:S(2)}, u32[]{:S(2)}) collective-permute-start(f32[16,9216]{1,0:T(8,128)S(1)} %add.6), channel_id=1, source_target_pairs={{0,2},{1,3},{2,0},{3,1},{4,5},{5,4},{6,7},{7,6},{8,10},{9,11},{10,... | collective-permute-start | bytes 1769480 | tf_op jit(solution)/shard_map/ppermute | solution.py:37
  86.5 10.3 %collective-permute-start.28 = (bf16[1024,256]{1,0:T(8,128)(2,1)S(1)}, bf16[1024,256]{1,0:T(8,128)(2,1)S(1)}, u32[]{:S(2)}, u32[]{:S(2)}) collective-permute-start(bf16[1024,256]{1,0:T(8,128)(2,1)S(1)} %collective-permute-done.26.refs_1_), channel_id=1, source_target_pairs={{0,4},{1,5},{2,6},{3,7},{4,0},{5,1},{6,2},{7,3},{8,12},{9,13},{10,... | collective-permute-start | bytes 1572872 | tf_op jit(solution)/shard_map/ppermute | solution.py:37
  86.6 10.3 %collective-permute-start.29 = (bf16[1024,256]{1,0:T(8,128)(2,1)S(1)}, bf16[1024,256]{1,0:T(8,128)(2,1)S(1)}, u32[]{:S(2)}, u32[]{:S(2)}) collective-permute-start(bf16[1024,256]{1,0:T(8,128)(2,1)S(1)} %collective-permute-done.25.refs_3_), channel_id=1, source_target_pairs={{0,4},{1,5},{2,6},{3,7},{4,0},{5,1},{6,2},{7,3},{8,12},{9,13},{10,... | collective-permute-start | bytes 1572872 | tf_op jit(solution)/shard_map/ppermute | solution.py:37
  87.1 9.8 %collective-permute-start.31 = (bf16[1024,256]{1,0:T(8,128)(2,1)S(1)}, bf16[1024,256]{1,0:T(8,128)(2,1)S(1)}, u32[]{:S(2)}, u32[]{:S(2)}) collective-permute-start(bf16[1024,256]{1,0:T(8,128)(2,1)S(1)} %collective-permute-done.26.refs_1_), channel_id=1, source_target_pairs={{0,2},{1,0},{2,3},{3,1},{4,5},{5,7},{6,4},{7,6},{8,10},{9,8},{10,1... | collective-permute-start | bytes 1572872 | tf_op jit(solution)/shard_map/ppermute | solution.py:37
  (33 other events, 540.8 us)

commit v4 on v3

--- a/solution.py
+++ b/solution.py
@@ -34,10 +34,7 @@
             for seq in range(self.seqs):
                 to_blk, to_seq = target(blk // 2, blk % 2, seq)
                 pairs.append((blk * self.seqs + seq, to_blk * self.seqs + to_seq))
-        moved = lax.ppermute(value, axes, pairs)
-        if value.dtype == bf16:
-            moved = pltpu.with_memory_space_constraint(moved, pltpu.HBM)
-        return moved
+        return lax.ppermute(value, axes, pairs)
 
     def along_depth(self, value, shift):
         return self.permute(
@@ -263,9 +260,8 @@
     size = rows // chunks
     whole = pl.BlockSpec(memory_space=pltpu.VMEM)
     remote = pl.BlockSpec(memory_space=pl.ANY)
-    held = [pltpu.with_memory_space_constraint(piece, pltpu.HBM) for piece in [*mine, *other]]
     in_specs = [remote] * (2 * count + 2) + [whole, remote]
-    operands = [*held, a, c, low_b, down]
+    operands = [*mine, *other, a, c, low_b, down]
     aliases = {}
     if first:
         in_specs += [whole, whole]
@@ -335,9 +331,11 @@
         besides = {
             0: [("rise", 1, 0, 0), ("local",)],
             2: [("rise", 2, 0, 0)],
-            4: [("rise", 3, 0, 1), ("slab", 0)],
+            4: [("rise", 3, 0, 1)],
+            5: [("slab", 0)],
             6: [("rise", 2, -1, 0)],
-            8: [("rise", 3, -1, 1), ("slab", 1)],
+            8: [("rise", 3, -1, 1)],
+            9: [("slab", 1)],
             10: [("slab", 2)],
         }
         stages = []

time: 110 us -> 104 us (0.945)
  Pallas kernels: 43.8 us -> 37.7 us
  local copies, waits for them, and re-layouts: 1.68 us -> 0.01 us
  waiting for transfers between devices: 35.5 us -> 37.1 us
  starting transfers between devices: 25.4 us -> 26.9 us
    pallas_call x4, Pallas kernels: 36.7 us -> 30.6 us  [slab(): pl.pallas_call(functools.partial(slab_kernel, layout, shift, first, last)...]
    unnamed x64 -> x2, local copies, waits for them, and re-layouts: 1.68 us -> 0.01 us
    ppermute x33, waiting for transfers between devices: 35.5 us -> 37.1 us  [permute(): return lax.ppermute(value, axes, pairs)]
    ppermute x33, starting transfers between devices: 25.4 us -> 26.9 us  [permute(): return lax.ppermute(value, axes, pairs)]
  transfers between devices with their start and end apart: 33 -> 33, of which waited for: 10 -> 14; matrix products, arithmetic and copies ran while one was open for 2% -> 2% of each run, Pallas kernels for 31% -> 29%
where the time goes in v4:
time: 104 us
  Pallas kernels  37.7 us (36%)
  waiting for transfers between devices  37.1 us (36%)
  starting transfers between devices  26.9 us (26%)
  other arithmetic  1.59 us (2%)
    ppermute x33, waiting for transfers between devices, permute(): return lax.ppermute(value, axes, pairs)  37.1 us
    pallas_call x4, Pallas kernels, slab(): pl.pallas_call(functools.partial(slab_kernel, layout, shift, first, last)...  30.6 us
    ppermute x33, starting transfers between devices, permute(): return lax.ppermute(value, axes, pairs)  26.9 us
    pallas_call x1, Pallas kernels, local_terms(): pl.pallas_call(functools.partial(local_kernel, steps), grid=(steps,), in_...  7.1 us
  transfers between devices with their start and end apart: 33, of which 14 were waited for; matrix products, arithmetic and copies ran while one was open for 2% of the time, Pallas kernels for 29%

profile of v4, /device:TPU:0, one launch (start us, length us, event | category | flops | bytes accessed | tf_op | source)
XLA Modules:
  0.0 104.2 jit_solution(6767524145243345799)
XLA Ops:
  0.6 3.0 %collective-permute-start.1 = (bf16[1024,256]{1,0:T(8,128)(2,1)}, bf16[1024,256]{1,0:T(8,128)(2,1)S(1)}, u32[]{:S(2)}, u32[]{:S(2)}) collective-permute-start(bf16[1024,256]{1,0:T(8,128)(2,1)} %refs_0_), channel_id=1, source_target_pairs={{0,2},{1,0},{2,3},{3,1},{4,5},{5,7},{6,4},{7,6},{8,10},{9,8},{10,1... | collective-permute-start | bytes 1572872 | tf_op jit(solution)/shard_map/ppermute | solution.py:37
  3.7 1.0 %collective-permute-start = (bf16[1024,256]{1,0:T(8,128)(2,1)}, bf16[1024,256]{1,0:T(8,128)(2,1)S(1)}, u32[]{:S(2)}, u32[]{:S(2)}) collective-permute-start(bf16[1024,256]{1,0:T(8,128)(2,1)} %refs_0_), channel_id=1, source_target_pairs={{0,1},{1,3},{2,0},{3,2},{4,6},{5,4},{6,7},{7,5},{8,9},{9,11},{10,8... | collective-permute-start | bytes 1572872 | tf_op jit(solution)/shard_map/ppermute | solution.py:37
  4.7 1.6 %collective-permute-start.3 = (bf16[1024,256]{1,0:T(8,128)(2,1)}, bf16[1024,256]{1,0:T(8,128)(2,1)S(1)}, u32[]{:S(2)}, u32[]{:S(2)}) collective-permute-start(bf16[1024,256]{1,0:T(8,128)(2,1)} %refs_0_), channel_id=1, source_target_pairs={{0,8},{1,9},{2,10},{3,11},{4,12},{5,13},{6,14},{7,15},{8,16},{9,17... | collective-permute-start | bytes 1572872 | tf_op jit(solution)/shard_map/ppermute | solution.py:37
  6.3 7.1 %local_terms.1 = (bf16[512,16]{1,0:T(8,128)(2,1)S(1)}, bf16[512,16]{1,0:T(8,128)(2,1)S(1)}, f32[16,9216]{1,0:T(8,128)S(1)}) custom-call(bf16[512,8192]{1,0:T(8,128)(2,1)} %bitcast.10, bf16[512,1024]{1,0:T(8,128)(2,1)} %bitcast.16, bf16[16,8192]{1,0:T(8,128)(2,1)} %bitcast.21, bf16[16,1024]{1,0:T(8,128)(2,1)} %bitcast.26), custom_call_target="tpu_custom_call" | custom-call | flops 1 | bytes 1 | tf_op jit(solution)/shard_map/local_terms/pallas_call | solution.py:101
  13.4 1.9 %collective-permute-done.1.refs_1_ = bf16[1024,256]{1,0:T(8,128)(2,1)S(1)} collective-permute-done((bf16[1024,256]{1,0:T(8,128)(2,1)}, bf16[1024,256]{1,0:T(8,128)(2,1)S(1)}, u32[]{:S(2)}, u32[]{:S(2)}) %collective-permute-start.1) | collective-permute-done | bytes 524320 | tf_op jit(solution)/shard_map/ppermute | solution.py:37
  15.3 2.5 %collective-permute-start.5 = (bf16[1024,256]{1,0:T(8,128)(2,1)S(1)}, bf16[1024,256]{1,0:T(8,128)(2,1)S(1)}, u32[]{:S(2)}, u32[]{:S(2)}) collective-permute-start(bf16[1024,256]{1,0:T(8,128)(2,1)S(1)} %collective-permute-done.1.refs_1_), channel_id=1, source_target_pairs={{0,2},{1,0},{2,3},{3,1},{4,5},{5,7},{6,4},{7,6},{8,10},{9,8},{10,1... | collective-permute-start | bytes 1572872 | tf_op jit(solution)/shard_map/ppermute | solution.py:37
  17.7 3.6 %collective-permute-done.3.refs_0_ = bf16[1024,256]{1,0:T(8,128)(2,1)S(1)} collective-permute-done((bf16[1024,256]{1,0:T(8,128)(2,1)}, bf16[1024,256]{1,0:T(8,128)(2,1)S(1)}, u32[]{:S(2)}, u32[]{:S(2)}) %collective-permute-start.3) | collective-permute-done | bytes 524320 | tf_op jit(solution)/shard_map/ppermute | solution.py:37
  22.4 2.2 %collective-permute-start.8 = (bf16[1024,256]{1,0:T(8,128)(2,1)S(1)}, bf16[1024,256]{1,0:T(8,128)(2,1)S(1)}, u32[]{:S(2)}, u32[]{:S(2)}) collective-permute-start(bf16[1024,256]{1,0:T(8,128)(2,1)S(1)} %copy-done), channel_id=1, source_target_pairs={{0,24},{1,25},{2,26},{3,27},{4,28},{5,29},{6,30},{7,31},{8,0},{9,1... | collective-permute-start | bytes 1572872 | tf_op jit(solution)/shard_map/ppermute | solution.py:37
  24.6 1.8 %collective-permute-done.5.refs_2_ = bf16[1024,256]{1,0:T(8,128)(2,1)S(1)} collective-permute-done((bf16[1024,256]{1,0:T(8,128)(2,1)S(1)}, bf16[1024,256]{1,0:T(8,128)(2,1)S(1)}, u32[]{:S(2)}, u32[]{:S(2)}) %collective-permute-start.5) | collective-permute-done | bytes 524320 | tf_op jit(solution)/shard_map/ppermute | solution.py:37
  26.4 2.5 %collective-permute-start.11 = (bf16[1024,256]{1,0:T(8,128)(2,1)S(1)}, bf16[1024,256]{1,0:T(8,128)(2,1)S(1)}, u32[]{:S(2)}, u32[]{:S(2)}) collective-permute-start(bf16[1024,256]{1,0:T(8,128)(2,1)S(1)} %collective-permute-done.3.refs_0_), channel_id=1, source_target_pairs={{0,2},{1,0},{2,3},{3,1},{4,5},{5,7},{6,4},{7,6},{8,10},{9,8},{10,1... | collective-permute-start | bytes 1572872 | tf_op jit(solution)/shard_map/ppermute | solution.py:37
  28.9 3.1 %collective-permute-done.10 = f32[16,9216]{1,0:T(8,128)S(1)} collective-permute-done((f32[16,9216]{1,0:T(8,128)S(1)}, f32[16,9216]{1,0:T(8,128)S(1)}, u32[]{:S(2)}, u32[]{:S(2)}) %collective-permute-start.10) | collective-permute-done | bytes 589856 | tf_op jit(solution)/shard_map/ppermute | solution.py:37
  32.1 3.8 %collective-permute-done.8.refs_0_ = bf16[1024,256]{1,0:T(8,128)(2,1)S(1)} collective-permute-done((bf16[1024,256]{1,0:T(8,128)(2,1)S(1)}, bf16[1024,256]{1,0:T(8,128)(2,1)S(1)}, u32[]{:S(2)}, u32[]{:S(2)}) %collective-permute-start.8) | collective-permute-done | bytes 524320 | tf_op jit(solution)/shard_map/ppermute | solution.py:37
  35.9 1.5 %collective-permute-start.13 = (bf16[1024,256]{1,0:T(8,128)(2,1)S(1)}, bf16[1024,256]{1,0:T(8,128)(2,1)S(1)}, u32[]{:S(2)}, u32[]{:S(2)}) collective-permute-start(bf16[1024,256]{1,0:T(8,128)(2,1)S(1)} %collective-permute-done.3.refs_0_), channel_id=1, source_target_pairs={{0,1},{1,3},{2,0},{3,2},{4,6},{5,4},{6,7},{7,5},{8,9},{9,11},{10,8... | collective-permute-start | bytes 1572872 | tf_op jit(solution)/shard_map/ppermute | solution.py:37
  37.9 1.5 %collective-permute-start.16 = (bf16[1024,256]{1,0:T(8,128)(2,1)S(1)}, bf16[1024,256]{1,0:T(8,128)(2,1)S(1)}, u32[]{:S(2)}, u32[]{:S(2)}) collective-permute-start(bf16[1024,256]{1,0:T(8,128)(2,1)S(1)} %collective-permute-done.8.refs_0_), channel_id=1, source_target_pairs={{0,2},{1,0},{2,3},{3,1},{4,5},{5,7},{6,4},{7,6},{8,10},{9,8},{10,1... | collective-permute-start | bytes 1572872 | tf_op jit(solution)/shard_map/ppermute | solution.py:37
  39.5 8.1 %slab.4 = (f32[512,1024]{1,0:T(8,128)S(1)}, bf16[512,8192]{1,0:T(8,128)(2,1)}) custom-call(bf16[1024,256]{1,0:T(8,128)(2,1)S(1)} %copy-done, bf16[1024,256]{1,0:T(8,128)(2,1)S(1)} %collective-permute-done.1.refs_1_, bf16[1024,256]{1,0:T(8,128)(2,1)S(1)} %collective-permute-done.5.refs_2_, bf16[1024,256]{1,0:T(8,128)(2,1)S(1)} %collective-permute-done.refs_3_, ...), custom_call_target="tpu_custom_call" | custom-call | flops 1 | bytes 1 | tf_op jit(solution)/shard_map/slab/pallas_call | solution.py:296
  47.6 1.5 %collective-permute-done.13.refs_3_ = bf16[1024,256]{1,0:T(8,128)(2,1)S(1)} collective-permute-done((bf16[1024,256]{1,0:T(8,128)(2,1)S(1)}, bf16[1024,256]{1,0:T(8,128)(2,1)S(1)}, u32[]{:S(2)}, u32[]{:S(2)}) %collective-permute-start.13) | collective-permute-done | bytes 524320 | tf_op jit(solution)/shard_map/ppermute | solution.py:37
  49.2 4.1 %collective-permute-done.14.refs_0_ = bf16[1024,256]{1,0:T(8,128)(2,1)S(1)} collective-permute-done((bf16[1024,256]{1,0:T(8,128)(2,1)S(1)}, bf16[1024,256]{1,0:T(8,128)(2,1)S(1)}, u32[]{:S(2)}, u32[]{:S(2)}) %collective-permute-start.14) | collective-permute-done | bytes 524320 | tf_op jit(solution)/shard_map/ppermute | solution.py:37
  53.8 1.1 %collective-permute-start.19 = (bf16[1024,256]{1,0:T(8,128)(2,1)S(1)}, bf16[1024,256]{1,0:T(8,128)(2,1)S(1)}, u32[]{:S(2)}, u32[]{:S(2)}) collective-permute-start(bf16[1024,256]{1,0:T(8,128)(2,1)S(1)} %collective-permute-done.11.refs_1_), channel_id=1, source_target_pairs={{0,2},{1,0},{2,3},{3,1},{4,5},{5,7},{6,4},{7,6},{8,10},{9,8},{10,1... | collective-permute-start | bytes 1572872 | tf_op jit(solution)/shard_map/ppermute | solution.py:37
  54.9 1.7 %collective-permute-start.20 = (bf16[1024,256]{1,0:T(8,128)(2,1)S(1)}, bf16[1024,256]{1,0:T(8,128)(2,1)S(1)}, u32[]{:S(2)}, u32[]{:S(2)}) collective-permute-start(bf16[1024,256]{1,0:T(8,128)(2,1)S(1)} %collective-permute-done.refs_3_), channel_id=1, source_target_pairs={{0,24},{1,25},{2,26},{3,27},{4,28},{5,29},{6,30},{7,31},{8,0},{9,1... | collective-permute-start | bytes 1572872 | tf_op jit(solution)/shard_map/ppermute | solution.py:37
  56.7 1.6 %collective-permute-start.22 = (bf16[1024,256]{1,0:T(8,128)(2,1)S(1)}, bf16[1024,256]{1,0:T(8,128)(2,1)S(1)}, u32[]{:S(2)}, u32[]{:S(2)}) collective-permute-start(bf16[1024,256]{1,0:T(8,128)(2,1)S(1)} %collective-permute-done.16.refs_1_), channel_id=1, source_target_pairs={{0,2},{1,0},{2,3},{3,1},{4,5},{5,7},{6,4},{7,6},{8,10},{9,8},{10,1... | collective-permute-start | bytes 1572872 | tf_op jit(solution)/shard_map/ppermute | solution.py:37
  58.4 4.6 %collective-permute-done.19.refs_2_ = bf16[1024,256]{1,0:T(8,128)(2,1)S(1)} collective-permute-done((bf16[1024,256]{1,0:T(8,128)(2,1)S(1)}, bf16[1024,256]{1,0:T(8,128)(2,1)S(1)}, u32[]{:S(2)}, u32[]{:S(2)}) %collective-permute-start.19) | collective-permute-done | bytes 524320 | tf_op jit(solution)/shard_map/ppermute | solution.py:37
  63.0 5.3 %collective-permute-done.20.refs_3_ = bf16[1024,256]{1,0:T(8,128)(2,1)S(1)} collective-permute-done((bf16[1024,256]{1,0:T(8,128)(2,1)S(1)}, bf16[1024,256]{1,0:T(8,128)(2,1)S(1)}, u32[]{:S(2)}, u32[]{:S(2)}) %collective-permute-start.20) | collective-permute-done | bytes 524320 | tf_op jit(solution)/shard_map/ppermute | solution.py:37
  68.8 1.1 %collective-permute-start.26 = (bf16[1024,256]{1,0:T(8,128)(2,1)S(1)}, bf16[1024,256]{1,0:T(8,128)(2,1)S(1)}, u32[]{:S(2)}, u32[]{:S(2)}) collective-permute-start(bf16[1024,256]{1,0:T(8,128)(2,1)S(1)} %collective-permute-done.14.refs_0_), channel_id=1, source_target_pairs={{0,2},{1,0},{2,3},{3,1},{4,5},{5,7},{6,4},{7,6},{8,10},{9,8},{10,1... | collective-permute-start | bytes 1572872 | tf_op jit(solution)/shard_map/ppermute | solution.py:37
  70.2 0.7 collective-permute-done.24.refs_5_
  71.1 1.1 %collective-permute-start.30 = (f32[16,9216]{1,0:T(8,128)S(1)}, f32[16,9216]{1,0:T(8,128)S(1)}, u32[]{:S(2)}, u32[]{:S(2)}) collective-permute-start(f32[16,9216]{1,0:T(8,128)S(1)} %add.6), channel_id=1, source_target_pairs={{0,2},{1,3},{2,0},{3,1},{4,5},{5,4},{6,7},{7,6},{8,10},{9,11},{10,... | collective-permute-start | bytes 1769480 | tf_op jit(solution)/shard_map/ppermute | solution.py:37
  72.2 7.3 %slab.5 = (f32[512,1024]{1,0:T(8,128)S(1)}, bf16[512,8192]{1,0:T(8,128)(2,1)}) custom-call(bf16[1024,256]{1,0:T(8,128)(2,1)S(1)} %collective-permute-done.3.refs_0_, bf16[1024,256]{1,0:T(8,128)(2,1)S(1)} %collective-permute-done.11.refs_1_, bf16[1024,256]{1,0:T(8,128)(2,1)S(1)} %collective-permute-done.19.refs_2_, ...), custom_call_target="tpu_custom_call", output_to_operand_aliasing={{1}: (13, {}), {0}: (12, {})} | custom-call | flops 1 | bytes 1 | tf_op jit(solution)/shard_map/slab/pallas_call | solution.py:296
  79.5 5.0 %collective-permute-done.25.refs_3_ = bf16[1024,256]{1,0:T(8,128)(2,1)S(1)} collective-permute-done((bf16[1024,256]{1,0:T(8,128)(2,1)S(1)}, bf16[1024,256]{1,0:T(8,128)(2,1)S(1)}, u32[]{:S(2)}, u32[]{:S(2)}) %collective-permute-start.25) | collective-permute-done | bytes 524320 | tf_op jit(solution)/shard_map/ppermute | solution.py:37
  85.0 1.1 %collective-permute-start.31 = (bf16[1024,256]{1,0:T(8,128)(2,1)S(1)}, bf16[1024,256]{1,0:T(8,128)(2,1)S(1)}, u32[]{:S(2)}, u32[]{:S(2)}) collective-permute-start(bf16[1024,256]{1,0:T(8,128)(2,1)S(1)} %collective-permute-done.26.refs_1_), channel_id=1, source_target_pairs={{0,2},{1,0},{2,3},{3,1},{4,5},{5,7},{6,4},{7,6},{8,10},{9,8},{10,1... | collective-permute-start | bytes 1572872 | tf_op jit(solution)/shard_map/ppermute | solution.py:37
  86.0 7.3 %slab.6 = (f32[512,1024]{1,0:T(8,128)S(1)}, bf16[512,8192]{1,0:T(8,128)(2,1)}) custom-call(bf16[1024,256]{1,0:T(8,128)(2,1)S(1)} %collective-permute-done.8.refs_0_, bf16[1024,256]{1,0:T(8,128)(2,1)S(1)} %collective-permute-done.16.refs_1_, bf16[1024,256]{1,0:T(8,128)(2,1)S(1)} %collective-permute-done.22.refs_2_, ...), custom_call_target="tpu_custom_call", output_to_operand_aliasing={{1}: (13, {}), {0}: (12, {})} | custom-call | flops 1 | bytes 1 | tf_op jit(solution)/shard_map/slab/pallas_call | solution.py:296
  93.4 0.7 collective-permute-done.31.refs_2_
  94.2 0.8 multiply_bitcast_fusion
  96.1 7.9 %slab.7 = (bf16[512,1024]{1,0:T(8,128)(2,1)}, bf16[512,8192]{1,0:T(8,128)(2,1)}) custom-call(bf16[1024,256]{1,0:T(8,128)(2,1)S(1)} %collective-permute-done.14.refs_0_, bf16[1024,256]{1,0:T(8,128)(2,1)S(1)} %collective-permute-done.26.refs_1_, bf16[1024,256]{1,0:T(8,128)(2,1)S(1)} %collective-permute-done.31.refs_2_, ...), custom_call_target="tpu_custom_call", output_to_operand_aliasing={{1}: (13, {})} | custom-call | flops 1 | bytes 1 | tf_op jit(solution)/shard_map/slab/pallas_call | solution.py:296
  (45 shorter events, 5.0 us)
Async XLA Ops:
  0.6 14.6 %collective-permute-start.1 = (bf16[1024,256]{1,0:T(8,128)(2,1)}, bf16[1024,256]{1,0:T(8,128)(2,1)S(1)}, u32[]{:S(2)}, u32[]{:S(2)}) collective-permute-start(bf16[1024,256]{1,0:T(8,128)(2,1)} %refs_0_), channel_id=1, source_target_pairs={{0,2},{1,0},{2,3},{3,1},{4,5},{5,7},{6,4},{7,6},{8,10},{9,8},{10,1... | collective-permute-start | bytes 1572872 | tf_op jit(solution)/shard_map/ppermute | solution.py:37
  3.7 11.6 %collective-permute-start.2 = (bf16[1024,256]{1,0:T(8,128)(2,1)}, bf16[1024,256]{1,0:T(8,128)(2,1)S(1)}, u32[]{:S(2)}, u32[]{:S(2)}) collective-permute-start(bf16[1024,256]{1,0:T(8,128)(2,1)} %refs_0_), channel_id=1, source_target_pairs={{0,4},{1,5},{2,6},{3,7},{4,0},{5,1},{6,2},{7,3},{8,12},{9,13},{10,... | collective-permute-start | bytes 1572872 | tf_op jit(solution)/shard_map/ppermute | solution.py:37
  3.7 14.1 %collective-permute-start = (bf16[1024,256]{1,0:T(8,128)(2,1)}, bf16[1024,256]{1,0:T(8,128)(2,1)S(1)}, u32[]{:S(2)}, u32[]{:S(2)}) collective-permute-start(bf16[1024,256]{1,0:T(8,128)(2,1)} %refs_0_), channel_id=1, source_target_pairs={{0,1},{1,3},{2,0},{3,2},{4,6},{5,4},{6,7},{7,5},{8,9},{9,11},{10,8... | collective-permute-start | bytes 1572872 | tf_op jit(solution)/shard_map/ppermute | solution.py:37
  4.7 16.6 %collective-permute-start.3 = (bf16[1024,256]{1,0:T(8,128)(2,1)}, bf16[1024,256]{1,0:T(8,128)(2,1)S(1)}, u32[]{:S(2)}, u32[]{:S(2)}) collective-permute-start(bf16[1024,256]{1,0:T(8,128)(2,1)} %refs_0_), channel_id=1, source_target_pairs={{0,8},{1,9},{2,10},{3,11},{4,12},{5,13},{6,14},{7,15},{8,16},{9,17... | collective-permute-start | bytes 1572872 | tf_op jit(solution)/shard_map/ppermute | solution.py:37
  15.3 6.1 %collective-permute-start.4 = (bf16[1024,256]{1,0:T(8,128)(2,1)S(1)}, bf16[1024,256]{1,0:T(8,128)(2,1)S(1)}, u32[]{:S(2)}, u32[]{:S(2)}) collective-permute-start(bf16[1024,256]{1,0:T(8,128)(2,1)S(1)} %collective-permute-done.1.refs_1_), channel_id=1, source_target_pairs={{0,4},{1,5},{2,6},{3,7},{4,0},{5,1},{6,2},{7,3},{8,12},{9,13},{10,... | collective-permute-start | bytes 1572872 | tf_op jit(solution)/shard_map/ppermute | solution.py:37
  15.3 11.1 %collective-permute-start.5 = (bf16[1024,256]{1,0:T(8,128)(2,1)S(1)}, bf16[1024,256]{1,0:T(8,128)(2,1)S(1)}, u32[]{:S(2)}, u32[]{:S(2)}) collective-permute-start(bf16[1024,256]{1,0:T(8,128)(2,1)S(1)} %collective-permute-done.1.refs_1_), channel_id=1, source_target_pairs={{0,2},{1,0},{2,3},{3,1},{4,5},{5,7},{6,4},{7,6},{8,10},{9,8},{10,1... | collective-permute-start | bytes 1572872 | tf_op jit(solution)/shard_map/ppermute | solution.py:37
  21.3 5.1 %collective-permute-start.6 = (bf16[1024,256]{1,0:T(8,128)(2,1)S(1)}, bf16[1024,256]{1,0:T(8,128)(2,1)S(1)}, u32[]{:S(2)}, u32[]{:S(2)}) collective-permute-start(bf16[1024,256]{1,0:T(8,128)(2,1)S(1)} %collective-permute-done.refs_3_), channel_id=1, source_target_pairs={{0,4},{1,5},{2,6},{3,7},{4,0},{5,1},{6,2},{7,3},{8,12},{9,13},{10,... | collective-permute-start | bytes 1572872 | tf_op jit(solution)/shard_map/ppermute | solution.py:37
  21.3 5.1 %collective-permute-start.7 = (bf16[1024,256]{1,0:T(8,128)(2,1)S(1)}, bf16[1024,256]{1,0:T(8,128)(2,1)S(1)}, u32[]{:S(2)}, u32[]{:S(2)}) collective-permute-start(bf16[1024,256]{1,0:T(8,128)(2,1)S(1)} %collective-permute-done.3.refs_0_), channel_id=1, source_target_pairs={{0,4},{1,5},{2,6},{3,7},{4,0},{5,1},{6,2},{7,3},{8,12},{9,13},{10,... | collective-permute-start | bytes 1572872 | tf_op jit(solution)/shard_map/ppermute | solution.py:37
  21.8 10.2 %collective-permute-start.10 = (f32[16,9216]{1,0:T(8,128)S(1)}, f32[16,9216]{1,0:T(8,128)S(1)}, u32[]{:S(2)}, u32[]{:S(2)}) collective-permute-start(f32[16,9216]{1,0:T(8,128)S(1)} %get-tuple-element.205), channel_id=1, source_target_pairs={{0,1},{1,0},{2,3},{3,2},{4,6},{5,7},{6,4},{7,5},{8,9},{9,8},{10,11... | collective-permute-start | bytes 1769480 | tf_op jit(solution)/shard_map/ppermute | solution.py:37
  22.4 13.5 %collective-permute-start.8 = (bf16[1024,256]{1,0:T(8,128)(2,1)S(1)}, bf16[1024,256]{1,0:T(8,128)(2,1)S(1)}, u32[]{:S(2)}, u32[]{:S(2)}) collective-permute-start(bf16[1024,256]{1,0:T(8,128)(2,1)S(1)} %copy-done), channel_id=1, source_target_pairs={{0,24},{1,25},{2,26},{3,27},{4,28},{5,29},{6,30},{7,31},{8,0},{9,1... | collective-permute-start | bytes 1572872 | tf_op jit(solution)/shard_map/ppermute | solution.py:37
  26.4 9.5 %collective-permute-start.9 = (bf16[1024,256]{1,0:T(8,128)(2,1)S(1)}, bf16[1024,256]{1,0:T(8,128)(2,1)S(1)}, u32[]{:S(2)}, u32[]{:S(2)}) collective-permute-start(bf16[1024,256]{1,0:T(8,128)(2,1)S(1)} %collective-permute-done.5.refs_2_), channel_id=1, source_target_pairs={{0,4},{1,5},{2,6},{3,7},{4,0},{5,1},{6,2},{7,3},{8,12},{9,13},{10,... | collective-permute-start | bytes 1572872 | tf_op jit(solution)/shard_map/ppermute | solution.py:37
  26.4 11.4 %collective-permute-start.11 = (bf16[1024,256]{1,0:T(8,128)(2,1)S(1)}, bf16[1024,256]{1,0:T(8,128)(2,1)S(1)}, u32[]{:S(2)}, u32[]{:S(2)}) collective-permute-start(bf16[1024,256]{1,0:T(8,128)(2,1)S(1)} %collective-permute-done.3.refs_0_), channel_id=1, source_target_pairs={{0,2},{1,0},{2,3},{3,1},{4,5},{5,7},{6,4},{7,6},{8,10},{9,8},{10,1... | collective-permute-start | bytes 1572872 | tf_op jit(solution)/shard_map/ppermute | solution.py:37
  35.9 1.9 %collective-permute-start.12 = (bf16[1024,256]{1,0:T(8,128)(2,1)S(1)}, bf16[1024,256]{1,0:T(8,128)(2,1)S(1)}, u32[]{:S(2)}, u32[]{:S(2)}) collective-permute-start(bf16[1024,256]{1,0:T(8,128)(2,1)S(1)} %collective-permute-done.8.refs_0_), channel_id=1, source_target_pairs={{0,4},{1,5},{2,6},{3,7},{4,0},{5,1},{6,2},{7,3},{8,12},{9,13},{10,... | collective-permute-start | bytes 1572872 | tf_op jit(solution)/shard_map/ppermute | solution.py:37
  35.9 13.3 %collective-permute-start.13 = (bf16[1024,256]{1,0:T(8,128)(2,1)S(1)}, bf16[1024,256]{1,0:T(8,128)(2,1)S(1)}, u32[]{:S(2)}, u32[]{:S(2)}) collective-permute-start(bf16[1024,256]{1,0:T(8,128)(2,1)S(1)} %collective-permute-done.3.refs_0_), channel_id=1, source_target_pairs={{0,1},{1,3},{2,0},{3,2},{4,6},{5,4},{6,7},{7,5},{8,9},{9,11},{10,8... | collective-permute-start | bytes 1572872 | tf_op jit(solution)/shard_map/ppermute | solution.py:37
  37.4 15.9 %collective-permute-start.14 = (bf16[1024,256]{1,0:T(8,128)(2,1)S(1)}, bf16[1024,256]{1,0:T(8,128)(2,1)S(1)}, u32[]{:S(2)}, u32[]{:S(2)}) collective-permute-start(bf16[1024,256]{1,0:T(8,128)(2,1)S(1)} %collective-permute-done.3.refs_0_), channel_id=1, source_target_pairs={{0,8},{1,9},{2,10},{3,11},{4,12},{5,13},{6,14},{7,15},{8,16},{9,17... | collective-permute-start | bytes 1572872 | tf_op jit(solution)/shard_map/ppermute | solution.py:37
  37.8 15.4 %collective-permute-start.15 = (bf16[1024,256]{1,0:T(8,128)(2,1)S(1)}, bf16[1024,256]{1,0:T(8,128)(2,1)S(1)}, u32[]{:S(2)}, u32[]{:S(2)}) collective-permute-start(bf16[1024,256]{1,0:T(8,128)(2,1)S(1)} %collective-permute-done.11.refs_1_), channel_id=1, source_target_pairs={{0,4},{1,5},{2,6},{3,7},{4,0},{5,1},{6,2},{7,3},{8,12},{9,13},{10,... | collective-permute-start | bytes 1572872 | tf_op jit(solution)/shard_map/ppermute | solution.py:37
  37.9 18.7 %collective-permute-start.16 = (bf16[1024,256]{1,0:T(8,128)(2,1)S(1)}, bf16[1024,256]{1,0:T(8,128)(2,1)S(1)}, u32[]{:S(2)}, u32[]{:S(2)}) collective-permute-start(bf16[1024,256]{1,0:T(8,128)(2,1)S(1)} %collective-permute-done.8.refs_0_), channel_id=1, source_target_pairs={{0,2},{1,0},{2,3},{3,1},{4,5},{5,7},{6,4},{7,6},{8,10},{9,8},{10,1... | collective-permute-start | bytes 1572872 | tf_op jit(solution)/shard_map/ppermute | solution.py:37
  53.3 3.4 %collective-permute-start.17 = (bf16[1024,256]{1,0:T(8,128)(2,1)S(1)}, bf16[1024,256]{1,0:T(8,128)(2,1)S(1)}, u32[]{:S(2)}, u32[]{:S(2)}) collective-permute-start(bf16[1024,256]{1,0:T(8,128)(2,1)S(1)} %collective-permute-done.13.refs_3_), channel_id=1, source_target_pairs={{0,4},{1,5},{2,6},{3,7},{4,0},{5,1},{6,2},{7,3},{8,12},{9,13},{10,... | collective-permute-start | bytes 1572872 | tf_op jit(solution)/shard_map/ppermute | solution.py:37
  53.3 3.4 %collective-permute-start.18 = (bf16[1024,256]{1,0:T(8,128)(2,1)S(1)}, bf16[1024,256]{1,0:T(8,128)(2,1)S(1)}, u32[]{:S(2)}, u32[]{:S(2)}) collective-permute-start(bf16[1024,256]{1,0:T(8,128)(2,1)S(1)} %collective-permute-done.14.refs_0_), channel_id=1, source_target_pairs={{0,4},{1,5},{2,6},{3,7},{4,0},{5,1},{6,2},{7,3},{8,12},{9,13},{10,... | collective-permute-start | bytes 1572872 | tf_op jit(solution)/shard_map/ppermute | solution.py:37
  53.8 9.2 %collective-permute-start.19 = (bf16[1024,256]{1,0:T(8,128)(2,1)S(1)}, bf16[1024,256]{1,0:T(8,128)(2,1)S(1)}, u32[]{:S(2)}, u32[]{:S(2)}) collective-permute-start(bf16[1024,256]{1,0:T(8,128)(2,1)S(1)} %collective-permute-done.11.refs_1_), channel_id=1, source_target_pairs={{0,2},{1,0},{2,3},{3,1},{4,5},{5,7},{6,4},{7,6},{8,10},{9,8},{10,1... | collective-permute-start | bytes 1572872 | tf_op jit(solution)/shard_map/ppermute | solution.py:37
  54.9 13.4 %collective-permute-start.20 = (bf16[1024,256]{1,0:T(8,128)(2,1)S(1)}, bf16[1024,256]{1,0:T(8,128)(2,1)S(1)}, u32[]{:S(2)}, u32[]{:S(2)}) collective-permute-start(bf16[1024,256]{1,0:T(8,128)(2,1)S(1)} %collective-permute-done.refs_3_), channel_id=1, source_target_pairs={{0,24},{1,25},{2,26},{3,27},{4,28},{5,29},{6,30},{7,31},{8,0},{9,1... | collective-permute-start | bytes 1572872 | tf_op jit(solution)/shard_map/ppermute | solution.py:37
  56.7 11.7 %collective-permute-start.21 = (bf16[1024,256]{1,0:T(8,128)(2,1)S(1)}, bf16[1024,256]{1,0:T(8,128)(2,1)S(1)}, u32[]{:S(2)}, u32[]{:S(2)}) collective-permute-start(bf16[1024,256]{1,0:T(8,128)(2,1)S(1)} %collective-permute-done.16.refs_1_), channel_id=1, source_target_pairs={{0,4},{1,5},{2,6},{3,7},{4,0},{5,1},{6,2},{7,3},{8,12},{9,13},{10,... | collective-permute-start | bytes 1572872 | tf_op jit(solution)/shard_map/ppermute | solution.py:37
  56.7 13.1 %collective-permute-start.22 = (bf16[1024,256]{1,0:T(8,128)(2,1)S(1)}, bf16[1024,256]{1,0:T(8,128)(2,1)S(1)}, u32[]{:S(2)}, u32[]{:S(2)}) collective-permute-start(bf16[1024,256]{1,0:T(8,128)(2,1)S(1)} %collective-permute-done.16.refs_1_), channel_id=1, source_target_pairs={{0,2},{1,0},{2,3},{3,1},{4,5},{5,7},{6,4},{7,6},{8,10},{9,8},{10,1... | collective-permute-start | bytes 1572872 | tf_op jit(solution)/shard_map/ppermute | solution.py:37
  68.3 1.9 %collective-permute-start.23 = (bf16[1024,256]{1,0:T(8,128)(2,1)S(1)}, bf16[1024,256]{1,0:T(8,128)(2,1)S(1)}, u32[]{:S(2)}, u32[]{:S(2)}) collective-permute-start(bf16[1024,256]{1,0:T(8,128)(2,1)S(1)} %collective-permute-done.19.refs_2_), channel_id=1, source_target_pairs={{0,4},{1,5},{2,6},{3,7},{4,0},{5,1},{6,2},{7,3},{8,12},{9,13},{10,... | collective-permute-start | bytes 1572872 | tf_op jit(solution)/shard_map/ppermute | solution.py:37
  68.3 2.7 %collective-permute-start.24 = (bf16[1024,256]{1,0:T(8,128)(2,1)S(1)}, bf16[1024,256]{1,0:T(8,128)(2,1)S(1)}, u32[]{:S(2)}, u32[]{:S(2)}) collective-permute-start(bf16[1024,256]{1,0:T(8,128)(2,1)S(1)} %collective-permute-done.20.refs_3_), channel_id=1, source_target_pairs={{0,4},{1,5},{2,6},{3,7},{4,0},{5,1},{6,2},{7,3},{8,12},{9,13},{10,... | collective-permute-start | bytes 1572872 | tf_op jit(solution)/shard_map/ppermute | solution.py:37
  68.8 15.6 %collective-permute-start.25 = (bf16[1024,256]{1,0:T(8,128)(2,1)S(1)}, bf16[1024,256]{1,0:T(8,128)(2,1)S(1)}, u32[]{:S(2)}, u32[]{:S(2)}) collective-permute-start(bf16[1024,256]{1,0:T(8,128)(2,1)S(1)} %collective-permute-done.13.refs_3_), channel_id=1, source_target_pairs={{0,8},{1,9},{2,10},{3,11},{4,12},{5,13},{6,14},{7,15},{8,16},{9,17... | collective-permute-start | bytes 1572872 | tf_op jit(solution)/shard_map/ppermute | solution.py:37
  68.8 15.6 %collective-permute-start.26 = (bf16[1024,256]{1,0:T(8,128)(2,1)S(1)}, bf16[1024,256]{1,0:T(8,128)(2,1)S(1)}, u32[]{:S(2)}, u32[]{:S(2)}) collective-permute-start(bf16[1024,256]{1,0:T(8,128)(2,1)S(1)} %collective-permute-done.14.refs_0_), channel_id=1, source_target_pairs={{0,2},{1,0},{2,3},{3,1},{4,5},{5,7},{6,4},{7,6},{8,10},{9,8},{10,1... | collective-permute-start | bytes 1572872 | tf_op jit(solution)/shard_map/ppermute | solution.py:37
  71.0 13.5 %collective-permute-start.27 = (bf16[1024,256]{1,0:T(8,128)(2,1)S(1)}, bf16[1024,256]{1,0:T(8,128)(2,1)S(1)}, u32[]{:S(2)}, u32[]{:S(2)}) collective-permute-start(bf16[1024,256]{1,0:T(8,128)(2,1)S(1)} %collective-permute-done.22.refs_2_), channel_id=1, source_target_pairs={{0,4},{1,5},{2,6},{3,7},{4,0},{5,1},{6,2},{7,3},{8,12},{9,13},{10,... | collective-permute-start | bytes 1572872 | tf_op jit(solution)/shard_map/ppermute | solution.py:37
  71.1 22.2 %collective-permute-start.30 = (f32[16,9216]{1,0:T(8,128)S(1)}, f32[16,9216]{1,0:T(8,128)S(1)}, u32[]{:S(2)}, u32[]{:S(2)}) collective-permute-start(f32[16,9216]{1,0:T(8,128)S(1)} %add.6), channel_id=1, source_target_pairs={{0,2},{1,3},{2,0},{3,1},{4,5},{5,4},{6,7},{7,6},{8,10},{9,11},{10,... | collective-permute-start | bytes 1769480 | tf_op jit(solution)/shard_map/ppermute | solution.py:37
  84.5 8.9 %collective-permute-start.28 = (bf16[1024,256]{1,0:T(8,128)(2,1)S(1)}, bf16[1024,256]{1,0:T(8,128)(2,1)S(1)}, u32[]{:S(2)}, u32[]{:S(2)}) collective-permute-start(bf16[1024,256]{1,0:T(8,128)(2,1)S(1)} %collective-permute-done.26.refs_1_), channel_id=1, source_target_pairs={{0,4},{1,5},{2,6},{3,7},{4,0},{5,1},{6,2},{7,3},{8,12},{9,13},{10,... | collective-permute-start | bytes 1572872 | tf_op jit(solution)/shard_map/ppermute | solution.py:37
  84.5 8.9 %collective-permute-start.29 = (bf16[1024,256]{1,0:T(8,128)(2,1)S(1)}, bf16[1024,256]{1,0:T(8,128)(2,1)S(1)}, u32[]{:S(2)}, u32[]{:S(2)}) collective-permute-start(bf16[1024,256]{1,0:T(8,128)(2,1)S(1)} %collective-permute-done.25.refs_3_), channel_id=1, source_target_pairs={{0,4},{1,5},{2,6},{3,7},{4,0},{5,1},{6,2},{7,3},{8,12},{9,13},{10,... | collective-permute-start | bytes 1572872 | tf_op jit(solution)/shard_map/ppermute | solution.py:37
  85.0 9.2 %collective-permute-start.31 = (bf16[1024,256]{1,0:T(8,128)(2,1)S(1)}, bf16[1024,256]{1,0:T(8,128)(2,1)S(1)}, u32[]{:S(2)}, u32[]{:S(2)}) collective-permute-start(bf16[1024,256]{1,0:T(8,128)(2,1)S(1)} %collective-permute-done.26.refs_1_), channel_id=1, source_target_pairs={{0,2},{1,0},{2,3},{3,1},{4,5},{5,7},{6,4},{7,6},{8,10},{9,8},{10,1... | collective-permute-start | bytes 1572872 | tf_op jit(solution)/shard_map/ppermute | solution.py:37
  (2 other events, 23.6 us)

commit v5 on v4

--- a/solution.py
+++ b/solution.py
@@ -334,8 +334,7 @@
             4: [("rise", 3, 0, 1)],
             5: [("slab", 0)],
             6: [("rise", 2, -1, 0)],
-            8: [("rise", 3, -1, 1)],
-            9: [("slab", 1)],
+            9: [("rise", 3, -1, 1), ("slab", 1)],
             10: [("slab", 2)],
         }
         stages = []

time: 104 us -> 102 us (0.981)
  waiting for transfers between devices: 37.1 us -> 34.9 us
    ppermute x33, waiting for transfers between devices: 37.1 us -> 34.9 us  [permute(): return lax.ppermute(value, axes, pairs)]
  transfers between devices with their start and end apart: 33 -> 33, of which waited for: 14 -> 15; matrix products, arithmetic and copies ran while one was open for 2% -> 2% of each run, Pallas kernels for 29% -> 29%
where the time goes in v5:
time: 102 us; the launch traced here: 101 us
  Pallas kernels  37.7 us (37%)
  waiting for transfers between devices  34.9 us (34%)
  starting transfers between devices  26.2 us (26%)
  other arithmetic  1.59 us (2%)
    ppermute x33, waiting for transfers between devices, permute(): return lax.ppermute(value, axes, pairs)  34.9 us
    pallas_call x4, Pallas kernels, slab(): pl.pallas_call(functools.partial(slab_kernel, layout, shift, first, last)...  30.6 us
    ppermute x33, starting transfers between devices, permute(): return lax.ppermute(value, axes, pairs)  26.2 us
    pallas_call x1, Pallas kernels, local_terms(): pl.pallas_call(functools.partial(local_kernel, steps), grid=(steps,), in_...  7.1 us
  transfers between devices with their start and end apart: 33, of which 15 were waited for; matrix products, arithmetic and copies ran while one was open for 2% of the time, Pallas kernels for 29%

profile of v5, /device:TPU:0, one launch (start us, length us, event | category | flops | bytes accessed | tf_op | source)
XLA Modules:
  0.0 101.3 jit_solution(7896993847192903460)
XLA Ops:
  0.6 3.0 %collective-permute-start.1 = (bf16[1024,256]{1,0:T(8,128)(2,1)}, bf16[1024,256]{1,0:T(8,128)(2,1)S(1)}, u32[]{:S(2)}, u32[]{:S(2)}) collective-permute-start(bf16[1024,256]{1,0:T(8,128)(2,1)} %refs_0_), channel_id=1, source_target_pairs={{0,2},{1,0},{2,3},{3,1},{4,5},{5,7},{6,4},{7,6},{8,10},{9,8},{10,1... | collective-permute-start | bytes 1572872 | tf_op jit(solution)/shard_map/ppermute | solution.py:37
  3.7 1.0 %collective-permute-start = (bf16[1024,256]{1,0:T(8,128)(2,1)}, bf16[1024,256]{1,0:T(8,128)(2,1)S(1)}, u32[]{:S(2)}, u32[]{:S(2)}) collective-permute-start(bf16[1024,256]{1,0:T(8,128)(2,1)} %refs_0_), channel_id=1, source_target_pairs={{0,1},{1,3},{2,0},{3,2},{4,6},{5,4},{6,7},{7,5},{8,9},{9,11},{10,8... | collective-permute-start | bytes 1572872 | tf_op jit(solution)/shard_map/ppermute | solution.py:37
  4.7 1.6 %collective-permute-start.3 = (bf16[1024,256]{1,0:T(8,128)(2,1)}, bf16[1024,256]{1,0:T(8,128)(2,1)S(1)}, u32[]{:S(2)}, u32[]{:S(2)}) collective-permute-start(bf16[1024,256]{1,0:T(8,128)(2,1)} %refs_0_), channel_id=1, source_target_pairs={{0,8},{1,9},{2,10},{3,11},{4,12},{5,13},{6,14},{7,15},{8,16},{9,17... | collective-permute-start | bytes 1572872 | tf_op jit(solution)/shard_map/ppermute | solution.py:37
  6.3 7.1 %local_terms.1 = (bf16[512,16]{1,0:T(8,128)(2,1)S(1)}, bf16[512,16]{1,0:T(8,128)(2,1)S(1)}, f32[16,9216]{1,0:T(8,128)S(1)}) custom-call(bf16[512,8192]{1,0:T(8,128)(2,1)} %bitcast.10, bf16[512,1024]{1,0:T(8,128)(2,1)} %bitcast.16, bf16[16,8192]{1,0:T(8,128)(2,1)} %bitcast.21, bf16[16,1024]{1,0:T(8,128)(2,1)} %bitcast.26), custom_call_target="tpu_custom_call" | custom-call | flops 1 | bytes 1 | tf_op jit(solution)/shard_map/local_terms/pallas_call | solution.py:101
  13.4 1.9 %collective-permute-done.1.refs_1_ = bf16[1024,256]{1,0:T(8,128)(2,1)S(1)} collective-permute-done((bf16[1024,256]{1,0:T(8,128)(2,1)}, bf16[1024,256]{1,0:T(8,128)(2,1)S(1)}, u32[]{:S(2)}, u32[]{:S(2)}) %collective-permute-start.1) | collective-permute-done | bytes 524320 | tf_op jit(solution)/shard_map/ppermute | solution.py:37
  15.3 2.5 %collective-permute-start.5 = (bf16[1024,256]{1,0:T(8,128)(2,1)S(1)}, bf16[1024,256]{1,0:T(8,128)(2,1)S(1)}, u32[]{:S(2)}, u32[]{:S(2)}) collective-permute-start(bf16[1024,256]{1,0:T(8,128)(2,1)S(1)} %collective-permute-done.1.refs_1_), channel_id=1, source_target_pairs={{0,2},{1,0},{2,3},{3,1},{4,5},{5,7},{6,4},{7,6},{8,10},{9,8},{10,1... | collective-permute-start | bytes 1572872 | tf_op jit(solution)/shard_map/ppermute | solution.py:37
  17.7 3.6 %collective-permute-done.3.refs_0_ = bf16[1024,256]{1,0:T(8,128)(2,1)S(1)} collective-permute-done((bf16[1024,256]{1,0:T(8,128)(2,1)}, bf16[1024,256]{1,0:T(8,128)(2,1)S(1)}, u32[]{:S(2)}, u32[]{:S(2)}) %collective-permute-start.3) | collective-permute-done | bytes 524320 | tf_op jit(solution)/shard_map/ppermute | solution.py:37
  22.4 2.2 %collective-permute-start.8 = (bf16[1024,256]{1,0:T(8,128)(2,1)S(1)}, bf16[1024,256]{1,0:T(8,128)(2,1)S(1)}, u32[]{:S(2)}, u32[]{:S(2)}) collective-permute-start(bf16[1024,256]{1,0:T(8,128)(2,1)S(1)} %copy-done), channel_id=1, source_target_pairs={{0,24},{1,25},{2,26},{3,27},{4,28},{5,29},{6,30},{7,31},{8,0},{9,1... | collective-permute-start | bytes 1572872 | tf_op jit(solution)/shard_map/ppermute | solution.py:37
  24.6 1.8 %collective-permute-done.5.refs_2_ = bf16[1024,256]{1,0:T(8,128)(2,1)S(1)} collective-permute-done((bf16[1024,256]{1,0:T(8,128)(2,1)S(1)}, bf16[1024,256]{1,0:T(8,128)(2,1)S(1)}, u32[]{:S(2)}, u32[]{:S(2)}) %collective-permute-start.5) | collective-permute-done | bytes 524320 | tf_op jit(solution)/shard_map/ppermute | solution.py:37
  26.4 2.5 %collective-permute-start.11 = (bf16[1024,256]{1,0:T(8,128)(2,1)S(1)}, bf16[1024,256]{1,0:T(8,128)(2,1)S(1)}, u32[]{:S(2)}, u32[]{:S(2)}) collective-permute-start(bf16[1024,256]{1,0:T(8,128)(2,1)S(1)} %collective-permute-done.3.refs_0_), channel_id=1, source_target_pairs={{0,2},{1,0},{2,3},{3,1},{4,5},{5,7},{6,4},{7,6},{8,10},{9,8},{10,1... | collective-permute-start | bytes 1572872 | tf_op jit(solution)/shard_map/ppermute | solution.py:37
  28.9 3.1 %collective-permute-done.10 = f32[16,9216]{1,0:T(8,128)S(1)} collective-permute-done((f32[16,9216]{1,0:T(8,128)S(1)}, f32[16,9216]{1,0:T(8,128)S(1)}, u32[]{:S(2)}, u32[]{:S(2)}) %collective-permute-start.10) | collective-permute-done | bytes 589856 | tf_op jit(solution)/shard_map/ppermute | solution.py:37
  32.1 3.8 %collective-permute-done.8.refs_0_ = bf16[1024,256]{1,0:T(8,128)(2,1)S(1)} collective-permute-done((bf16[1024,256]{1,0:T(8,128)(2,1)S(1)}, bf16[1024,256]{1,0:T(8,128)(2,1)S(1)}, u32[]{:S(2)}, u32[]{:S(2)}) %collective-permute-start.8) | collective-permute-done | bytes 524320 | tf_op jit(solution)/shard_map/ppermute | solution.py:37
  35.9 1.5 %collective-permute-start.13 = (bf16[1024,256]{1,0:T(8,128)(2,1)S(1)}, bf16[1024,256]{1,0:T(8,128)(2,1)S(1)}, u32[]{:S(2)}, u32[]{:S(2)}) collective-permute-start(bf16[1024,256]{1,0:T(8,128)(2,1)S(1)} %collective-permute-done.3.refs_0_), channel_id=1, source_target_pairs={{0,1},{1,3},{2,0},{3,2},{4,6},{5,4},{6,7},{7,5},{8,9},{9,11},{10,8... | collective-permute-start | bytes 1572872 | tf_op jit(solution)/shard_map/ppermute | solution.py:37
  37.9 1.5 %collective-permute-start.16 = (bf16[1024,256]{1,0:T(8,128)(2,1)S(1)}, bf16[1024,256]{1,0:T(8,128)(2,1)S(1)}, u32[]{:S(2)}, u32[]{:S(2)}) collective-permute-start(bf16[1024,256]{1,0:T(8,128)(2,1)S(1)} %collective-permute-done.8.refs_0_), channel_id=1, source_target_pairs={{0,2},{1,0},{2,3},{3,1},{4,5},{5,7},{6,4},{7,6},{8,10},{9,8},{10,1... | collective-permute-start | bytes 1572872 | tf_op jit(solution)/shard_map/ppermute | solution.py:37
  39.5 8.1 %slab.4 = (f32[512,1024]{1,0:T(8,128)S(1)}, bf16[512,8192]{1,0:T(8,128)(2,1)}) custom-call(bf16[1024,256]{1,0:T(8,128)(2,1)S(1)} %copy-done, bf16[1024,256]{1,0:T(8,128)(2,1)S(1)} %collective-permute-done.1.refs_1_, bf16[1024,256]{1,0:T(8,128)(2,1)S(1)} %collective-permute-done.5.refs_2_, bf16[1024,256]{1,0:T(8,128)(2,1)S(1)} %collective-permute-done.refs_3_, ...), custom_call_target="tpu_custom_call" | custom-call | flops 1 | bytes 1 | tf_op jit(solution)/shard_map/slab/pallas_call | solution.py:296
  47.6 1.5 %collective-permute-done.13.refs_3_ = bf16[1024,256]{1,0:T(8,128)(2,1)S(1)} collective-permute-done((bf16[1024,256]{1,0:T(8,128)(2,1)S(1)}, bf16[1024,256]{1,0:T(8,128)(2,1)S(1)}, u32[]{:S(2)}, u32[]{:S(2)}) %collective-permute-start.13) | collective-permute-done | bytes 524320 | tf_op jit(solution)/shard_map/ppermute | solution.py:37
  49.2 4.1 %collective-permute-done.14.refs_0_ = bf16[1024,256]{1,0:T(8,128)(2,1)S(1)} collective-permute-done((bf16[1024,256]{1,0:T(8,128)(2,1)S(1)}, bf16[1024,256]{1,0:T(8,128)(2,1)S(1)}, u32[]{:S(2)}, u32[]{:S(2)}) %collective-permute-start.14) | collective-permute-done | bytes 524320 | tf_op jit(solution)/shard_map/ppermute | solution.py:37
  53.8 1.1 %collective-permute-start.19 = (bf16[1024,256]{1,0:T(8,128)(2,1)S(1)}, bf16[1024,256]{1,0:T(8,128)(2,1)S(1)}, u32[]{:S(2)}, u32[]{:S(2)}) collective-permute-start(bf16[1024,256]{1,0:T(8,128)(2,1)S(1)} %collective-permute-done.11.refs_1_), channel_id=1, source_target_pairs={{0,2},{1,0},{2,3},{3,1},{4,5},{5,7},{6,4},{7,6},{8,10},{9,8},{10,1... | collective-permute-start | bytes 1572872 | tf_op jit(solution)/shard_map/ppermute | solution.py:37
  54.9 1.7 %collective-permute-start.20 = (bf16[1024,256]{1,0:T(8,128)(2,1)S(1)}, bf16[1024,256]{1,0:T(8,128)(2,1)S(1)}, u32[]{:S(2)}, u32[]{:S(2)}) collective-permute-start(bf16[1024,256]{1,0:T(8,128)(2,1)S(1)} %collective-permute-done.refs_3_), channel_id=1, source_target_pairs={{0,24},{1,25},{2,26},{3,27},{4,28},{5,29},{6,30},{7,31},{8,0},{9,1... | collective-permute-start | bytes 1572872 | tf_op jit(solution)/shard_map/ppermute | solution.py:37
  56.7 1.6 %collective-permute-start.22 = (bf16[1024,256]{1,0:T(8,128)(2,1)S(1)}, bf16[1024,256]{1,0:T(8,128)(2,1)S(1)}, u32[]{:S(2)}, u32[]{:S(2)}) collective-permute-start(bf16[1024,256]{1,0:T(8,128)(2,1)S(1)} %collective-permute-done.16.refs_1_), channel_id=1, source_target_pairs={{0,2},{1,0},{2,3},{3,1},{4,5},{5,7},{6,4},{7,6},{8,10},{9,8},{10,1... | collective-permute-start | bytes 1572872 | tf_op jit(solution)/shard_map/ppermute | solution.py:37
  58.4 4.6 %collective-permute-done.19.refs_2_ = bf16[1024,256]{1,0:T(8,128)(2,1)S(1)} collective-permute-done((bf16[1024,256]{1,0:T(8,128)(2,1)S(1)}, bf16[1024,256]{1,0:T(8,128)(2,1)S(1)}, u32[]{:S(2)}, u32[]{:S(2)}) %collective-permute-start.19) | collective-permute-done | bytes 524320 | tf_op jit(solution)/shard_map/ppermute | solution.py:37
  63.0 5.3 %collective-permute-done.20.refs_3_ = bf16[1024,256]{1,0:T(8,128)(2,1)S(1)} collective-permute-done((bf16[1024,256]{1,0:T(8,128)(2,1)S(1)}, bf16[1024,256]{1,0:T(8,128)(2,1)S(1)}, u32[]{:S(2)}, u32[]{:S(2)}) %collective-permute-start.20) | collective-permute-done | bytes 524320 | tf_op jit(solution)/shard_map/ppermute | solution.py:37
  68.8 1.1 %collective-permute-start.25 = (bf16[1024,256]{1,0:T(8,128)(2,1)S(1)}, bf16[1024,256]{1,0:T(8,128)(2,1)S(1)}, u32[]{:S(2)}, u32[]{:S(2)}) collective-permute-start(bf16[1024,256]{1,0:T(8,128)(2,1)S(1)} %collective-permute-done.14.refs_0_), channel_id=1, source_target_pairs={{0,2},{1,0},{2,3},{3,1},{4,5},{5,7},{6,4},{7,6},{8,10},{9,8},{10,1... | collective-permute-start | bytes 1572872 | tf_op jit(solution)/shard_map/ppermute | solution.py:37
  70.2 0.7 collective-permute-done.24.refs_5_
  71.1 1.1 %collective-permute-start.29 = (f32[16,9216]{1,0:T(8,128)S(1)}, f32[16,9216]{1,0:T(8,128)S(1)}, u32[]{:S(2)}, u32[]{:S(2)}) collective-permute-start(f32[16,9216]{1,0:T(8,128)S(1)} %add.6), channel_id=1, source_target_pairs={{0,2},{1,3},{2,0},{3,1},{4,5},{5,4},{6,7},{7,6},{8,10},{9,11},{10,... | collective-permute-start | bytes 1769480 | tf_op jit(solution)/shard_map/ppermute | solution.py:37
  72.2 7.3 %slab.5 = (f32[512,1024]{1,0:T(8,128)S(1)}, bf16[512,8192]{1,0:T(8,128)(2,1)}) custom-call(bf16[1024,256]{1,0:T(8,128)(2,1)S(1)} %collective-permute-done.3.refs_0_, bf16[1024,256]{1,0:T(8,128)(2,1)S(1)} %collective-permute-done.11.refs_1_, bf16[1024,256]{1,0:T(8,128)(2,1)S(1)} %collective-permute-done.19.refs_2_, ...), custom_call_target="tpu_custom_call", output_to_operand_aliasing={{1}: (13, {}), {0}: (12, {})} | custom-call | flops 1 | bytes 1 | tf_op jit(solution)/shard_map/slab/pallas_call | solution.py:296
  79.5 2.4 %collective-permute-done.25.refs_1_ = bf16[1024,256]{1,0:T(8,128)(2,1)S(1)} collective-permute-done((bf16[1024,256]{1,0:T(8,128)(2,1)S(1)}, bf16[1024,256]{1,0:T(8,128)(2,1)S(1)}, u32[]{:S(2)}, u32[]{:S(2)}) %collective-permute-start.25) | collective-permute-done | bytes 524320 | tf_op jit(solution)/shard_map/ppermute | solution.py:37
  81.8 7.3 %slab.6 = (f32[512,1024]{1,0:T(8,128)S(1)}, bf16[512,8192]{1,0:T(8,128)(2,1)}) custom-call(bf16[1024,256]{1,0:T(8,128)(2,1)S(1)} %collective-permute-done.8.refs_0_, bf16[1024,256]{1,0:T(8,128)(2,1)S(1)} %collective-permute-done.16.refs_1_, bf16[1024,256]{1,0:T(8,128)(2,1)S(1)} %collective-permute-done.22.refs_2_, ...), custom_call_target="tpu_custom_call", output_to_operand_aliasing={{1}: (13, {}), {0}: (12, {})} | custom-call | flops 1 | bytes 1 | tf_op jit(solution)/shard_map/slab/pallas_call | solution.py:296
  89.8 1.2 %collective-permute-done.30.refs_2_ = bf16[1024,256]{1,0:T(8,128)(2,1)S(1)} collective-permute-done((bf16[1024,256]{1,0:T(8,128)(2,1)S(1)}, bf16[1024,256]{1,0:T(8,128)(2,1)S(1)}, u32[]{:S(2)}, u32[]{:S(2)}) %collective-permute-start.30) | collective-permute-done | bytes 524320 | tf_op jit(solution)/shard_map/ppermute | solution.py:37
  91.7 0.8 multiply_bitcast_fusion
  92.5 0.6 multiply_bitcast_fusion.1
  93.2 7.9 %slab.7 = (bf16[512,1024]{1,0:T(8,128)(2,1)}, bf16[512,8192]{1,0:T(8,128)(2,1)}) custom-call(bf16[1024,256]{1,0:T(8,128)(2,1)S(1)} %collective-permute-done.14.refs_0_, bf16[1024,256]{1,0:T(8,128)(2,1)S(1)} %collective-permute-done.25.refs_1_, bf16[1024,256]{1,0:T(8,128)(2,1)S(1)} %collective-permute-done.30.refs_2_, ...), custom_call_target="tpu_custom_call", output_to_operand_aliasing={{1}: (13, {})} | custom-call | flops 1 | bytes 1 | tf_op jit(solution)/shard_map/slab/pallas_call | solution.py:296
  (45 shorter events, 4.7 us)
Async XLA Ops:
  0.6 14.6 %collective-permute-start.1 = (bf16[1024,256]{1,0:T(8,128)(2,1)}, bf16[1024,256]{1,0:T(8,128)(2,1)S(1)}, u32[]{:S(2)}, u32[]{:S(2)}) collective-permute-start(bf16[1024,256]{1,0:T(8,128)(2,1)} %refs_0_), channel_id=1, source_target_pairs={{0,2},{1,0},{2,3},{3,1},{4,5},{5,7},{6,4},{7,6},{8,10},{9,8},{10,1... | collective-permute-start | bytes 1572872 | tf_op jit(solution)/shard_map/ppermute | solution.py:37
  3.7 11.6 %collective-permute-start.2 = (bf16[1024,256]{1,0:T(8,128)(2,1)}, bf16[1024,256]{1,0:T(8,128)(2,1)S(1)}, u32[]{:S(2)}, u32[]{:S(2)}) collective-permute-start(bf16[1024,256]{1,0:T(8,128)(2,1)} %refs_0_), channel_id=1, source_target_pairs={{0,4},{1,5},{2,6},{3,7},{4,0},{5,1},{6,2},{7,3},{8,12},{9,13},{10,... | collective-permute-start | bytes 1572872 | tf_op jit(solution)/shard_map/ppermute | solution.py:37
  3.7 14.1 %collective-permute-start = (bf16[1024,256]{1,0:T(8,128)(2,1)}, bf16[1024,256]{1,0:T(8,128)(2,1)S(1)}, u32[]{:S(2)}, u32[]{:S(2)}) collective-permute-start(bf16[1024,256]{1,0:T(8,128)(2,1)} %refs_0_), channel_id=1, source_target_pairs={{0,1},{1,3},{2,0},{3,2},{4,6},{5,4},{6,7},{7,5},{8,9},{9,11},{10,8... | collective-permute-start | bytes 1572872 | tf_op jit(solution)/shard_map/ppermute | solution.py:37
  4.7 16.6 %collective-permute-start.3 = (bf16[1024,256]{1,0:T(8,128)(2,1)}, bf16[1024,256]{1,0:T(8,128)(2,1)S(1)}, u32[]{:S(2)}, u32[]{:S(2)}) collective-permute-start(bf16[1024,256]{1,0:T(8,128)(2,1)} %refs_0_), channel_id=1, source_target_pairs={{0,8},{1,9},{2,10},{3,11},{4,12},{5,13},{6,14},{7,15},{8,16},{9,17... | collective-permute-start | bytes 1572872 | tf_op jit(solution)/shard_map/ppermute | solution.py:37
  15.3 6.1 %collective-permute-start.4 = (bf16[1024,256]{1,0:T(8,128)(2,1)S(1)}, bf16[1024,256]{1,0:T(8,128)(2,1)S(1)}, u32[]{:S(2)}, u32[]{:S(2)}) collective-permute-start(bf16[1024,256]{1,0:T(8,128)(2,1)S(1)} %collective-permute-done.1.refs_1_), channel_id=1, source_target_pairs={{0,4},{1,5},{2,6},{3,7},{4,0},{5,1},{6,2},{7,3},{8,12},{9,13},{10,... | collective-permute-start | bytes 1572872 | tf_op jit(solution)/shard_map/ppermute | solution.py:37
  15.3 11.1 %collective-permute-start.5 = (bf16[1024,256]{1,0:T(8,128)(2,1)S(1)}, bf16[1024,256]{1,0:T(8,128)(2,1)S(1)}, u32[]{:S(2)}, u32[]{:S(2)}) collective-permute-start(bf16[1024,256]{1,0:T(8,128)(2,1)S(1)} %collective-permute-done.1.refs_1_), channel_id=1, source_target_pairs={{0,2},{1,0},{2,3},{3,1},{4,5},{5,7},{6,4},{7,6},{8,10},{9,8},{10,1... | collective-permute-start | bytes 1572872 | tf_op jit(solution)/shard_map/ppermute | solution.py:37
  21.3 5.1 %collective-permute-start.6 = (bf16[1024,256]{1,0:T(8,128)(2,1)S(1)}, bf16[1024,256]{1,0:T(8,128)(2,1)S(1)}, u32[]{:S(2)}, u32[]{:S(2)}) collective-permute-start(bf16[1024,256]{1,0:T(8,128)(2,1)S(1)} %collective-permute-done.refs_3_), channel_id=1, source_target_pairs={{0,4},{1,5},{2,6},{3,7},{4,0},{5,1},{6,2},{7,3},{8,12},{9,13},{10,... | collective-permute-start | bytes 1572872 | tf_op jit(solution)/shard_map/ppermute | solution.py:37
  21.3 5.1 %collective-permute-start.7 = (bf16[1024,256]{1,0:T(8,128)(2,1)S(1)}, bf16[1024,256]{1,0:T(8,128)(2,1)S(1)}, u32[]{:S(2)}, u32[]{:S(2)}) collective-permute-start(bf16[1024,256]{1,0:T(8,128)(2,1)S(1)} %collective-permute-done.3.refs_0_), channel_id=1, source_target_pairs={{0,4},{1,5},{2,6},{3,7},{4,0},{5,1},{6,2},{7,3},{8,12},{9,13},{10,... | collective-permute-start | bytes 1572872 | tf_op jit(solution)/shard_map/ppermute | solution.py:37
  21.8 10.2 %collective-permute-start.10 = (f32[16,9216]{1,0:T(8,128)S(1)}, f32[16,9216]{1,0:T(8,128)S(1)}, u32[]{:S(2)}, u32[]{:S(2)}) collective-permute-start(f32[16,9216]{1,0:T(8,128)S(1)} %get-tuple-element.203), channel_id=1, source_target_pairs={{0,1},{1,0},{2,3},{3,2},{4,6},{5,7},{6,4},{7,5},{8,9},{9,8},{10,11... | collective-permute-start | bytes 1769480 | tf_op jit(solution)/shard_map/ppermute | solution.py:37
  22.4 13.5 %collective-permute-start.8 = (bf16[1024,256]{1,0:T(8,128)(2,1)S(1)}, bf16[1024,256]{1,0:T(8,128)(2,1)S(1)}, u32[]{:S(2)}, u32[]{:S(2)}) collective-permute-start(bf16[1024,256]{1,0:T(8,128)(2,1)S(1)} %copy-done), channel_id=1, source_target_pairs={{0,24},{1,25},{2,26},{3,27},{4,28},{5,29},{6,30},{7,31},{8,0},{9,1... | collective-permute-start | bytes 1572872 | tf_op jit(solution)/shard_map/ppermute | solution.py:37
  26.4 9.5 %collective-permute-start.9 = (bf16[1024,256]{1,0:T(8,128)(2,1)S(1)}, bf16[1024,256]{1,0:T(8,128)(2,1)S(1)}, u32[]{:S(2)}, u32[]{:S(2)}) collective-permute-start(bf16[1024,256]{1,0:T(8,128)(2,1)S(1)} %collective-permute-done.5.refs_2_), channel_id=1, source_target_pairs={{0,4},{1,5},{2,6},{3,7},{4,0},{5,1},{6,2},{7,3},{8,12},{9,13},{10,... | collective-permute-start | bytes 1572872 | tf_op jit(solution)/shard_map/ppermute | solution.py:37
  26.4 11.4 %collective-permute-start.11 = (bf16[1024,256]{1,0:T(8,128)(2,1)S(1)}, bf16[1024,256]{1,0:T(8,128)(2,1)S(1)}, u32[]{:S(2)}, u32[]{:S(2)}) collective-permute-start(bf16[1024,256]{1,0:T(8,128)(2,1)S(1)} %collective-permute-done.3.refs_0_), channel_id=1, source_target_pairs={{0,2},{1,0},{2,3},{3,1},{4,5},{5,7},{6,4},{7,6},{8,10},{9,8},{10,1... | collective-permute-start | bytes 1572872 | tf_op jit(solution)/shard_map/ppermute | solution.py:37
  35.9 1.9 %collective-permute-start.12 = (bf16[1024,256]{1,0:T(8,128)(2,1)S(1)}, bf16[1024,256]{1,0:T(8,128)(2,1)S(1)}, u32[]{:S(2)}, u32[]{:S(2)}) collective-permute-start(bf16[1024,256]{1,0:T(8,128)(2,1)S(1)} %collective-permute-done.8.refs_0_), channel_id=1, source_target_pairs={{0,4},{1,5},{2,6},{3,7},{4,0},{5,1},{6,2},{7,3},{8,12},{9,13},{10,... | collective-permute-start | bytes 1572872 | tf_op jit(solution)/shard_map/ppermute | solution.py:37
  35.9 13.3 %collective-permute-start.13 = (bf16[1024,256]{1,0:T(8,128)(2,1)S(1)}, bf16[1024,256]{1,0:T(8,128)(2,1)S(1)}, u32[]{:S(2)}, u32[]{:S(2)}) collective-permute-start(bf16[1024,256]{1,0:T(8,128)(2,1)S(1)} %collective-permute-done.3.refs_0_), channel_id=1, source_target_pairs={{0,1},{1,3},{2,0},{3,2},{4,6},{5,4},{6,7},{7,5},{8,9},{9,11},{10,8... | collective-permute-start | bytes 1572872 | tf_op jit(solution)/shard_map/ppermute | solution.py:37
  37.4 15.9 %collective-permute-start.14 = (bf16[1024,256]{1,0:T(8,128)(2,1)S(1)}, bf16[1024,256]{1,0:T(8,128)(2,1)S(1)}, u32[]{:S(2)}, u32[]{:S(2)}) collective-permute-start(bf16[1024,256]{1,0:T(8,128)(2,1)S(1)} %collective-permute-done.3.refs_0_), channel_id=1, source_target_pairs={{0,8},{1,9},{2,10},{3,11},{4,12},{5,13},{6,14},{7,15},{8,16},{9,17... | collective-permute-start | bytes 1572872 | tf_op jit(solution)/shard_map/ppermute | solution.py:37
  37.8 15.4 %collective-permute-start.15 = (bf16[1024,256]{1,0:T(8,128)(2,1)S(1)}, bf16[1024,256]{1,0:T(8,128)(2,1)S(1)}, u32[]{:S(2)}, u32[]{:S(2)}) collective-permute-start(bf16[1024,256]{1,0:T(8,128)(2,1)S(1)} %collective-permute-done.11.refs_1_), channel_id=1, source_target_pairs={{0,4},{1,5},{2,6},{3,7},{4,0},{5,1},{6,2},{7,3},{8,12},{9,13},{10,... | collective-permute-start | bytes 1572872 | tf_op jit(solution)/shard_map/ppermute | solution.py:37
  37.9 18.7 %collective-permute-start.16 = (bf16[1024,256]{1,0:T(8,128)(2,1)S(1)}, bf16[1024,256]{1,0:T(8,128)(2,1)S(1)}, u32[]{:S(2)}, u32[]{:S(2)}) collective-permute-start(bf16[1024,256]{1,0:T(8,128)(2,1)S(1)} %collective-permute-done.8.refs_0_), channel_id=1, source_target_pairs={{0,2},{1,0},{2,3},{3,1},{4,5},{5,7},{6,4},{7,6},{8,10},{9,8},{10,1... | collective-permute-start | bytes 1572872 | tf_op jit(solution)/shard_map/ppermute | solution.py:37
  53.3 3.4 %collective-permute-start.17 = (bf16[1024,256]{1,0:T(8,128)(2,1)S(1)}, bf16[1024,256]{1,0:T(8,128)(2,1)S(1)}, u32[]{:S(2)}, u32[]{:S(2)}) collective-permute-start(bf16[1024,256]{1,0:T(8,128)(2,1)S(1)} %collective-permute-done.13.refs_3_), channel_id=1, source_target_pairs={{0,4},{1,5},{2,6},{3,7},{4,0},{5,1},{6,2},{7,3},{8,12},{9,13},{10,... | collective-permute-start | bytes 1572872 | tf_op jit(solution)/shard_map/ppermute | solution.py:37
  53.3 3.4 %collective-permute-start.18 = (bf16[1024,256]{1,0:T(8,128)(2,1)S(1)}, bf16[1024,256]{1,0:T(8,128)(2,1)S(1)}, u32[]{:S(2)}, u32[]{:S(2)}) collective-permute-start(bf16[1024,256]{1,0:T(8,128)(2,1)S(1)} %collective-permute-done.14.refs_0_), channel_id=1, source_target_pairs={{0,4},{1,5},{2,6},{3,7},{4,0},{5,1},{6,2},{7,3},{8,12},{9,13},{10,... | collective-permute-start | bytes 1572872 | tf_op jit(solution)/shard_map/ppermute | solution.py:37
  53.8 9.2 %collective-permute-start.19 = (bf16[1024,256]{1,0:T(8,128)(2,1)S(1)}, bf16[1024,256]{1,0:T(8,128)(2,1)S(1)}, u32[]{:S(2)}, u32[]{:S(2)}) collective-permute-start(bf16[1024,256]{1,0:T(8,128)(2,1)S(1)} %collective-permute-done.11.refs_1_), channel_id=1, source_target_pairs={{0,2},{1,0},{2,3},{3,1},{4,5},{5,7},{6,4},{7,6},{8,10},{9,8},{10,1... | collective-permute-start | bytes 1572872 | tf_op jit(solution)/shard_map/ppermute | solution.py:37
  54.9 13.4 %collective-permute-start.20 = (bf16[1024,256]{1,0:T(8,128)(2,1)S(1)}, bf16[1024,256]{1,0:T(8,128)(2,1)S(1)}, u32[]{:S(2)}, u32[]{:S(2)}) collective-permute-start(bf16[1024,256]{1,0:T(8,128)(2,1)S(1)} %collective-permute-done.refs_3_), channel_id=1, source_target_pairs={{0,24},{1,25},{2,26},{3,27},{4,28},{5,29},{6,30},{7,31},{8,0},{9,1... | collective-permute-start | bytes 1572872 | tf_op jit(solution)/shard_map/ppermute | solution.py:37
  56.7 11.7 %collective-permute-start.21 = (bf16[1024,256]{1,0:T(8,128)(2,1)S(1)}, bf16[1024,256]{1,0:T(8,128)(2,1)S(1)}, u32[]{:S(2)}, u32[]{:S(2)}) collective-permute-start(bf16[1024,256]{1,0:T(8,128)(2,1)S(1)} %collective-permute-done.16.refs_1_), channel_id=1, source_target_pairs={{0,4},{1,5},{2,6},{3,7},{4,0},{5,1},{6,2},{7,3},{8,12},{9,13},{10,... | collective-permute-start | bytes 1572872 | tf_op jit(solution)/shard_map/ppermute | solution.py:37
  56.7 13.1 %collective-permute-start.22 = (bf16[1024,256]{1,0:T(8,128)(2,1)S(1)}, bf16[1024,256]{1,0:T(8,128)(2,1)S(1)}, u32[]{:S(2)}, u32[]{:S(2)}) collective-permute-start(bf16[1024,256]{1,0:T(8,128)(2,1)S(1)} %collective-permute-done.16.refs_1_), channel_id=1, source_target_pairs={{0,2},{1,0},{2,3},{3,1},{4,5},{5,7},{6,4},{7,6},{8,10},{9,8},{10,1... | collective-permute-start | bytes 1572872 | tf_op jit(solution)/shard_map/ppermute | solution.py:37
  68.3 1.9 %collective-permute-start.23 = (bf16[1024,256]{1,0:T(8,128)(2,1)S(1)}, bf16[1024,256]{1,0:T(8,128)(2,1)S(1)}, u32[]{:S(2)}, u32[]{:S(2)}) collective-permute-start(bf16[1024,256]{1,0:T(8,128)(2,1)S(1)} %collective-permute-done.19.refs_2_), channel_id=1, source_target_pairs={{0,4},{1,5},{2,6},{3,7},{4,0},{5,1},{6,2},{7,3},{8,12},{9,13},{10,... | collective-permute-start | bytes 1572872 | tf_op jit(solution)/shard_map/ppermute | solution.py:37
  68.3 2.7 %collective-permute-start.24 = (bf16[1024,256]{1,0:T(8,128)(2,1)S(1)}, bf16[1024,256]{1,0:T(8,128)(2,1)S(1)}, u32[]{:S(2)}, u32[]{:S(2)}) collective-permute-start(bf16[1024,256]{1,0:T(8,128)(2,1)S(1)} %collective-permute-done.20.refs_3_), channel_id=1, source_target_pairs={{0,4},{1,5},{2,6},{3,7},{4,0},{5,1},{6,2},{7,3},{8,12},{9,13},{10,... | collective-permute-start | bytes 1572872 | tf_op jit(solution)/shard_map/ppermute | solution.py:37
  68.8 13.0 %collective-permute-start.25 = (bf16[1024,256]{1,0:T(8,128)(2,1)S(1)}, bf16[1024,256]{1,0:T(8,128)(2,1)S(1)}, u32[]{:S(2)}, u32[]{:S(2)}) collective-permute-start(bf16[1024,256]{1,0:T(8,128)(2,1)S(1)} %collective-permute-done.14.refs_0_), channel_id=1, source_target_pairs={{0,2},{1,0},{2,3},{3,1},{4,5},{5,7},{6,4},{7,6},{8,10},{9,8},{10,1... | collective-permute-start | bytes 1572872 | tf_op jit(solution)/shard_map/ppermute | solution.py:37
  71.0 10.8 %collective-permute-start.26 = (bf16[1024,256]{1,0:T(8,128)(2,1)S(1)}, bf16[1024,256]{1,0:T(8,128)(2,1)S(1)}, u32[]{:S(2)}, u32[]{:S(2)}) collective-permute-start(bf16[1024,256]{1,0:T(8,128)(2,1)S(1)} %collective-permute-done.22.refs_2_), channel_id=1, source_target_pairs={{0,4},{1,5},{2,6},{3,7},{4,0},{5,1},{6,2},{7,3},{8,12},{9,13},{10,... | collective-permute-start | bytes 1572872 | tf_op jit(solution)/shard_map/ppermute | solution.py:37
  71.1 18.0 %collective-permute-start.29 = (f32[16,9216]{1,0:T(8,128)S(1)}, f32[16,9216]{1,0:T(8,128)S(1)}, u32[]{:S(2)}, u32[]{:S(2)}) collective-permute-start(f32[16,9216]{1,0:T(8,128)S(1)} %add.6), channel_id=1, source_target_pairs={{0,2},{1,3},{2,0},{3,1},{4,5},{5,4},{6,7},{7,6},{8,10},{9,11},{10,... | collective-permute-start | bytes 1769480 | tf_op jit(solution)/shard_map/ppermute | solution.py:37
  72.2 17.1 %collective-permute-start.27 = (bf16[1024,256]{1,0:T(8,128)(2,1)S(1)}, bf16[1024,256]{1,0:T(8,128)(2,1)S(1)}, u32[]{:S(2)}, u32[]{:S(2)}) collective-permute-start(bf16[1024,256]{1,0:T(8,128)(2,1)S(1)} %collective-permute-done.13.refs_3_), channel_id=1, source_target_pairs={{0,8},{1,9},{2,10},{3,11},{4,12},{5,13},{6,14},{7,15},{8,16},{9,17... | collective-permute-start | bytes 1572872 | tf_op jit(solution)/shard_map/ppermute | solution.py:37
  81.8 7.4 %collective-permute-start.28 = (bf16[1024,256]{1,0:T(8,128)(2,1)S(1)}, bf16[1024,256]{1,0:T(8,128)(2,1)S(1)}, u32[]{:S(2)}, u32[]{:S(2)}) collective-permute-start(bf16[1024,256]{1,0:T(8,128)(2,1)S(1)} %collective-permute-done.25.refs_1_), channel_id=1, source_target_pairs={{0,4},{1,5},{2,6},{3,7},{4,0},{5,1},{6,2},{7,3},{8,12},{9,13},{10,... | collective-permute-start | bytes 1572872 | tf_op jit(solution)/shard_map/ppermute | solution.py:37
  81.8 9.2 %collective-permute-start.30 = (bf16[1024,256]{1,0:T(8,128)(2,1)S(1)}, bf16[1024,256]{1,0:T(8,128)(2,1)S(1)}, u32[]{:S(2)}, u32[]{:S(2)}) collective-permute-start(bf16[1024,256]{1,0:T(8,128)(2,1)S(1)} %collective-permute-done.25.refs_1_), channel_id=1, source_target_pairs={{0,2},{1,0},{2,3},{3,1},{4,5},{5,7},{6,4},{7,6},{8,10},{9,8},{10,1... | collective-permute-start | bytes 1572872 | tf_op jit(solution)/shard_map/ppermute | solution.py:37
  89.2 2.1 %collective-permute-start.31 = (bf16[1024,256]{1,0:T(8,128)(2,1)S(1)}, bf16[1024,256]{1,0:T(8,128)(2,1)S(1)}, u32[]{:S(2)}, u32[]{:S(2)}) collective-permute-start(bf16[1024,256]{1,0:T(8,128)(2,1)S(1)} %collective-permute-done.27.refs_3_), channel_id=1, source_target_pairs={{0,4},{1,5},{2,6},{3,7},{4,0},{5,1},{6,2},{7,3},{8,12},{9,13},{10,... | collective-permute-start | bytes 1572872 | tf_op jit(solution)/shard_map/ppermute | solution.py:37
  (2 other events, 23.6 us)

commit v6 on v5

--- a/solution.py
+++ b/solution.py
@@ -333,7 +333,7 @@
             2: [("rise", 2, 0, 0)],
             4: [("rise", 3, 0, 1)],
             5: [("slab", 0)],
-            6: [("rise", 2, -1, 0)],
+            7: [("rise", 2, -1, 0)],
             9: [("rise", 3, -1, 1), ("slab", 1)],
             10: [("slab", 2)],
         }

time: 102 us -> 101 us (level)
  transfers between devices with their start and end apart: 33 -> 33, of which waited for: 15 -> 15; matrix products, arithmetic and copies ran while one was open for 2% -> 2% of each run, Pallas kernels for 29% -> 30%
where the time goes in v6:
time: 101 us
  Pallas kernels  37.7 us (37%)
  waiting for transfers between devices  34.3 us (34%)
  starting transfers between devices  26.1 us (26%)
  other arithmetic  1.59 us (2%)
    ppermute x33, waiting for transfers between devices, permute(): return lax.ppermute(value, axes, pairs)  34.3 us
    pallas_call x4, Pallas kernels, slab(): pl.pallas_call(functools.partial(slab_kernel, layout, shift, first, last)...  30.6 us
    ppermute x33, starting transfers between devices, permute(): return lax.ppermute(value, axes, pairs)  26.1 us
    pallas_call x1, Pallas kernels, local_terms(): pl.pallas_call(functools.partial(local_kernel, steps), grid=(steps,), in_...  7.1 us
  transfers between devices with their start and end apart: 33, of which 15 were waited for; matrix products, arithmetic and copies ran while one was open for 2% of the time, Pallas kernels for 30%

profile of v6, /device:TPU:0, one launch (start us, length us, event | category | flops | bytes accessed | tf_op | source)
XLA Modules:
  0.0 100.6 jit_solution(11205982341063382866)
XLA Ops:
  0.6 3.0 %collective-permute-start.1 = (bf16[1024,256]{1,0:T(8,128)(2,1)}, bf16[1024,256]{1,0:T(8,128)(2,1)S(1)}, u32[]{:S(2)}, u32[]{:S(2)}) collective-permute-start(bf16[1024,256]{1,0:T(8,128)(2,1)} %refs_0_), channel_id=1, source_target_pairs={{0,2},{1,0},{2,3},{3,1},{4,5},{5,7},{6,4},{7,6},{8,10},{9,8},{10,1... | collective-permute-start | bytes 1572872 | tf_op jit(solution)/shard_map/ppermute | solution.py:37
  3.7 1.0 %collective-permute-start = (bf16[1024,256]{1,0:T(8,128)(2,1)}, bf16[1024,256]{1,0:T(8,128)(2,1)S(1)}, u32[]{:S(2)}, u32[]{:S(2)}) collective-permute-start(bf16[1024,256]{1,0:T(8,128)(2,1)} %refs_0_), channel_id=1, source_target_pairs={{0,1},{1,3},{2,0},{3,2},{4,6},{5,4},{6,7},{7,5},{8,9},{9,11},{10,8... | collective-permute-start | bytes 1572872 | tf_op jit(solution)/shard_map/ppermute | solution.py:37
  4.7 1.6 %collective-permute-start.3 = (bf16[1024,256]{1,0:T(8,128)(2,1)}, bf16[1024,256]{1,0:T(8,128)(2,1)S(1)}, u32[]{:S(2)}, u32[]{:S(2)}) collective-permute-start(bf16[1024,256]{1,0:T(8,128)(2,1)} %refs_0_), channel_id=1, source_target_pairs={{0,8},{1,9},{2,10},{3,11},{4,12},{5,13},{6,14},{7,15},{8,16},{9,17... | collective-permute-start | bytes 1572872 | tf_op jit(solution)/shard_map/ppermute | solution.py:37
  6.3 7.1 %local_terms.1 = (bf16[512,16]{1,0:T(8,128)(2,1)S(1)}, bf16[512,16]{1,0:T(8,128)(2,1)S(1)}, f32[16,9216]{1,0:T(8,128)S(1)}) custom-call(bf16[512,8192]{1,0:T(8,128)(2,1)} %bitcast.10, bf16[512,1024]{1,0:T(8,128)(2,1)} %bitcast.16, bf16[16,8192]{1,0:T(8,128)(2,1)} %bitcast.21, bf16[16,1024]{1,0:T(8,128)(2,1)} %bitcast.26), custom_call_target="tpu_custom_call" | custom-call | flops 1 | bytes 1 | tf_op jit(solution)/shard_map/local_terms/pallas_call | solution.py:101
  13.4 1.9 %collective-permute-done.1.refs_1_ = bf16[1024,256]{1,0:T(8,128)(2,1)S(1)} collective-permute-done((bf16[1024,256]{1,0:T(8,128)(2,1)}, bf16[1024,256]{1,0:T(8,128)(2,1)S(1)}, u32[]{:S(2)}, u32[]{:S(2)}) %collective-permute-start.1) | collective-permute-done | bytes 524320 | tf_op jit(solution)/shard_map/ppermute | solution.py:37
  15.3 2.5 %collective-permute-start.5 = (bf16[1024,256]{1,0:T(8,128)(2,1)S(1)}, bf16[1024,256]{1,0:T(8,128)(2,1)S(1)}, u32[]{:S(2)}, u32[]{:S(2)}) collective-permute-start(bf16[1024,256]{1,0:T(8,128)(2,1)S(1)} %collective-permute-done.1.refs_1_), channel_id=1, source_target_pairs={{0,2},{1,0},{2,3},{3,1},{4,5},{5,7},{6,4},{7,6},{8,10},{9,8},{10,1... | collective-permute-start | bytes 1572872 | tf_op jit(solution)/shard_map/ppermute | solution.py:37
  17.7 3.6 %collective-permute-done.3.refs_0_ = bf16[1024,256]{1,0:T(8,128)(2,1)S(1)} collective-permute-done((bf16[1024,256]{1,0:T(8,128)(2,1)}, bf16[1024,256]{1,0:T(8,128)(2,1)S(1)}, u32[]{:S(2)}, u32[]{:S(2)}) %collective-permute-start.3) | collective-permute-done | bytes 524320 | tf_op jit(solution)/shard_map/ppermute | solution.py:37
  22.4 2.2 %collective-permute-start.8 = (bf16[1024,256]{1,0:T(8,128)(2,1)S(1)}, bf16[1024,256]{1,0:T(8,128)(2,1)S(1)}, u32[]{:S(2)}, u32[]{:S(2)}) collective-permute-start(bf16[1024,256]{1,0:T(8,128)(2,1)S(1)} %copy-done), channel_id=1, source_target_pairs={{0,24},{1,25},{2,26},{3,27},{4,28},{5,29},{6,30},{7,31},{8,0},{9,1... | collective-permute-start | bytes 1572872 | tf_op jit(solution)/shard_map/ppermute | solution.py:37
  24.6 1.8 %collective-permute-done.5.refs_2_ = bf16[1024,256]{1,0:T(8,128)(2,1)S(1)} collective-permute-done((bf16[1024,256]{1,0:T(8,128)(2,1)S(1)}, bf16[1024,256]{1,0:T(8,128)(2,1)S(1)}, u32[]{:S(2)}, u32[]{:S(2)}) %collective-permute-start.5) | collective-permute-done | bytes 524320 | tf_op jit(solution)/shard_map/ppermute | solution.py:37
  26.4 2.5 %collective-permute-start.11 = (bf16[1024,256]{1,0:T(8,128)(2,1)S(1)}, bf16[1024,256]{1,0:T(8,128)(2,1)S(1)}, u32[]{:S(2)}, u32[]{:S(2)}) collective-permute-start(bf16[1024,256]{1,0:T(8,128)(2,1)S(1)} %collective-permute-done.3.refs_0_), channel_id=1, source_target_pairs={{0,2},{1,0},{2,3},{3,1},{4,5},{5,7},{6,4},{7,6},{8,10},{9,8},{10,1... | collective-permute-start | bytes 1572872 | tf_op jit(solution)/shard_map/ppermute | solution.py:37
  28.9 3.1 %collective-permute-done.10 = f32[16,9216]{1,0:T(8,128)S(1)} collective-permute-done((f32[16,9216]{1,0:T(8,128)S(1)}, f32[16,9216]{1,0:T(8,128)S(1)}, u32[]{:S(2)}, u32[]{:S(2)}) %collective-permute-start.10) | collective-permute-done | bytes 589856 | tf_op jit(solution)/shard_map/ppermute | solution.py:37
  32.1 3.8 %collective-permute-done.8.refs_0_ = bf16[1024,256]{1,0:T(8,128)(2,1)S(1)} collective-permute-done((bf16[1024,256]{1,0:T(8,128)(2,1)S(1)}, bf16[1024,256]{1,0:T(8,128)(2,1)S(1)}, u32[]{:S(2)}, u32[]{:S(2)}) %collective-permute-start.8) | collective-permute-done | bytes 524320 | tf_op jit(solution)/shard_map/ppermute | solution.py:37
  35.9 1.5 %collective-permute-start.13 = (bf16[1024,256]{1,0:T(8,128)(2,1)S(1)}, bf16[1024,256]{1,0:T(8,128)(2,1)S(1)}, u32[]{:S(2)}, u32[]{:S(2)}) collective-permute-start(bf16[1024,256]{1,0:T(8,128)(2,1)S(1)} %collective-permute-done.3.refs_0_), channel_id=1, source_target_pairs={{0,1},{1,3},{2,0},{3,2},{4,6},{5,4},{6,7},{7,5},{8,9},{9,11},{10,8... | collective-permute-start | bytes 1572872 | tf_op jit(solution)/shard_map/ppermute | solution.py:37
  37.9 1.5 %collective-permute-start.16 = (bf16[1024,256]{1,0:T(8,128)(2,1)S(1)}, bf16[1024,256]{1,0:T(8,128)(2,1)S(1)}, u32[]{:S(2)}, u32[]{:S(2)}) collective-permute-start(bf16[1024,256]{1,0:T(8,128)(2,1)S(1)} %collective-permute-done.8.refs_0_), channel_id=1, source_target_pairs={{0,2},{1,0},{2,3},{3,1},{4,5},{5,7},{6,4},{7,6},{8,10},{9,8},{10,1... | collective-permute-start | bytes 1572872 | tf_op jit(solution)/shard_map/ppermute | solution.py:37
  39.5 8.1 %slab.4 = (f32[512,1024]{1,0:T(8,128)S(1)}, bf16[512,8192]{1,0:T(8,128)(2,1)}) custom-call(bf16[1024,256]{1,0:T(8,128)(2,1)S(1)} %copy-done, bf16[1024,256]{1,0:T(8,128)(2,1)S(1)} %collective-permute-done.1.refs_1_, bf16[1024,256]{1,0:T(8,128)(2,1)S(1)} %collective-permute-done.5.refs_2_, bf16[1024,256]{1,0:T(8,128)(2,1)S(1)} %collective-permute-done.refs_3_, ...), custom_call_target="tpu_custom_call" | custom-call | flops 1 | bytes 1 | tf_op jit(solution)/shard_map/slab/pallas_call | solution.py:296
  47.6 1.5 %collective-permute-done.13.refs_3_ = bf16[1024,256]{1,0:T(8,128)(2,1)S(1)} collective-permute-done((bf16[1024,256]{1,0:T(8,128)(2,1)S(1)}, bf16[1024,256]{1,0:T(8,128)(2,1)S(1)}, u32[]{:S(2)}, u32[]{:S(2)}) %collective-permute-start.13) | collective-permute-done | bytes 524320 | tf_op jit(solution)/shard_map/ppermute | solution.py:37
  49.2 4.1 %collective-permute-done.14.refs_0_ = bf16[1024,256]{1,0:T(8,128)(2,1)S(1)} collective-permute-done((bf16[1024,256]{1,0:T(8,128)(2,1)S(1)}, bf16[1024,256]{1,0:T(8,128)(2,1)S(1)}, u32[]{:S(2)}, u32[]{:S(2)}) %collective-permute-start.14) | collective-permute-done | bytes 524320 | tf_op jit(solution)/shard_map/ppermute | solution.py:37
  53.8 1.1 %collective-permute-start.19 = (bf16[1024,256]{1,0:T(8,128)(2,1)S(1)}, bf16[1024,256]{1,0:T(8,128)(2,1)S(1)}, u32[]{:S(2)}, u32[]{:S(2)}) collective-permute-start(bf16[1024,256]{1,0:T(8,128)(2,1)S(1)} %collective-permute-done.11.refs_1_), channel_id=1, source_target_pairs={{0,2},{1,0},{2,3},{3,1},{4,5},{5,7},{6,4},{7,6},{8,10},{9,8},{10,1... | collective-permute-start | bytes 1572872 | tf_op jit(solution)/shard_map/ppermute | solution.py:37
  55.2 0.7 collective-permute-done.18.refs_4_
  56.1 1.1 %collective-permute-start.22 = (bf16[1024,256]{1,0:T(8,128)(2,1)S(1)}, bf16[1024,256]{1,0:T(8,128)(2,1)S(1)}, u32[]{:S(2)}, u32[]{:S(2)}) collective-permute-start(bf16[1024,256]{1,0:T(8,128)(2,1)S(1)} %collective-permute-done.16.refs_1_), channel_id=1, source_target_pairs={{0,2},{1,0},{2,3},{3,1},{4,5},{5,7},{6,4},{7,6},{8,10},{9,8},{10,1... | collective-permute-start | bytes 1572872 | tf_op jit(solution)/shard_map/ppermute | solution.py:37
  57.2 1.7 %collective-permute-start.21 = (bf16[1024,256]{1,0:T(8,128)(2,1)S(1)}, bf16[1024,256]{1,0:T(8,128)(2,1)S(1)}, u32[]{:S(2)}, u32[]{:S(2)}) collective-permute-start(bf16[1024,256]{1,0:T(8,128)(2,1)S(1)} %collective-permute-done.refs_3_), channel_id=1, source_target_pairs={{0,24},{1,25},{2,26},{3,27},{4,28},{5,29},{6,30},{7,31},{8,0},{9,1... | collective-permute-start | bytes 1572872 | tf_op jit(solution)/shard_map/ppermute | solution.py:37
  58.9 4.0 %collective-permute-done.19.refs_2_ = bf16[1024,256]{1,0:T(8,128)(2,1)S(1)} collective-permute-done((bf16[1024,256]{1,0:T(8,128)(2,1)S(1)}, bf16[1024,256]{1,0:T(8,128)(2,1)S(1)}, u32[]{:S(2)}, u32[]{:S(2)}) %collective-permute-start.19) | collective-permute-done | bytes 524320 | tf_op jit(solution)/shard_map/ppermute | solution.py:37
  63.0 1.1 %collective-permute-start.24 = (bf16[1024,256]{1,0:T(8,128)(2,1)S(1)}, bf16[1024,256]{1,0:T(8,128)(2,1)S(1)}, u32[]{:S(2)}, u32[]{:S(2)}) collective-permute-start(bf16[1024,256]{1,0:T(8,128)(2,1)S(1)} %collective-permute-done.14.refs_0_), channel_id=1, source_target_pairs={{0,2},{1,0},{2,3},{3,1},{4,5},{5,7},{6,4},{7,6},{8,10},{9,8},{10,1... | collective-permute-start | bytes 1572872 | tf_op jit(solution)/shard_map/ppermute | solution.py:37
  64.1 6.9 %collective-permute-done.21.refs_3_ = bf16[1024,256]{1,0:T(8,128)(2,1)S(1)} collective-permute-done((bf16[1024,256]{1,0:T(8,128)(2,1)S(1)}, bf16[1024,256]{1,0:T(8,128)(2,1)S(1)}, u32[]{:S(2)}, u32[]{:S(2)}) %collective-permute-start.21) | collective-permute-done | bytes 524320 | tf_op jit(solution)/shard_map/ppermute | solution.py:37
  71.5 1.1 %collective-permute-start.29 = (f32[16,9216]{1,0:T(8,128)S(1)}, f32[16,9216]{1,0:T(8,128)S(1)}, u32[]{:S(2)}, u32[]{:S(2)}) collective-permute-start(f32[16,9216]{1,0:T(8,128)S(1)} %add.6), channel_id=1, source_target_pairs={{0,2},{1,3},{2,0},{3,1},{4,5},{5,4},{6,7},{7,6},{8,10},{9,11},{10,... | collective-permute-start | bytes 1769480 | tf_op jit(solution)/shard_map/ppermute | solution.py:37
  72.5 7.3 %slab.5 = (f32[512,1024]{1,0:T(8,128)S(1)}, bf16[512,8192]{1,0:T(8,128)(2,1)}) custom-call(bf16[1024,256]{1,0:T(8,128)(2,1)S(1)} %collective-permute-done.3.refs_0_, bf16[1024,256]{1,0:T(8,128)(2,1)S(1)} %collective-permute-done.11.refs_1_, bf16[1024,256]{1,0:T(8,128)(2,1)S(1)} %collective-permute-done.19.refs_2_, ...), custom_call_target="tpu_custom_call", output_to_operand_aliasing={{1}: (13, {}), {0}: (12, {})} | custom-call | flops 1 | bytes 1 | tf_op jit(solution)/shard_map/slab/pallas_call | solution.py:296
  81.0 7.3 %slab.6 = (f32[512,1024]{1,0:T(8,128)S(1)}, bf16[512,8192]{1,0:T(8,128)(2,1)}) custom-call(bf16[1024,256]{1,0:T(8,128)(2,1)S(1)} %collective-permute-done.8.refs_0_, bf16[1024,256]{1,0:T(8,128)(2,1)S(1)} %collective-permute-done.16.refs_1_, bf16[1024,256]{1,0:T(8,128)(2,1)S(1)} %collective-permute-done.22.refs_2_, ...), custom_call_target="tpu_custom_call", output_to_operand_aliasing={{1}: (13, {}), {0}: (12, {})} | custom-call | flops 1 | bytes 1 | tf_op jit(solution)/shard_map/slab/pallas_call | solution.py:296
  88.7 0.9 collective-permute-done.30.refs_2_
  89.6 1.0 collective-permute-done.31.refs_5_
  90.7 0.8 multiply_bitcast_fusion
  91.5 0.6 multiply_bitcast_fusion.1
  92.5 7.9 %slab.7 = (bf16[512,1024]{1,0:T(8,128)(2,1)}, bf16[512,8192]{1,0:T(8,128)(2,1)}) custom-call(bf16[1024,256]{1,0:T(8,128)(2,1)S(1)} %collective-permute-done.14.refs_0_, bf16[1024,256]{1,0:T(8,128)(2,1)S(1)} %collective-permute-done.24.refs_1_, bf16[1024,256]{1,0:T(8,128)(2,1)S(1)} %collective-permute-done.30.refs_2_, ...), custom_call_target="tpu_custom_call", output_to_operand_aliasing={{1}: (13, {})} | custom-call | flops 1 | bytes 1 | tf_op jit(solution)/shard_map/slab/pallas_call | solution.py:296
  (45 shorter events, 5.2 us)
Async XLA Ops:
  0.6 14.6 %collective-permute-start.1 = (bf16[1024,256]{1,0:T(8,128)(2,1)}, bf16[1024,256]{1,0:T(8,128)(2,1)S(1)}, u32[]{:S(2)}, u32[]{:S(2)}) collective-permute-start(bf16[1024,256]{1,0:T(8,128)(2,1)} %refs_0_), channel_id=1, source_target_pairs={{0,2},{1,0},{2,3},{3,1},{4,5},{5,7},{6,4},{7,6},{8,10},{9,8},{10,1... | collective-permute-start | bytes 1572872 | tf_op jit(solution)/shard_map/ppermute | solution.py:37
  3.7 11.6 %collective-permute-start.2 = (bf16[1024,256]{1,0:T(8,128)(2,1)}, bf16[1024,256]{1,0:T(8,128)(2,1)S(1)}, u32[]{:S(2)}, u32[]{:S(2)}) collective-permute-start(bf16[1024,256]{1,0:T(8,128)(2,1)} %refs_0_), channel_id=1, source_target_pairs={{0,4},{1,5},{2,6},{3,7},{4,0},{5,1},{6,2},{7,3},{8,12},{9,13},{10,... | collective-permute-start | bytes 1572872 | tf_op jit(solution)/shard_map/ppermute | solution.py:37
  3.7 14.1 %collective-permute-start = (bf16[1024,256]{1,0:T(8,128)(2,1)}, bf16[1024,256]{1,0:T(8,128)(2,1)S(1)}, u32[]{:S(2)}, u32[]{:S(2)}) collective-permute-start(bf16[1024,256]{1,0:T(8,128)(2,1)} %refs_0_), channel_id=1, source_target_pairs={{0,1},{1,3},{2,0},{3,2},{4,6},{5,4},{6,7},{7,5},{8,9},{9,11},{10,8... | collective-permute-start | bytes 1572872 | tf_op jit(solution)/shard_map/ppermute | solution.py:37
  4.7 16.6 %collective-permute-start.3 = (bf16[1024,256]{1,0:T(8,128)(2,1)}, bf16[1024,256]{1,0:T(8,128)(2,1)S(1)}, u32[]{:S(2)}, u32[]{:S(2)}) collective-permute-start(bf16[1024,256]{1,0:T(8,128)(2,1)} %refs_0_), channel_id=1, source_target_pairs={{0,8},{1,9},{2,10},{3,11},{4,12},{5,13},{6,14},{7,15},{8,16},{9,17... | collective-permute-start | bytes 1572872 | tf_op jit(solution)/shard_map/ppermute | solution.py:37
  15.3 6.1 %collective-permute-start.4 = (bf16[1024,256]{1,0:T(8,128)(2,1)S(1)}, bf16[1024,256]{1,0:T(8,128)(2,1)S(1)}, u32[]{:S(2)}, u32[]{:S(2)}) collective-permute-start(bf16[1024,256]{1,0:T(8,128)(2,1)S(1)} %collective-permute-done.1.refs_1_), channel_id=1, source_target_pairs={{0,4},{1,5},{2,6},{3,7},{4,0},{5,1},{6,2},{7,3},{8,12},{9,13},{10,... | collective-permute-start | bytes 1572872 | tf_op jit(solution)/shard_map/ppermute | solution.py:37
  15.3 11.1 %collective-permute-start.5 = (bf16[1024,256]{1,0:T(8,128)(2,1)S(1)}, bf16[1024,256]{1,0:T(8,128)(2,1)S(1)}, u32[]{:S(2)}, u32[]{:S(2)}) collective-permute-start(bf16[1024,256]{1,0:T(8,128)(2,1)S(1)} %collective-permute-done.1.refs_1_), channel_id=1, source_target_pairs={{0,2},{1,0},{2,3},{3,1},{4,5},{5,7},{6,4},{7,6},{8,10},{9,8},{10,1... | collective-permute-start | bytes 1572872 | tf_op jit(solution)/shard_map/ppermute | solution.py:37
  21.3 5.1 %collective-permute-start.6 = (bf16[1024,256]{1,0:T(8,128)(2,1)S(1)}, bf16[1024,256]{1,0:T(8,128)(2,1)S(1)}, u32[]{:S(2)}, u32[]{:S(2)}) collective-permute-start(bf16[1024,256]{1,0:T(8,128)(2,1)S(1)} %collective-permute-done.refs_3_), channel_id=1, source_target_pairs={{0,4},{1,5},{2,6},{3,7},{4,0},{5,1},{6,2},{7,3},{8,12},{9,13},{10,... | collective-permute-start | bytes 1572872 | tf_op jit(solution)/shard_map/ppermute | solution.py:37
  21.3 5.1 %collective-permute-start.7 = (bf16[1024,256]{1,0:T(8,128)(2,1)S(1)}, bf16[1024,256]{1,0:T(8,128)(2,1)S(1)}, u32[]{:S(2)}, u32[]{:S(2)}) collective-permute-start(bf16[1024,256]{1,0:T(8,128)(2,1)S(1)} %collective-permute-done.3.refs_0_), channel_id=1, source_target_pairs={{0,4},{1,5},{2,6},{3,7},{4,0},{5,1},{6,2},{7,3},{8,12},{9,13},{10,... | collective-permute-start | bytes 1572872 | tf_op jit(solution)/shard_map/ppermute | solution.py:37
  21.8 10.2 %collective-permute-start.10 = (f32[16,9216]{1,0:T(8,128)S(1)}, f32[16,9216]{1,0:T(8,128)S(1)}, u32[]{:S(2)}, u32[]{:S(2)}) collective-permute-start(f32[16,9216]{1,0:T(8,128)S(1)} %get-tuple-element.202), channel_id=1, source_target_pairs={{0,1},{1,0},{2,3},{3,2},{4,6},{5,7},{6,4},{7,5},{8,9},{9,8},{10,11... | collective-permute-start | bytes 1769480 | tf_op jit(solution)/shard_map/ppermute | solution.py:37
  22.4 13.5 %collective-permute-start.8 = (bf16[1024,256]{1,0:T(8,128)(2,1)S(1)}, bf16[1024,256]{1,0:T(8,128)(2,1)S(1)}, u32[]{:S(2)}, u32[]{:S(2)}) collective-permute-start(bf16[1024,256]{1,0:T(8,128)(2,1)S(1)} %copy-done), channel_id=1, source_target_pairs={{0,24},{1,25},{2,26},{3,27},{4,28},{5,29},{6,30},{7,31},{8,0},{9,1... | collective-permute-start | bytes 1572872 | tf_op jit(solution)/shard_map/ppermute | solution.py:37
  26.4 9.5 %collective-permute-start.9 = (bf16[1024,256]{1,0:T(8,128)(2,1)S(1)}, bf16[1024,256]{1,0:T(8,128)(2,1)S(1)}, u32[]{:S(2)}, u32[]{:S(2)}) collective-permute-start(bf16[1024,256]{1,0:T(8,128)(2,1)S(1)} %collective-permute-done.5.refs_2_), channel_id=1, source_target_pairs={{0,4},{1,5},{2,6},{3,7},{4,0},{5,1},{6,2},{7,3},{8,12},{9,13},{10,... | collective-permute-start | bytes 1572872 | tf_op jit(solution)/shard_map/ppermute | solution.py:37
  26.4 11.4 %collective-permute-start.11 = (bf16[1024,256]{1,0:T(8,128)(2,1)S(1)}, bf16[1024,256]{1,0:T(8,128)(2,1)S(1)}, u32[]{:S(2)}, u32[]{:S(2)}) collective-permute-start(bf16[1024,256]{1,0:T(8,128)(2,1)S(1)} %collective-permute-done.3.refs_0_), channel_id=1, source_target_pairs={{0,2},{1,0},{2,3},{3,1},{4,5},{5,7},{6,4},{7,6},{8,10},{9,8},{10,1... | collective-permute-start | bytes 1572872 | tf_op jit(solution)/shard_map/ppermute | solution.py:37
  35.9 1.9 %collective-permute-start.12 = (bf16[1024,256]{1,0:T(8,128)(2,1)S(1)}, bf16[1024,256]{1,0:T(8,128)(2,1)S(1)}, u32[]{:S(2)}, u32[]{:S(2)}) collective-permute-start(bf16[1024,256]{1,0:T(8,128)(2,1)S(1)} %collective-permute-done.8.refs_0_), channel_id=1, source_target_pairs={{0,4},{1,5},{2,6},{3,7},{4,0},{5,1},{6,2},{7,3},{8,12},{9,13},{10,... | collective-permute-start | bytes 1572872 | tf_op jit(solution)/shard_map/ppermute | solution.py:37
  35.9 13.3 %collective-permute-start.13 = (bf16[1024,256]{1,0:T(8,128)(2,1)S(1)}, bf16[1024,256]{1,0:T(8,128)(2,1)S(1)}, u32[]{:S(2)}, u32[]{:S(2)}) collective-permute-start(bf16[1024,256]{1,0:T(8,128)(2,1)S(1)} %collective-permute-done.3.refs_0_), channel_id=1, source_target_pairs={{0,1},{1,3},{2,0},{3,2},{4,6},{5,4},{6,7},{7,5},{8,9},{9,11},{10,8... | collective-permute-start | bytes 1572872 | tf_op jit(solution)/shard_map/ppermute | solution.py:37
  37.4 15.9 %collective-permute-start.14 = (bf16[1024,256]{1,0:T(8,128)(2,1)S(1)}, bf16[1024,256]{1,0:T(8,128)(2,1)S(1)}, u32[]{:S(2)}, u32[]{:S(2)}) collective-permute-start(bf16[1024,256]{1,0:T(8,128)(2,1)S(1)} %collective-permute-done.3.refs_0_), channel_id=1, source_target_pairs={{0,8},{1,9},{2,10},{3,11},{4,12},{5,13},{6,14},{7,15},{8,16},{9,17... | collective-permute-start | bytes 1572872 | tf_op jit(solution)/shard_map/ppermute | solution.py:37
  37.8 15.4 %collective-permute-start.15 = (bf16[1024,256]{1,0:T(8,128)(2,1)S(1)}, bf16[1024,256]{1,0:T(8,128)(2,1)S(1)}, u32[]{:S(2)}, u32[]{:S(2)}) collective-permute-start(bf16[1024,256]{1,0:T(8,128)(2,1)S(1)} %collective-permute-done.11.refs_1_), channel_id=1, source_target_pairs={{0,4},{1,5},{2,6},{3,7},{4,0},{5,1},{6,2},{7,3},{8,12},{9,13},{10,... | collective-permute-start | bytes 1572872 | tf_op jit(solution)/shard_map/ppermute | solution.py:37
  37.9 17.0 %collective-permute-start.16 = (bf16[1024,256]{1,0:T(8,128)(2,1)S(1)}, bf16[1024,256]{1,0:T(8,128)(2,1)S(1)}, u32[]{:S(2)}, u32[]{:S(2)}) collective-permute-start(bf16[1024,256]{1,0:T(8,128)(2,1)S(1)} %collective-permute-done.8.refs_0_), channel_id=1, source_target_pairs={{0,2},{1,0},{2,3},{3,1},{4,5},{5,7},{6,4},{7,6},{8,10},{9,8},{10,1... | collective-permute-start | bytes 1572872 | tf_op jit(solution)/shard_map/ppermute | solution.py:37
  53.3 1.9 %collective-permute-start.17 = (bf16[1024,256]{1,0:T(8,128)(2,1)S(1)}, bf16[1024,256]{1,0:T(8,128)(2,1)S(1)}, u32[]{:S(2)}, u32[]{:S(2)}) collective-permute-start(bf16[1024,256]{1,0:T(8,128)(2,1)S(1)} %collective-permute-done.13.refs_3_), channel_id=1, source_target_pairs={{0,4},{1,5},{2,6},{3,7},{4,0},{5,1},{6,2},{7,3},{8,12},{9,13},{10,... | collective-permute-start | bytes 1572872 | tf_op jit(solution)/shard_map/ppermute | solution.py:37
  53.3 2.7 %collective-permute-start.18 = (bf16[1024,256]{1,0:T(8,128)(2,1)S(1)}, bf16[1024,256]{1,0:T(8,128)(2,1)S(1)}, u32[]{:S(2)}, u32[]{:S(2)}) collective-permute-start(bf16[1024,256]{1,0:T(8,128)(2,1)S(1)} %collective-permute-done.14.refs_0_), channel_id=1, source_target_pairs={{0,4},{1,5},{2,6},{3,7},{4,0},{5,1},{6,2},{7,3},{8,12},{9,13},{10,... | collective-permute-start | bytes 1572872 | tf_op jit(solution)/shard_map/ppermute | solution.py:37
  53.8 9.2 %collective-permute-start.19 = (bf16[1024,256]{1,0:T(8,128)(2,1)S(1)}, bf16[1024,256]{1,0:T(8,128)(2,1)S(1)}, u32[]{:S(2)}, u32[]{:S(2)}) collective-permute-start(bf16[1024,256]{1,0:T(8,128)(2,1)S(1)} %collective-permute-done.11.refs_1_), channel_id=1, source_target_pairs={{0,2},{1,0},{2,3},{3,1},{4,5},{5,7},{6,4},{7,6},{8,10},{9,8},{10,1... | collective-permute-start | bytes 1572872 | tf_op jit(solution)/shard_map/ppermute | solution.py:37
  55.9 7.0 %collective-permute-start.20 = (bf16[1024,256]{1,0:T(8,128)(2,1)S(1)}, bf16[1024,256]{1,0:T(8,128)(2,1)S(1)}, u32[]{:S(2)}, u32[]{:S(2)}) collective-permute-start(bf16[1024,256]{1,0:T(8,128)(2,1)S(1)} %collective-permute-done.16.refs_1_), channel_id=1, source_target_pairs={{0,4},{1,5},{2,6},{3,7},{4,0},{5,1},{6,2},{7,3},{8,12},{9,13},{10,... | collective-permute-start | bytes 1572872 | tf_op jit(solution)/shard_map/ppermute | solution.py:37
  56.1 14.9 %collective-permute-start.22 = (bf16[1024,256]{1,0:T(8,128)(2,1)S(1)}, bf16[1024,256]{1,0:T(8,128)(2,1)S(1)}, u32[]{:S(2)}, u32[]{:S(2)}) collective-permute-start(bf16[1024,256]{1,0:T(8,128)(2,1)S(1)} %collective-permute-done.16.refs_1_), channel_id=1, source_target_pairs={{0,2},{1,0},{2,3},{3,1},{4,5},{5,7},{6,4},{7,6},{8,10},{9,8},{10,1... | collective-permute-start | bytes 1572872 | tf_op jit(solution)/shard_map/ppermute | solution.py:37
  57.2 13.8 %collective-permute-start.21 = (bf16[1024,256]{1,0:T(8,128)(2,1)S(1)}, bf16[1024,256]{1,0:T(8,128)(2,1)S(1)}, u32[]{:S(2)}, u32[]{:S(2)}) collective-permute-start(bf16[1024,256]{1,0:T(8,128)(2,1)S(1)} %collective-permute-done.refs_3_), channel_id=1, source_target_pairs={{0,24},{1,25},{2,26},{3,27},{4,28},{5,29},{6,30},{7,31},{8,0},{9,1... | collective-permute-start | bytes 1572872 | tf_op jit(solution)/shard_map/ppermute | solution.py:37
  63.0 8.0 %collective-permute-start.23 = (bf16[1024,256]{1,0:T(8,128)(2,1)S(1)}, bf16[1024,256]{1,0:T(8,128)(2,1)S(1)}, u32[]{:S(2)}, u32[]{:S(2)}) collective-permute-start(bf16[1024,256]{1,0:T(8,128)(2,1)S(1)} %collective-permute-done.19.refs_2_), channel_id=1, source_target_pairs={{0,4},{1,5},{2,6},{3,7},{4,0},{5,1},{6,2},{7,3},{8,12},{9,13},{10,... | collective-permute-start | bytes 1572872 | tf_op jit(solution)/shard_map/ppermute | solution.py:37
  63.0 16.9 %collective-permute-start.24 = (bf16[1024,256]{1,0:T(8,128)(2,1)S(1)}, bf16[1024,256]{1,0:T(8,128)(2,1)S(1)}, u32[]{:S(2)}, u32[]{:S(2)}) collective-permute-start(bf16[1024,256]{1,0:T(8,128)(2,1)S(1)} %collective-permute-done.14.refs_0_), channel_id=1, source_target_pairs={{0,2},{1,0},{2,3},{3,1},{4,5},{5,7},{6,4},{7,6},{8,10},{9,8},{10,1... | collective-permute-start | bytes 1572872 | tf_op jit(solution)/shard_map/ppermute | solution.py:37
  71.0 8.9 %collective-permute-start.25 = (bf16[1024,256]{1,0:T(8,128)(2,1)S(1)}, bf16[1024,256]{1,0:T(8,128)(2,1)S(1)}, u32[]{:S(2)}, u32[]{:S(2)}) collective-permute-start(bf16[1024,256]{1,0:T(8,128)(2,1)S(1)} %collective-permute-done.21.refs_3_), channel_id=1, source_target_pairs={{0,4},{1,5},{2,6},{3,7},{4,0},{5,1},{6,2},{7,3},{8,12},{9,13},{10,... | collective-permute-start | bytes 1572872 | tf_op jit(solution)/shard_map/ppermute | solution.py:37
  71.0 8.9 %collective-permute-start.26 = (bf16[1024,256]{1,0:T(8,128)(2,1)S(1)}, bf16[1024,256]{1,0:T(8,128)(2,1)S(1)}, u32[]{:S(2)}, u32[]{:S(2)}) collective-permute-start(bf16[1024,256]{1,0:T(8,128)(2,1)S(1)} %collective-permute-done.22.refs_2_), channel_id=1, source_target_pairs={{0,4},{1,5},{2,6},{3,7},{4,0},{5,1},{6,2},{7,3},{8,12},{9,13},{10,... | collective-permute-start | bytes 1572872 | tf_op jit(solution)/shard_map/ppermute | solution.py:37
  71.5 16.8 %collective-permute-start.29 = (f32[16,9216]{1,0:T(8,128)S(1)}, f32[16,9216]{1,0:T(8,128)S(1)}, u32[]{:S(2)}, u32[]{:S(2)}) collective-permute-start(f32[16,9216]{1,0:T(8,128)S(1)} %add.6), channel_id=1, source_target_pairs={{0,2},{1,3},{2,0},{3,1},{4,5},{5,4},{6,7},{7,6},{8,10},{9,11},{10,... | collective-permute-start | bytes 1769480 | tf_op jit(solution)/shard_map/ppermute | solution.py:37
  72.5 16.1 %collective-permute-start.27 = (bf16[1024,256]{1,0:T(8,128)(2,1)S(1)}, bf16[1024,256]{1,0:T(8,128)(2,1)S(1)}, u32[]{:S(2)}, u32[]{:S(2)}) collective-permute-start(bf16[1024,256]{1,0:T(8,128)(2,1)S(1)} %collective-permute-done.13.refs_3_), channel_id=1, source_target_pairs={{0,8},{1,9},{2,10},{3,11},{4,12},{5,13},{6,14},{7,15},{8,16},{9,17... | collective-permute-start | bytes 1572872 | tf_op jit(solution)/shard_map/ppermute | solution.py:37
  79.9 8.8 %collective-permute-start.28 = (bf16[1024,256]{1,0:T(8,128)(2,1)S(1)}, bf16[1024,256]{1,0:T(8,128)(2,1)S(1)}, u32[]{:S(2)}, u32[]{:S(2)}) collective-permute-start(bf16[1024,256]{1,0:T(8,128)(2,1)S(1)} %collective-permute-done.24.refs_1_), channel_id=1, source_target_pairs={{0,4},{1,5},{2,6},{3,7},{4,0},{5,1},{6,2},{7,3},{8,12},{9,13},{10,... | collective-permute-start | bytes 1572872 | tf_op jit(solution)/shard_map/ppermute | solution.py:37
  80.4 9.2 %collective-permute-start.30 = (bf16[1024,256]{1,0:T(8,128)(2,1)S(1)}, bf16[1024,256]{1,0:T(8,128)(2,1)S(1)}, u32[]{:S(2)}, u32[]{:S(2)}) collective-permute-start(bf16[1024,256]{1,0:T(8,128)(2,1)S(1)} %collective-permute-done.24.refs_1_), channel_id=1, source_target_pairs={{0,2},{1,0},{2,3},{3,1},{4,5},{5,7},{6,4},{7,6},{8,10},{9,8},{10,1... | collective-permute-start | bytes 1572872 | tf_op jit(solution)/shard_map/ppermute | solution.py:37
  88.7 1.9 %collective-permute-start.31 = (bf16[1024,256]{1,0:T(8,128)(2,1)S(1)}, bf16[1024,256]{1,0:T(8,128)(2,1)S(1)}, u32[]{:S(2)}, u32[]{:S(2)}) collective-permute-start(bf16[1024,256]{1,0:T(8,128)(2,1)S(1)} %collective-permute-done.27.refs_3_), channel_id=1, source_target_pairs={{0,4},{1,5},{2,6},{3,7},{4,0},{5,1},{6,2},{7,3},{8,12},{9,13},{10,... | collective-permute-start | bytes 1572872 | tf_op jit(solution)/shard_map/ppermute | solution.py:37
  (2 other events, 23.6 us)
